TPU v7x, 128 devices: a whole 4x4x4 slice. The times are simulated.
128 devices in a mesh: facet: 4 (over x), sub: 32 (over z, y, core).
Axes of the slice: x: 4, y: 4, z: 4, core: 2. Of those that a mesh axis runs over, the one named last changes fastest.
Arguments:
- facet_slab: bfloat16 [4, 2, 512, 8192], P('facet', None, 'sub'), may hold values from -6 to 6
- facet_offsets: int32 [4, 2], P('facet'), may hold values from 0 to 24576
- visibility_position: float32 [2, 131072], P(None, ('facet', 'sub')), may hold values from -32 to 32
- observed: float32 [2, 131072], P(None, ('facet', 'sub')), may hold values from -3 to 3
- visibility_subgrid: int32 [131072, 1], P(('facet', 'sub')), may hold values from 0 to 255; in each aligned block of 1024 rows (0 to 1023, 1024 to 2047, ...) at most 8 rows name the same one
- clip_levels: int32 [4096], P(('facet', 'sub')), may hold values from 1 to 8
Outputs:
- facet_adjoint: float32 [4, 2, 512, 8192], P('facet', None, 'sub')
- weighted_residual: float32 [2, 131072], P(None, ('facet', 'sub'))
Inputs may be any that keep to these rules, and one draw needn't show every extreme that they name: `visibility_subgrid`: subgrid p * 32 + q covers subgrid row block p and column block q; within the rows of one device no subgrid is named more than 8 times. `facet_offsets`: column 0 is a facet's first image row, column 1 its first image column.
All inputs are finite; a program needn't handle non-finite values.
Results may differ from a plain program's by a relative error of at most 0.012.
Values may be sent and summed in bfloat16 or wider, within the bound.
No kernel may reach another device: no remote copies, remote signals or barrier semaphores. Data moves between devices by JAX's collectives and lax.ppermute only.
A program may use at most 128 MiB of HBM per device.

v0:
```python
import math

import jax
import jax.numpy as jnp
from jax import lax
from jax.sharding import PartitionSpec as P

FS = 8192
N_IMG = 32768
SUBG = 64
PR_DEV = 2
QC_DEV = 1
VIS_BLOCK = 32


TWO_PI = 2.0 * math.pi


def phase_pair(position, frequency, image_size, factor):
    phase_index = position[:, None] * frequency[None, :] % image_size
    angles = phase_index.astype(jnp.float32) * (-TWO_PI / image_size)
    return (
        (jnp.cos(angles) * factor).astype(jnp.bfloat16),
        (jnp.sin(angles) * factor).astype(jnp.bfloat16),
    )


def column_tables(col_offset, facet_width, image_size, subgrid_size, column_count):
    position = col_offset + jnp.arange(facet_width, dtype=jnp.int32)
    fine_cos, fine_sin = phase_pair(
        position, jnp.arange(subgrid_size, dtype=jnp.int32), image_size, facet_width ** (-0.5)
    )
    coarse_freq = jnp.arange(column_count, dtype=jnp.int32) * (image_size // column_count)
    coarse_cos, coarse_sin = phase_pair(position, coarse_freq, image_size, 1.0)
    return (fine_cos, fine_sin, coarse_cos, coarse_sin)


def row_tables(position, image_size, subgrid_size, row_blocks, total_rows):
    block_start = jnp.arange(row_blocks, dtype=jnp.int32)[:, None] * (image_size // row_blocks)
    frequency = (block_start + jnp.arange(subgrid_size, dtype=jnp.int32)[None, :]).reshape(-1)
    return phase_pair(position, frequency, image_size, 0.5 * total_rows ** (-0.5))


def column_forward(slab_real, slab_imag, tables):
    fine_cos, fine_sin, coarse_cos, coarse_sin = tables
    facet_width = fine_cos.shape[0]
    column_count = coarse_cos.shape[1]
    row_count = slab_real.shape[0]
    grouping = 4
    forward_matrix = jnp.concatenate(
        [jnp.concatenate([fine_cos, fine_sin], 1), jnp.concatenate([-fine_sin, fine_cos], 1)], 0
    )
    real_wide = slab_real.astype(jnp.float32)[None]
    imag_wide = slab_imag.astype(jnp.float32)[None]

    def one_group(cos_sin):
        cos_group = cos_sin[0].astype(jnp.float32)[:, None, :]
        sin_group = cos_sin[1].astype(jnp.float32)[:, None, :]
        mod_real = (real_wide * cos_group - imag_wide * sin_group).astype(jnp.bfloat16)
        mod_imag = (real_wide * sin_group + imag_wide * cos_group).astype(jnp.bfloat16)
        joined = jnp.concatenate([mod_real, mod_imag], 2).reshape(
            grouping * row_count, 2 * facet_width
        )
        return jnp.dot(joined, forward_matrix, preferred_element_type=jnp.float32).reshape(
            grouping, row_count, -1
        )

    cos_groups = coarse_cos.T.reshape(column_count // grouping, grouping, facet_width)
    sin_groups = coarse_sin.T.reshape(column_count // grouping, grouping, facet_width)
    spectra = lax.map(one_group, (cos_groups, sin_groups))
    spectra = spectra.reshape(column_count, row_count, -1).transpose(1, 0, 2)
    return spectra.astype(jnp.bfloat16)


def row_forward(row_cos, row_sin, spectra):
    half_width = spectra.shape[2] // 2
    swapped = jnp.concatenate([-spectra[:, :, half_width:], spectra[:, :, :half_width]], 2)
    stacked = jnp.concatenate([spectra, swapped], 0)
    left_rows = jnp.concatenate([row_cos, row_sin], 0)
    flat = stacked.reshape(stacked.shape[0], -1)
    result = jnp.dot(left_rows.T, flat, preferred_element_type=jnp.float32)
    return result.reshape(left_rows.shape[1], spectra.shape[1], spectra.shape[2])


def row_adjoint(row_cos, row_sin, corrected_rows):
    half_width = corrected_rows.shape[2] // 2
    swapped = jnp.concatenate(
        [corrected_rows[:, :, half_width:], -corrected_rows[:, :, :half_width]], 2
    )
    stacked = jnp.concatenate([corrected_rows, swapped], 0)
    left_rows = jnp.concatenate([row_cos, row_sin], 1)
    flat = stacked.reshape(stacked.shape[0], -1)
    result = jnp.dot(left_rows, flat, preferred_element_type=jnp.float32)
    return result.reshape(left_rows.shape[0], corrected_rows.shape[1], corrected_rows.shape[2])


def column_adjoint(images, tables):
    fine_cos, fine_sin, coarse_cos, coarse_sin = tables
    facet_width = fine_cos.shape[0]
    row_count = images.shape[0]
    column_count = images.shape[1]
    grouping = 4
    adjoint_matrix = jnp.concatenate(
        [
            jnp.concatenate([fine_cos.T, -fine_sin.T], 1),
            jnp.concatenate([fine_sin.T, fine_cos.T], 1),
        ],
        0,
    )
    image_groups = images.transpose(1, 0, 2).reshape(
        column_count // grouping, grouping * row_count, images.shape[2]
    )
    cos_groups = coarse_cos.T.reshape(column_count // grouping, grouping, facet_width)
    sin_groups = coarse_sin.T.reshape(column_count // grouping, grouping, facet_width)

    def accumulate(running, inputs):
        image_group, cos_group, sin_group = inputs
        spread = jnp.dot(image_group, adjoint_matrix, preferred_element_type=jnp.float32).reshape(
            grouping, row_count, 2 * facet_width
        )
        spread_real = spread[:, :, :facet_width]
        spread_imag = spread[:, :, facet_width:]
        cos_wide = cos_group.astype(jnp.float32)[:, None, :]
        sin_wide = sin_group.astype(jnp.float32)[:, None, :]
        new_real = running[0] + jnp.sum(cos_wide * spread_real + sin_wide * spread_imag, 0)
        new_imag = running[1] + jnp.sum(cos_wide * spread_imag - sin_wide * spread_real, 0)
        return ((new_real, new_imag), None)

    initial = (
        jnp.zeros((row_count, facet_width), jnp.float32),
        jnp.zeros((row_count, facet_width), jnp.float32),
    )
    finals, unused = lax.scan(accumulate, initial, (image_groups, cos_groups, sin_groups))
    return jnp.stack([finals[0], finals[1]])


def subgrid_pass(subgrids, payload, live_mask):
    subgrid_size = subgrids.shape[1]
    local_count = subgrids.shape[0]
    factor = subgrid_size ** (-0.5)
    offsets_grid = jnp.arange(subgrid_size, dtype=jnp.float32) * (TWO_PI / subgrid_size)
    angle_left = payload[0][:, :, None] * offsets_grid
    angle_right = payload[1][:, :, None] * offsets_grid
    left_real = jnp.cos(angle_left) * factor
    left_imag = jnp.sin(angle_left) * factor
    right_real = (jnp.cos(angle_right) * factor).astype(jnp.bfloat16)
    right_imag = (jnp.sin(angle_right) * factor).astype(jnp.bfloat16)
    first_basis = jnp.concatenate([right_real, -right_imag], 2)
    second_basis = jnp.concatenate([right_imag, right_real], 2)
    inner_real = jnp.stack(
        [
            jnp.dot(first_basis[item], subgrids[item].T, preferred_element_type=jnp.float32)
            for item in range(local_count)
        ]
    )
    inner_imag = jnp.stack(
        [
            jnp.dot(second_basis[item], subgrids[item].T, preferred_element_type=jnp.float32)
            for item in range(local_count)
        ]
    )
    predicted_real = jnp.sum(left_real * inner_real - left_imag * inner_imag, 2)
    predicted_imag = jnp.sum(left_real * inner_imag + left_imag * inner_real, 2)
    misfit_real = payload[2] - predicted_real
    misfit_imag = payload[3] - predicted_imag
    threshold = payload[4] + (1.0 - live_mask)
    magnitude = jnp.sqrt(misfit_real * misfit_real + misfit_imag * misfit_imag)
    weight = live_mask * threshold / jnp.maximum(magnitude, threshold)
    weighted_real = weight * misfit_real
    weighted_imag = weight * misfit_imag
    phasor_real = (
        left_real * weighted_real[:, :, None] + left_imag * weighted_imag[:, :, None]
    ).astype(jnp.bfloat16)
    phasor_imag = (
        left_real * weighted_imag[:, :, None] - left_imag * weighted_real[:, :, None]
    ).astype(jnp.bfloat16)
    phasors = jnp.concatenate([phasor_real, phasor_imag], 1)
    bases = jnp.concatenate([first_basis, second_basis], 1)
    gridded = jnp.stack(
        [
            jnp.dot(phasors[item].T, bases[item], preferred_element_type=jnp.float32)
            for item in range(local_count)
        ]
    )
    return (gridded.astype(jnp.bfloat16), weighted_real, weighted_imag)


def on_device(
    facet_slab, facet_offsets, visibility_position, observed, visibility_subgrid, clip_levels
):
    sub_count = lax.axis_size("sub")
    facet_count = lax.axis_size("facet")
    devices = sub_count * facet_count
    rows_dev = facet_slab.shape[2]
    total_rows = rows_dev * sub_count
    column_count = QC_DEV * sub_count
    row_blocks = PR_DEV * facet_count
    local_count = PR_DEV * QC_DEV
    vis_count = visibility_position.shape[1]
    most_slots = max(2, 2 * vis_count // (row_blocks * column_count))
    row_offset = facet_offsets[0, 0]
    tables = column_tables(facet_offsets[0, 1], FS, N_IMG, SUBG, column_count)
    spectra = column_forward(facet_slab[0, 0], facet_slab[0, 1], tables)
    own_rows = row_offset + lax.axis_index("sub") * rows_dev + jnp.arange(rows_dev, dtype=jnp.int32)
    row_cos, row_sin = row_tables(own_rows, N_IMG, SUBG, row_blocks, total_rows)
    partial_sum = row_forward(row_cos, row_sin, spectra)
    arranged = partial_sum.reshape(facet_count, PR_DEV, SUBG, sub_count, QC_DEV, 2 * SUBG)
    arranged = arranged.transpose(0, 3, 1, 4, 2, 5).reshape(devices * local_count, SUBG, 2 * SUBG)
    summed = lax.psum_scatter(arranged, ("facet", "sub"), scatter_dimension=0, tiled=True)
    subgrids = summed.astype(jnp.bfloat16)
    identity = visibility_subgrid[:, 0]
    block_row = identity // column_count
    block_col = identity % column_count
    owner = block_row // PR_DEV * sub_count + block_col // QC_DEV
    local_index = block_row % PR_DEV * QC_DEV + block_col % QC_DEV
    sort_order = jnp.argsort(identity, stable=True)
    sorted_ids = identity[sort_order]
    first_seen = jnp.searchsorted(sorted_ids, sorted_ids, side="left")
    ranked_sorted = jnp.arange(vis_count, dtype=jnp.int32) - first_seen
    ranked = jnp.zeros((vis_count,), jnp.int32).at[sort_order].set(ranked_sorted)
    slot_index = (owner * local_count + local_index) * most_slots + ranked
    slot_total = devices * local_count * most_slots
    levels = jnp.repeat(clip_levels, VIS_BLOCK).astype(jnp.float32) * 0.25
    rows_send = jnp.stack(
        [visibility_position[0], visibility_position[1], observed[0], observed[1], levels]
    )
    payload_out = jnp.zeros((5, slot_total), jnp.float32).at[:, slot_index].set(rows_send)
    live_out = jnp.zeros((1, slot_total), jnp.float32).at[0, slot_index].set(1.0)
    payload_in, live_in = (
        lax.all_to_all(
            payload_out.reshape(5, devices, -1),
            ("facet", "sub"),
            split_axis=1,
            concat_axis=1,
            tiled=True,
        ),
        lax.all_to_all(
            live_out.reshape(1, devices, -1),
            ("facet", "sub"),
            split_axis=1,
            concat_axis=1,
            tiled=True,
        ),
    )
    payload = (
        payload_in.reshape(5, devices, local_count, most_slots)
        .transpose(0, 2, 1, 3)
        .reshape(5, local_count, devices * most_slots)
    )
    live_mask = (
        live_in.reshape(devices, local_count, most_slots)
        .transpose(1, 0, 2)
        .reshape(local_count, devices * most_slots)
    )
    corrected, weighted_real, weighted_imag = subgrid_pass(subgrids, payload, live_mask)
    weighted_back = jnp.stack([weighted_real, weighted_imag]).reshape(
        2, local_count, devices, most_slots
    )
    weighted_back = weighted_back.transpose(0, 2, 1, 3).reshape(
        2, devices, local_count * most_slots
    )
    returned = lax.all_to_all(
        weighted_back, ("facet", "sub"), split_axis=1, concat_axis=1, tiled=True
    )
    weighted_residual = returned.reshape(2, slot_total)[:, slot_index]
    everything = lax.all_gather(corrected, ("facet", "sub"), axis=0, tiled=True)
    ordered = everything.reshape(facet_count, sub_count, PR_DEV, QC_DEV, SUBG, 2 * SUBG)
    ordered = ordered.transpose(0, 2, 4, 1, 3, 5).reshape(row_blocks * SUBG, column_count, 2 * SUBG)
    images = row_adjoint(row_cos, row_sin, ordered).astype(jnp.bfloat16)
    facet_adjoint = column_adjoint(images, tables)[None]
    return (facet_adjoint, weighted_residual)


def solution(mesh):
    placed = (
        P("facet", None, "sub", None),
        P("facet", None),
        P(None, ("facet", "sub")),
        P(None, ("facet", "sub")),
        P(("facet", "sub"), None),
        P(("facet", "sub")),
    )
    return jax.shard_map(
        on_device,
        mesh=mesh,
        in_specs=placed,
        out_specs=(P("facet", None, "sub", None), P(None, ("facet", "sub"))),
        check_vma=False,
    )
```

profile of v0, /device:TPU:1, one launch (start us, length us, event | category | flops | bytes accessed | tf_op | source)
XLA Modules:
  0.0 942.8 jit_solution(4647377624117171891)
XLA Ops:
  7.2 1.3 fusion.110
  9.2 20.3 %multiply_convert_fusion = (bf16[8192,64]{1,0:T(8,128)(2,1)S(1)}, bf16[8192,64]{1,0:T(8,128)(2,1)}) fusion(s32[8192]{0:T(1024)S(1)} %iota_add_fusion), kind=kLoop, calls=%fused_computation.44 | loop fusion | flops 9437184 | bytes 2129920 | tf_op jit(solution)/shard_map/convert_element_type | solution.py:24
  29.5 18.9 %fusion.40 = bf16[8192,64]{1,0:T(8,128)(2,1)} fusion(s32[8192]{0:T(1024)S(1)} %iota_add_fusion), kind=kLoop, calls=%fused_computation.96 | loop fusion | flops 9961472 | bytes 1081344 | tf_op jit(solution)/shard_map/neg | solution.py:51
  48.3 9.7 %sine_convert_fusion = (bf16[8,4,8192]{2,1,0:T(4,128)(2,1)}, bf16[8,4,8192]{2,1,0:T(4,128)(2,1)}) fusion(s32[8,4]{1,0:T(8,128)S(1)} %add_multiply_fusion, s32[8192]{0:T(1024)S(1)} %iota_add_fusion), kind=kLoop, calls=%fused_computation.80 | loop fusion | flops 4194304 | bytes 1081472 | tf_op jit(solution)/shard_map/convert_element_type | solution.py:24
  59.1 12.2 %maximum_maximum_fusion = bf16[16384,128]{1,0:T(8,128)(2,1)} fusion(bf16[8192,64]{1,0:T(8,128)(2,1)} %get-tuple-element.268, bf16[8192,64]{1,0:T(8,128)(2,1)} %fusion.40, bf16[8192,64]{1,0:T(8,128)(2,1)S(1)} %get-tuple-element.267), kind=kLoop, calls=%fused_computation.41 | loop fusion | flops 16777216 | bytes 7340032 | tf_op jit(solution)/shard_map/concatenate | solution.py:50
  71.3 36.2 %while.48 = (s32[]{:T(128)}, bf16[8,4,16,128]{3,2,1,0:T(8,128)(2,1)S(1)}, f32[1,16,8192]{2,1,0:T(8,128)S(1)}, bf16[8,4,8192]{2,1,0:T(4,128)(2,1)}, f32[1,16,8192...) while((s32[]{:T(128)}, ...), condition=%wide.region_7.8_spmd, body=%wide.region_6.7_spmd.sunk | while | flops 276889600 | bytes 10125405 | solution.py:70
  72.8 3.1 fusion.119
  77.3 3.1 fusion.119
  81.8 3.1 fusion.119
  86.3 3.1 fusion.119
  90.8 3.1 fusion.119
  95.3 3.1 fusion.119
  99.8 3.1 fusion.119
  104.3 3.1 fusion.119
  110.4 4.1 copy.65
  115.2 4.4 sort.17
  119.6 4.5 gather_fusion.1
  124.2 50.7 %while.49 = (s32[]{:T(128)}, u32[1024]{0:T(1024)S(1)}, u32[1024]{0:T(1024)S(1)}, s32[1024]{0:T(1024)S(1)}, s32[]{:T(128)}, /*index=5*/s32[]{:T(128)}, s32[]{}) while((s32[]{:T(128)}, u32[1024]{0:T(1024)S(1)}, u32[1024]{0:T(1024)S(1)}, s32[1024]{0:T(1024)S(1)}, s32[]{:T(128)}, /*index=5*/s32[]{:T(128)}, s32[]{}) %tuple.106), condition=%wide.region_2.3_spmd.clone, body=%wide.region_1.2_spmd.clone.sunk | while | flops 19460 | bytes 67685 | solution.py:218
  124.2 4.5 gather_fusion
  128.8 4.5 gather_fusion
  133.4 4.5 gather_fusion
  138.0 4.5 gather_fusion
  142.6 4.5 gather_fusion
  147.3 4.5 gather_fusion
  151.9 4.5 gather_fusion
  156.5 4.5 gather_fusion
  161.1 4.5 gather_fusion
  165.7 4.5 gather_fusion
  170.3 4.5 gather_fusion
  174.9 4.3 scatter_custom_fusion
  179.5 4.3 scatter_custom_fusion.2
  184.5 11.5 %all-to-all-start.1 = ((f32[1,128,16]{2,0,1:T(1,128)}), f32[1,128,16]{2,0,1:T(1,128)S(1)}, u32[]{:S(2)}, u32[]{:S(2)}) async-start(f32[1,128,16]{2,0,1:T(1,128)} %bitcast.16), calls=%async_computation.1 | async-start | bytes 131072 | tf_op jit(solution)/shard_map/all_to_all | solution.py:237
  196.4 3.3 scatter_custom_fusion.1
  199.8 1.7 copy.53
  201.5 4.1 all-to-all-done.1
  205.5 5.7 all-to-all-start
  211.6 13.1 %all-to-all-done = f32[5,128,16]{2,0,1:T(8,128)S(1)} async-done(((f32[5,128,16]{2,0,1:T(8,128)}), f32[5,128,16]{2,0,1:T(8,128)S(1)}, u32[]{:S(2)}, u32[]{:S(2)}) %all-to-all-start) | async-done | bytes 40992 | tf_op jit(solution)/shard_map/all_to_all | solution.py:230
  225.4 2.1 fusion.76
  227.5 2.2 fusion.52
  229.8 539.3 %reduce-scatter.2.cloned.1.call-done = f32[2,64,128]{2,1,0:T(8,128)} async-done(((f32[256,64,128]{2,1,0:T(8,128)}), f32[2,64,128]{2,1,0:T(8,128)}) %reduce-scatter.2.cloned.1.call-update) | async-done | bytes 65552 | tf_op jit(solution)/shard_map/reduce_scatter | solution.py:209
  770.7 2.5 fusion.42
  774.4 2.1 fusion.46
  777.8 7.9 fusion.74
  785.7 8.6 multiply_convert_fusion.2
  795.0 11.6 %all-to-all-start.2 = ((f32[2,128,16]{2,0,1:T(2,128)}), f32[2,128,16]{2,0,1:T(2,128)S(1)}, u32[]{:S(2)}, u32[]{:S(2)}) async-start(f32[2,128,16]{2,0,1:T(2,128)} %copy.72), calls=%async_computation.3 | async-start | bytes 262144 | tf_op jit(solution)/shard_map/all_to_all | solution.py:262
  806.7 18.2 %maximum_maximum_fusion.1 = bf16[128,16384]{1,0:T(8,128)(2,1)} fusion(bf16[64,8192]{1,0:T(8,128)(2,1)S(1)} %get-tuple-element.266, bf16[64,8192]{1,0:T(8,128)(2,1)S(1)} %get-tuple-element.265, bf16[64,8192]{1,0:T(8,128)(2,1)S(1)} %fusion.74), kind=kLoop, calls=%fused_computation.43 | loop fusion | flops 16777216 | bytes 7340032 | tf_op jit(solution)/shard_map/concatenate | solution.py:103
  825.7 3.0 gather_fusion.2
  829.4 15.9 %all-gather.2.cloned.1.call-done = bf16[256,64,128]{2,1,0:T(8,128)(2,1)} async-done(((bf16[2,64,128]{2,1,0:T(8,128)(2,1)}), bf16[256,64,128]{2,1,0:T(8,128)(2,1)}) %all-gather.2.cloned.1.call-update) | async-done | bytes 4194320 | tf_op jit(solution)/shard_map/all_gather | solution.py:266
  845.3 4.9 copy.67
  850.2 1.7 fusion.108
  851.9 2.4 pad_maximum_fusion
  854.3 10.5 %copy_bitcast_fusion = (bf16[512,4096]{1,0:T(8,128)(2,1)}, bf16[512,4096]{1,0:T(8,128)(2,1)}) fusion(bf16[64,8,32,128]{3,2,1,0:T(8,128)(2,1)S(1)} %bitcast.216, bf16[64,8,32,128]{3,2,1,0:T(8,128)(2,1)S(1)} %bitcast.209), kind=kLoop, calls=%fused_computation.38 | loop fusion | bytes 16777216 | tf_op jit(solution)/shard_map/concatenate | solution.py:90
  864.8 7.8 maximum_bitcast_fusion.6
  872.6 12.1 %copy.69 = bf16[4096,1024]{1,0:T(8,128)(2,1)} copy(bf16[4096,1024]{0,1:T(8,128)(2,1)} %maximum_bitcast_fusion.6) | data formatting | bytes 16777216 | tf_op jit(solution)/shard_map/dot_general | solution.py:93
  884.7 5.7 convolution_convert_fusion
  890.4 44.3 %while.50 = (s32[]{:T(128)}, f32[16,8192]{1,0:T(8,128)S(1)}, f32[16,8192]{1,0:T(8,128)S(1)}, bf16[8,4,8192]{2,1,0:T(4,128)(2,1)}, bf16[8,64,128]{2,1,0:T(8,128)(...) while((s32[]{:T(128)}, f32[16,8192]{1,0:T(8,128)S(1)}, ...), condition=%wide.region_14.15_spmd.clone, body=%wide.region_11.14_spmd.clone.sunk | while | flops 272957440 | bytes 17481844 | solution.py:133
  890.4 2.9 fusion.122
  895.9 2.9 fusion.122
  901.5 2.9 fusion.122
  907.0 2.9 fusion.122
  912.5 2.9 fusion.122
  918.1 2.9 fusion.122
  923.6 2.9 fusion.122
  929.1 2.9 fusion.122
  (190 shorter events, 46.7 us)
Async XLA Ops:
  7.2 762.0 %reduce-scatter.2.cloned.1.call-start = ((), (), s32[]{:S(2)}) async-start(), calls=%async_computation.4 | async-start | bytes 8454144 | tf_op jit(solution)/shard_map/reduce_scatter | solution.py:209
  114.5 0.7 copy-start
  124.1 55.2 %copy-start.3 = (s32[2]{0:T(128)S(1)}, s32[2]{0:T(128)}, u32[]{:S(2)}) copy-start(s32[2]{0:T(128)} %constant.199) | copy-start | bytes 28
  124.1 55.2 %copy-start.4 = (s32[2]{0:T(128)S(1)}, s32[2]{0:T(128)}, u32[]{:S(2)}) copy-start(s32[2]{0:T(128)} %constant.202) | copy-start | bytes 28
  124.1 71.9 %copy-start.5 = (s32[32]{0:T(128)S(1)}, s32[32]{0:T(128)}, u32[]{:S(2)}) copy-start(s32[32]{0:T(128)} %param.17) | copy-start | bytes 388
  124.1 72.0 %copy-start.1 = (f32[2,1024]{1,0:T(2,128)S(1)}, f32[2,1024]{1,0:T(2,128)}, u32[]{:S(2)}) copy-start(f32[2,1024]{1,0:T(2,128)} %param.15) | copy-start | bytes 24580
  124.1 72.0 %copy-start.2 = (f32[2,1024]{1,0:T(2,128)S(1)}, f32[2,1024]{1,0:T(2,128)}, u32[]{:S(2)}) copy-start(f32[2,1024]{1,0:T(2,128)} %param.14) | copy-start | bytes 24580
  184.5 21.0 %all-to-all-start.1 = ((f32[1,128,16]{2,0,1:T(1,128)}), f32[1,128,16]{2,0,1:T(1,128)S(1)}, u32[]{:S(2)}, u32[]{:S(2)}) async-start(f32[1,128,16]{2,0,1:T(1,128)} %bitcast.16), calls=%async_computation.1 | async-start | bytes 131072 | tf_op jit(solution)/shard_map/all_to_all | solution.py:237
  205.5 19.2 %all-to-all-start = ((f32[5,128,16]{2,0,1:T(8,128)}), f32[5,128,16]{2,0,1:T(8,128)S(1)}, u32[]{:S(2)}, u32[]{:S(2)}) async-start(f32[5,128,16]{2,0,1:T(8,128)} %copy.53), calls=%async_computation | async-start | bytes 1048576 | tf_op jit(solution)/shard_map/all_to_all | solution.py:230
  211.2 634.1 %all-gather.2.cloned.1.call-start = ((), (), s32[]{:S(2)}) async-start(), calls=%async_computation.5 | async-start | bytes 4227072 | tf_op jit(solution)/shard_map/all_gather | solution.py:266
  795.0 29.8 %all-to-all-start.2 = ((f32[2,128,16]{2,0,1:T(2,128)}), f32[2,128,16]{2,0,1:T(2,128)S(1)}, u32[]{:S(2)}, u32[]{:S(2)}) async-start(f32[2,128,16]{2,0,1:T(2,128)} %copy.72), calls=%async_computation.3 | async-start | bytes 262144 | tf_op jit(solution)/shard_map/all_to_all | solution.py:262
Sparse Core Ops, SparseCore 0:
  114.7 654.4 reduce-scatter.1
  777.9 67.3 all-gather.1
where the time goes:
time: 952 us; the launch traced here: 943 us
  waiting for transfers between devices  572 us (60%)
  other arithmetic  158 us (17%)
  local copies, waits for them, and re-layouts  110 us (12%)
  matrix products  55.9 us (6%)
  starting transfers between devices  28.9 us (3%)
  between operations  15.5 us (2%)
    reduce_scatter x1, waiting for transfers between devices, on_device(): lax.psum_scatter(arranged, ('facet', 'sub'), scatter_dimension=0, tiled=T...  539 us
    gather x11, local copies, waits for them, and re-layouts, on_device(): first_seen = jnp.searchsorted(sorted_ids, sorted_ids, side='left')  49.8 us
    convert_element_type x3, other arithmetic, phase_pair(): (jnp.sin(angles) * factor).astype(jnp.bfloat16)  38.6 us
    dot_general x8, matrix products, one_group(): jnp.dot(joined, forward_matrix, preferred_element_type=jnp.float32)  24.5 us
    dot_general x8, matrix products, accumulate(): jnp.dot(image_group, adjoint_matrix, preferred_element_type=jnp.float32)  23.2 us
  transfers between devices with their start and end apart: 5, of which 4 were waited for; matrix products, arithmetic and copies ran while one was open for 13% of the time, Pallas kernels for 0%

commit v1 on v0

v1 whole, which is shorter than its diff:
```python
import math

import jax
import jax.numpy as jnp
import numpy as np
from jax import lax
from jax.experimental import pallas as pl
from jax.experimental.pallas import tpu as pltpu
from jax.sharding import PartitionSpec as P

N_IMG = 32768
SUBG = 64
VIS_BLOCK = 32
LANES = 128
NQ = 32
NF = 4
NDEV = 128
RD = 16
NA = 64
NV = 1024
SLOT = 16
ROWS_MSG = 24
TWO_PI = 2.0 * math.pi
BF = jnp.bfloat16
F32 = jnp.float32
ALL = ("facet", "sub")


def unit(index, period):
    angle = TWO_PI * (np.asarray(index, np.int64) % period) / period
    return np.cos(angle), np.sin(angle)


def host_tables():
    block = np.arange(NA)
    lane = np.arange(LANES)
    fine = np.arange(SUBG)
    coarse = np.arange(NQ)
    c, s = unit(fine[:, None] * block[None, :], 256)
    c, s = c / 64.0, s / 64.0
    col_fwd = np.block([[c, s], [-s, c]])
    col_adj = np.block([[c.T, -s.T], [s.T, c.T]])
    tw_c, tw_s = unit(fine[:, None] * lane[None, :], N_IMG)
    twiddle_fwd = np.stack([tw_c, -tw_s])
    twiddle_adj = np.stack([np.tile(tw_c.T, (1, 2)), np.tile(tw_s.T, (1, 2))])
    wc, ws = unit(coarse[:, None] * lane[None, :], 32)
    coarse_fwd = np.concatenate([wc, -ws], 1)
    coarse_adj = np.concatenate([wc.T, ws.T], 0)
    k_row = (np.arange(8)[:, None] * 4096 + fine[None, :]).reshape(NF, 2 * SUBG)
    rc, rs = unit(k_row[:, :, None] * np.arange(NQ * RD)[None, None, :], N_IMG)
    rc, rs = rc / 64.0, rs / 64.0
    row_fwd = np.concatenate([rc, -rs], 1)
    row_adj = np.ascontiguousarray(row_fwd.transpose(0, 2, 1))
    bf = lambda x: np.asarray(x, np.float32).astype(jnp.bfloat16)
    return dict(
        col_fwd=bf(col_fwd),
        col_adj=bf(col_adj),
        tw_fwd=np.asarray(twiddle_fwd, np.float32),
        tw_adj=np.asarray(twiddle_adj, np.float32),
        coarse_fwd=bf(coarse_fwd),
        coarse_adj=bf(coarse_adj),
        row_fwd=bf(row_fwd),
        row_adj=bf(row_adj),
    )


def sincos_turn(turn):
    quarter = jnp.floor(turn * 4.0 + 0.5)
    y = (turn - quarter * 0.25) * TWO_PI
    y2 = y * y
    s = y * (1.0 + y2 * (-1.0 / 6 + y2 * (1.0 / 120 + y2 * (-1.0 / 5040 + y2 * (1.0 / 362880)))))
    c = 1.0 + y2 * (-0.5 + y2 * (1.0 / 24 + y2 * (-1.0 / 720 + y2 * (1.0 / 40320))))
    turns = quarter.astype(jnp.int32)
    odd = (turns & 1) == 1
    cos = jnp.where(odd, s, c)
    sin = jnp.where(odd, c, s)
    cos = jnp.where(((turns + 1) & 2) == 2, -cos, cos)
    sin = jnp.where((turns & 2) == 2, -sin, sin)
    return cos, sin


def phase_of(offset, frequency):
    index = (offset * frequency) & (N_IMG - 1)
    return sincos_turn(index.astype(F32) * (1.0 / N_IMG))


def swap(x):
    return pltpu.roll(x, SUBG, x.ndim - 1)


def iota(shape, dim):
    return lax.broadcasted_iota(jnp.int32, shape, dim)


def split3(x):
    high = x.astype(BF)
    rest = x - high.astype(F32)
    middle = rest.astype(BF)
    low = (rest - middle.astype(F32)).astype(BF)
    return high, middle, low


def lane_sign(rows):
    return jnp.where(iota((rows, LANES), 1) < SUBG, 1.0, -1.0).astype(F32)


def send_kernel(
    off_ref, slab_ref, pos_ref, obs_ref, ids_ref, clip_ref, col_ref, tw_ref, coarse_ref,
    msg_ref, meta_ref, wide, rows, extra,
):
    for part in range(2):
        for a in range(NA):
            wide[part, a * RD:(a + 1) * RD, :] = slab_ref[
                0, part, :, a * LANES:(a + 1) * LANES
            ].astype(F32)
    freq = iota((NQ, LANES), 0) * (N_IMG // NQ) + (iota((NQ, LANES), 1) & (SUBG - 1))
    ph_c, ph_s = phase_of(off_ref[0, 1], freq)
    ph_s = ph_s * lane_sign(NQ)
    tw_c, tw_s = tw_ref[0], tw_ref[1]
    group = 4
    for base in range(0, RD, group):
        cols = []
        for r in range(base, base + group):
            cols.append(
                jnp.concatenate(
                    [wide[0, pl.ds(r, NA, stride=RD), :], wide[1, pl.ds(r, NA, stride=RD), :]], 0
                ).astype(BF)
            )
        y = jnp.dot(col_ref[...], jnp.concatenate(cols, 1), preferred_element_type=F32)
        stacked = []
        for i in range(group):
            yr = y[:SUBG, i * LANES:(i + 1) * LANES]
            yi = y[SUBG:, i * LANES:(i + 1) * LANES]
            zr = yr * tw_c - yi * tw_s
            zi = yr * tw_s + yi * tw_c
            stacked.append(jnp.concatenate([zr, -zi], 1).astype(BF))
            stacked.append(jnp.concatenate([zi, zr], 1).astype(BF))
        out = lax.dot_general(
            coarse_ref[...], jnp.concatenate(stacked, 0), (((1,), (1,)), ((), ())),
            preferred_element_type=F32,
        )
        for i in range(group):
            piece = out[:, i * LANES:(i + 1) * LANES]
            rows[pl.ds(base + i, NQ, stride=RD), :] = piece * ph_c + swap(piece) * ph_s
    spectra = rows[...].astype(BF).reshape(NQ, RD, LANES)
    for f in range(NF):
        msg_ref[f * NQ:(f + 1) * NQ, 0:RD, :] = spectra

    ids = ids_ref[...]
    upper = jnp.where(iota((LANES, LANES), 0) < iota((LANES, LANES), 1), 1.0, 0.0).astype(BF)
    counter = jnp.concatenate([upper, jnp.ones((LANES, LANES), BF)], 1)
    before = jnp.zeros((2 * LANES, LANES), F32)
    ranks = []
    for b in range(NV // LANES):
        hot = iota((2 * LANES, LANES), 0) == ids[:, b * LANES:(b + 1) * LANES]
        hot_f = jnp.where(hot, 1.0, 0.0)
        count = jnp.dot(hot_f.astype(BF), counter, preferred_element_type=F32)
        ranks.append(jnp.sum(hot_f * (count[:, :LANES] + before), 0, keepdims=True))
        before = before + count[:, LANES:]
    rank = jnp.concatenate(ranks, 1).astype(jnp.int32)
    owner = (ids >> 6) * NQ + (ids & (NQ - 1))
    place = ((ids >> 5) & 1) * 8 + rank
    meta_ref[0:1, :] = owner
    meta_ref[1:2, :] = place
    here = iota((SLOT, NV), 0) == place
    picked = jnp.where(
        iota((NV // VIS_BLOCK, NV), 1) // VIS_BLOCK == iota((NV // VIS_BLOCK, NV), 0),
        clip_ref[...].astype(F32) * 0.25, 0.0,
    )
    level = jnp.sum(picked, 0, keepdims=True)
    values = [pos_ref[0:1, :], pos_ref[1:2, :], obs_ref[0:1, :], obs_ref[1:2, :], level]
    pieces = [split3(v) for v in values]
    own = jnp.where(iota((NDEV, NV), 0) == owner, 1.0, 0.0).astype(BF)
    zeros = jnp.zeros((LANES - 5 * SLOT, NV), BF)
    for part in range(3):
        table = jnp.concatenate(
            [jnp.where(here, p[part].astype(F32), 0.0).astype(BF) for p in pieces] + [zeros], 0
        )
        extra[pl.ds(part, NDEV, stride=8), :] = lax.dot_general(
            own, table, (((1,), (1,)), ((), ())), preferred_element_type=F32
        )
    row_offset = off_ref[0, 0]
    extra[pl.ds(3, NDEV, stride=8), :] = jnp.full((NDEV, LANES), row_offset >> 8, jnp.int32).astype(F32)
    extra[pl.ds(4, NDEV, stride=8), :] = jnp.full((NDEV, LANES), row_offset & 255, jnp.int32).astype(F32)
    for i in range(5, 8):
        extra[pl.ds(i, NDEV, stride=8), :] = jnp.zeros((NDEV, LANES), F32)
    msg_ref[:, RD:ROWS_MSG, :] = extra[...].astype(BF).reshape(NDEV, 8, LANES)


def powers(turn):
    sub = iota((8, LANES), 0).astype(F32)
    low = sincos_turn(turn * sub)
    high = sincos_turn(turn * (sub * 8.0))
    re, im = [], []
    for a in range(8):
        hr, hi = high[0][a:a + 1, :], high[1][a:a + 1, :]
        re.append(hr * low[0] - hi * low[1])
        im.append(hr * low[1] + hi * low[0])
    return jnp.concatenate(re, 0), jnp.concatenate(im, 0)


def owner_kernel(
    facet_ref, got_ref, fwd_ref, adj_ref, msg_ref, extra, left, right, inner, phasor, basis,
):
    sign = lane_sign(2 * SUBG)
    extra[...] = got_ref[:, RD:ROWS_MSG, :].astype(F32).reshape(NDEV * 8, LANES)
    row = iota((2 * SUBG, LANES), 0)
    k_row = (facet_ref[0] * 2 + row // SUBG) * (N_IMG // 8) + (row & (SUBG - 1))
    lane = iota((1, LANES), 1)
    offset = jnp.zeros((1, LANES), F32)
    for f in range(NF):
        at = f * NQ * 8
        value = extra[at + 3:at + 4, :] * 256.0 + extra[at + 4:at + 5, :]
        offset = jnp.where(lane == f, value, offset)
    rho_c, rho_s = phase_of(offset.astype(jnp.int32), k_row)
    real = jnp.zeros((2 * SUBG, LANES), F32)
    turned = jnp.zeros((2 * SUBG, LANES), F32)
    for f in range(NF):
        spectra = got_ref[f * NQ:(f + 1) * NQ, 0:RD, :].reshape(NQ * RD, LANES)
        both = jnp.dot(fwd_ref[0], spectra, preferred_element_type=F32)
        rc, rs = rho_c[:, f:f + 1], rho_s[:, f:f + 1]
        first, second = both[:2 * SUBG], both[2 * SUBG:]
        real = real + (rc * first + rs * second)
        turned = turned + (rc * second - rs * first)
    subgrids = (real - swap(turned) * sign).astype(BF).astype(F32)

    got = (
        extra[pl.ds(0, NDEV, stride=8), :]
        + extra[pl.ds(1, NDEV, stride=8), :]
        + extra[pl.ds(2, NDEV, stride=8), :]
    ).T
    sums = []
    returned = [[None, None], [None, None]]
    for l in range(2):
        def rows_of(c):
            return got[c * SLOT + l * 8:c * SLOT + l * 8 + 8, :]

        u, w, obs_r, obs_i, level = [rows_of(c) for c in range(5)]
        u, w = u * (1.0 / SUBG), w * (1.0 / SUBG)
        for k in range(8):
            at = slice(k * LANES, (k + 1) * LANES)
            cr, ci = powers(w[k:k + 1, :])
            basis[0:SUBG, at] = (cr * 0.125).astype(BF)
            basis[SUBG:, at] = (ci * 0.125).astype(BF)
        sub = subgrids[l * SUBG:(l + 1) * SUBG]
        matrix = jnp.concatenate([sub * sign[:SUBG], swap(sub)], 0).astype(BF)
        inner[...] = jnp.dot(matrix, basis[...], preferred_element_type=F32)
        pred_r, pred_i = [], []
        for k in range(8):
            at = slice(k * LANES, (k + 1) * LANES)
            lr, li = powers(u[k:k + 1, :])
            lr, li = lr * 0.125, li * 0.125
            left[0:SUBG, at] = lr
            left[SUBG:, at] = li
            ir, ii = inner[0:SUBG, at], inner[SUBG:, at]
            pred_r.append(jnp.sum(lr * ir - li * ii, 0, keepdims=True))
            pred_i.append(jnp.sum(lr * ii + li * ir, 0, keepdims=True))
        mis_r = obs_r - jnp.concatenate(pred_r, 0)
        mis_i = obs_i - jnp.concatenate(pred_i, 0)
        live = level > 0.0
        threshold = jnp.where(live, level, 1.0)
        magnitude = jnp.sqrt(mis_r * mis_r + mis_i * mis_i)
        weight = jnp.where(live, threshold / jnp.maximum(magnitude, threshold), 0.0)
        wr, wi = weight * mis_r, weight * mis_i
        returned[0][l], returned[1][l] = wr, wi
        for k in range(8):
            at = slice(k * LANES, (k + 1) * LANES)
            lr, li = left[0:SUBG, at], left[SUBG:, at]
            vr, vi = wr[k:k + 1, :], wi[k:k + 1, :]
            phasor[0:SUBG, at] = (lr * vr + li * vi).astype(BF)
            phasor[SUBG:, at] = (lr * vi - li * vr).astype(BF)
        product = lax.dot_general(
            phasor[...], basis[...], (((1,), (1,)), ((), ())), preferred_element_type=F32
        )
        sums.append(product[:SUBG] * sign[:SUBG] + swap(product[SUBG:]))
    corrected = jnp.concatenate(sums, 0)
    corrected = corrected.astype(BF).astype(F32)
    cols = []
    for f in range(NF):
        rc, rs = rho_c[:, f:f + 1], rho_s[:, f:f + 1]
        d = corrected * rc - swap(corrected) * (sign * rs)
        cols.append(jnp.concatenate([d, swap(d) * sign], 0).astype(BF))
    images = jnp.dot(adj_ref[0], jnp.concatenate(cols, 1), preferred_element_type=F32)
    for f in range(NF):
        msg_ref[f * NQ:(f + 1) * NQ, 0:RD, :] = (
            images[:, f * LANES:(f + 1) * LANES].astype(BF).reshape(NQ, RD, LANES)
        )
    back = jnp.concatenate(
        [returned[0][0], returned[0][1], returned[1][0], returned[1][1],
         jnp.zeros((LANES - 2 * SLOT, LANES), F32)], 0
    ).T
    for i, part in enumerate(split3(back)):
        extra[pl.ds(i, NDEV, stride=8), :] = part.astype(F32)
    msg_ref[:, RD:ROWS_MSG, :] = extra[...].astype(BF).reshape(NDEV, 8, LANES)


def facet_kernel(
    off_ref, got_ref, meta_ref, coarse_ref, tw_ref, col_ref, out_ref, res_ref, rows, extra, flat,
):
    freq = iota((NQ, LANES), 0) * (N_IMG // NQ) + (iota((NQ, LANES), 1) & (SUBG - 1))
    ph_c, ph_s = phase_of(off_ref[0, 1], freq)
    ph_s = -ph_s * lane_sign(NQ)
    for q in range(NQ):
        image = got_ref[q, 0:RD, :].astype(F32)
        for f in range(1, NF):
            image = image + got_ref[f * NQ + q, 0:RD, :].astype(F32)
        rows[q * RD:(q + 1) * RD, :] = image * ph_c[q:q + 1, :] + swap(image) * ph_s[q:q + 1, :]
    tw_c, tw_s = tw_ref[0], tw_ref[1]
    sign = lane_sign(LANES)
    group = 4
    for base in range(0, RD, group):
        image = jnp.concatenate(
            [rows[pl.ds(base + i, NQ, stride=RD), :].astype(BF) for i in range(group)], 1
        )
        spread = jnp.dot(coarse_ref[...], image, preferred_element_type=F32)
        stacked = []
        for i in range(group):
            first = spread[:LANES, i * LANES:(i + 1) * LANES]
            second = spread[LANES:, i * LANES:(i + 1) * LANES]
            z = (tw_c * first - tw_s * second) - swap(tw_s * first + tw_c * second) * sign
            stacked.append(z.astype(BF))
        out = lax.dot_general(
            col_ref[...], jnp.concatenate(stacked, 0), (((1,), (1,)), ((), ())),
            preferred_element_type=F32,
        )
        for i in range(group):
            r = base + i
            for part in range(2):
                at = (part * 2 + r // 8) * NA * 8 + r % 8
                flat[pl.ds(at, NA, stride=8), :] = out[
                    part * NA:(part + 1) * NA, i * LANES:(i + 1) * LANES
                ]
    for part in range(2):
        for half in range(2):
            for a in range(NA):
                at = ((part * 2 + half) * NA + a) * 8
                out_ref[0, part, half * 8:(half + 1) * 8, a * LANES:(a + 1) * LANES] = flat[at:at + 8, :]

    extra[...] = got_ref[:, RD:ROWS_MSG, :].astype(F32).reshape(NDEV * 8, LANES)
    back = (
        extra[pl.ds(0, NDEV, stride=8), :]
        + extra[pl.ds(1, NDEV, stride=8), :]
        + extra[pl.ds(2, NDEV, stride=8), :]
    ).T[:2 * SLOT]
    owner, place = meta_ref[0:1, :], meta_ref[1:2, :]
    own = jnp.where(iota((NDEV, NV), 0) == owner, 1.0, 0.0).astype(BF)
    found = jnp.dot(jnp.concatenate(split3(back), 0), own, preferred_element_type=F32)
    found = found[:2 * SLOT] + found[2 * SLOT:4 * SLOT] + found[4 * SLOT:]
    here = iota((SLOT, NV), 0) == place
    for c in range(2):
        res_ref[c:c + 1, :] = jnp.sum(
            jnp.where(here, found[c * SLOT:(c + 1) * SLOT], 0.0), 0, keepdims=True
        )


VMEM = pl.BlockSpec(memory_space=pltpu.VMEM)
SMEM = pl.BlockSpec(memory_space=pltpu.SMEM)
TABLES = host_tables()


def on_device(slab, offsets, position, observed, subgrid_of, clip):
    t = {name: jnp.asarray(value) for name, value in TABLES.items()}
    limit = pltpu.CompilerParams(vmem_limit_bytes=48 << 20)
    message = jax.ShapeDtypeStruct((NDEV, ROWS_MSG, LANES), BF)
    sent, meta = pl.pallas_call(
        send_kernel,
        out_shape=(message, jax.ShapeDtypeStruct((8, NV), jnp.int32)),
        in_specs=[SMEM] + [VMEM] * 8,
        out_specs=(VMEM, VMEM),
        scratch_shapes=[
            pltpu.VMEM((2, NA * RD, LANES), F32),
            pltpu.VMEM((NQ * RD, LANES), F32),
            pltpu.VMEM((NDEV * 8, LANES), F32),
        ],
        compiler_params=limit,
        name="send",
    )(
        offsets, slab, position, observed, subgrid_of.reshape(1, NV),
        clip.reshape(NV // VIS_BLOCK, 1), t["col_fwd"], t["tw_fwd"], t["coarse_fwd"],
    )
    got = lax.all_to_all(sent, ALL, split_axis=0, concat_axis=0, tiled=True)
    facet = lax.axis_index("facet").astype(jnp.int32).reshape(1)
    whole = lambda *shape: pl.BlockSpec(shape, lambda i, f: (0,) * len(shape))
    answer = pl.pallas_call(
        owner_kernel,
        out_shape=message,
        grid_spec=pltpu.PrefetchScalarGridSpec(
            num_scalar_prefetch=1,
            grid=(1,),
            in_specs=[
                whole(NDEV, ROWS_MSG, LANES),
                pl.BlockSpec((1, 4 * SUBG, NQ * RD), lambda i, f: (f[0], 0, 0)),
                pl.BlockSpec((1, NQ * RD, 4 * SUBG), lambda i, f: (f[0], 0, 0)),
            ],
            out_specs=whole(NDEV, ROWS_MSG, LANES),
            scratch_shapes=[
                pltpu.VMEM((NDEV * 8, LANES), F32),
                pltpu.VMEM((2 * SUBG, NV), F32),
                pltpu.VMEM((8, LANES), F32),
                pltpu.VMEM((2 * SUBG, NV), F32),
                pltpu.VMEM((2 * SUBG, NV), BF),
                pltpu.VMEM((2 * SUBG, NV), BF),
            ],
        ),
        compiler_params=limit,
        name="owner",
    )(facet, got, t["row_fwd"], t["row_adj"])
    back = lax.all_to_all(answer, ALL, split_axis=0, concat_axis=0, tiled=True)
    facet_adjoint, residual = pl.pallas_call(
        facet_kernel,
        out_shape=(
            jax.ShapeDtypeStruct((1, 2, RD, NA * LANES), F32),
            jax.ShapeDtypeStruct((2, NV), F32),
        ),
        in_specs=[SMEM] + [VMEM] * 5,
        out_specs=(VMEM, VMEM),
        scratch_shapes=[
            pltpu.VMEM((NQ * RD, LANES), F32),
            pltpu.VMEM((NDEV * 8, LANES), F32),
            pltpu.VMEM((4 * NA * 8, LANES), F32),
        ],
        compiler_params=limit,
        name="facet",
    )(offsets, back, meta, t["coarse_adj"], t["tw_adj"], t["col_adj"])
    return (facet_adjoint, residual)


def solution(mesh):
    placed = (
        P("facet", None, "sub", None),
        P("facet", None),
        P(None, ALL),
        P(None, ALL),
        P(ALL, None),
        P(ALL),
    )
    return jax.shard_map(
        on_device,
        mesh=mesh,
        in_specs=placed,
        out_specs=(P("facet", None, "sub", None), P(None, ALL)),
        check_vma=False,
    )
```

time: 952 us -> 65.3 us (0.07)
  waiting for transfers between devices: 572 us -> 16.2 us
  other arithmetic: 158 us -> 0 us
  local copies, waits for them, and re-layouts: 110 us -> 6.98 us
  matrix products: 55.9 us -> 0 us
  blocking collectives: 0 us -> 20.8 us
  starting transfers between devices: 28.9 us -> 11.5 us
  between operations: 15.5 us -> 0.71 us
    reduce_scatter x1 -> x0, waiting for transfers between devices: 539 us -> none  [on_device(): lax.psum_scatter(arranged, ('facet', 'sub'), scatter_dimension=0, tiled=T...]
    convert_element_type x40 -> x0, other arithmetic: 70.2 us -> none  [the longest x3 38.6 us: phase_pair(): (jnp.sin(angles) * factor).astype(jnp.bfloat16)]
    gather x13 -> x0, local copies, waits for them, and re-layouts: 57.3 us -> none  [the longest x11 49.8 us: on_device(): first_seen = jnp.searchsorted(sorted_ids, sorted_ids, side='left')]
    dot_general x24 -> x0, matrix products: 55.9 us -> none  [the longest x8 24.5 us: one_group(): jnp.dot(joined, forward_matrix, preferred_element_type=jnp.float32)]
    concatenate x5 -> x0, other arithmetic: 32.9 us -> none  [the longest x1 18.2 us: column_adjoint(): jnp.concatenate([jnp.concatenate([fine_cos.T, -fine_sin.T], 1), jnp.conca...]
    neg x4 -> x0, other arithmetic: 29 us -> none  [the longest x1 18.9 us: column_forward(): -fine_sin]
    all_to_all x0 -> x1, blocking collectives: none -> 20.8 us  [on_device(): back = lax.all_to_all(answer, ALL, split_axis=0, concat_axis=0, tiled=True)]
    all_to_all x3 -> x1, starting transfers between devices: 28.8 us -> 11.5 us  [on_device(): got = lax.all_to_all(sent, ALL, split_axis=0, concat_axis=0, tiled=True)]
  transfers between devices with their start and end apart: 5 -> 1, of which waited for: 4 -> 1; matrix products, arithmetic and copies ran while one was open for 13% -> 0% of each run, Pallas kernels for 0% -> 0%
where the time goes in v1:
time: 65.3 us; the launch traced here: 64.7 us
  blocking collectives  20.8 us (32%)
  waiting for transfers between devices  16.2 us (25%)
  starting transfers between devices  11.5 us (18%)
  Pallas kernels  8.54 us (13%)
  local copies, waits for them, and re-layouts  6.98 us (11%)
  between operations  0.71 us (1%)
    all_to_all x1, blocking collectives, on_device(): back = lax.all_to_all(answer, ALL, split_axis=0, concat_axis=0, tiled=True)  20.8 us
    all_to_all x1, waiting for transfers between devices, on_device(): got = lax.all_to_all(sent, ALL, split_axis=0, concat_axis=0, tiled=True)  16.2 us
    all_to_all x1, starting transfers between devices, on_device(): got = lax.all_to_all(sent, ALL, split_axis=0, concat_axis=0, tiled=True)  11.5 us
    unnamed x28, local copies, waits for them, and re-layouts  6.24 us
    pallas_call x1, Pallas kernels, on_device(): pl.pallas_call(facet_kernel, out_shape=(jax.ShapeDtypeStruct((1, 2, RD, N...  3.23 us
    pallas_call x1, Pallas kernels, on_device(): pl.pallas_call(send_kernel, out_shape=(message, jax.ShapeDtypeStruct((8,...  2.78 us
    pallas_call x1, Pallas kernels, on_device(): pl.pallas_call(owner_kernel, out_shape=message, grid_spec=pltpu.PrefetchS...  2.53 us
  transfers between devices with their start and end apart: 1, of which 1 were waited for; matrix products, arithmetic and copies ran while one was open for 0% of the time, Pallas kernels for 0%

profile of v1, /device:TPU:1, one launch (start us, length us, event | category | flops | bytes accessed | tf_op | source)
XLA Modules:
  0.0 64.7 jit_solution(7476436400243211609)
XLA Ops:
  0.6 0.0 copy-start.7
  0.6 0.7 %copy.16.clip_ref = s32[32,1]{1,0:T(8,128)S(1)} copy(s32[32,1]{0,1:T(1,128)} %bitcast.4) | data formatting | bytes 256 | tf_op jit(solution)/shard_map/reshape | solution.py:379
  1.4 0.0 copy-start.13
  1.4 0.0 copy-done.7
  1.4 0.6 %copy-done.13 = s32[1,2]{1,0:T(1,128)S(1)} copy-done((s32[1,2]{1,0:T(1,128)S(1)}, s32[1,2]{1,0:T(1,128)}, u32[]{:S(2)}) %copy-start.13) | copy-done | bytes 32
  2.0 0.0 copy-start.3
  2.0 1.0 %copy-done.3 = bf16[1,2,16,8192]{3,2,1,0:T(8,128)(2,1)S(1)} copy-done((bf16[1,2,16,8192]{3,2,1,0:T(8,128)(2,1)S(1)}, bf16[1,2,16,8192]{3,2,1,0:T(8,128)(2,1)}, u32[]{:S(2)}) %copy-start.3) | copy-done | bytes 524312
  3.1 0.0 copy-start.5
  3.1 0.8 %copy-done.5 = f32[2,64,128]{2,1,0:T(8,128)S(1)} copy-done((f32[2,64,128]{2,1,0:T(8,128)S(1)}, f32[2,64,128]{2,1,0:T(8,128)}, u32[]{:S(2)}) %copy-start.5) | copy-done | bytes 65560
  3.9 0.0 copy-start.9
  3.9 0.7 %copy-done.9 = bf16[32,256]{1,0:T(8,128)(2,1)S(1)} copy-done((bf16[32,256]{1,0:T(8,128)(2,1)S(1)}, bf16[32,256]{1,0:T(8,128)(2,1)}, u32[]{:S(2)}) %copy-start.9) | copy-done | bytes 16408
  4.6 0.0 copy-start.10
  4.6 0.7 %copy-done.10 = f32[2,1024]{1,0:T(2,128)S(1)} copy-done((f32[2,1024]{1,0:T(2,128)S(1)}, f32[2,1024]{1,0:T(2,128)}, u32[]{:S(2)}) %copy-start.10) | copy-done | bytes 8216
  5.3 0.0 copy-start.11
  5.3 0.7 %copy-done.11 = f32[2,1024]{1,0:T(2,128)S(1)} copy-done((f32[2,1024]{1,0:T(2,128)S(1)}, f32[2,1024]{1,0:T(2,128)}, u32[]{:S(2)}) %copy-start.11) | copy-done | bytes 8216
  6.0 0.0 copy-start.12
  6.0 0.7 %copy-done.12 = s32[1024,1]{0,1:T(1,128)S(1)} copy-done((s32[1024,1]{0,1:T(1,128)S(1)}, s32[1024,1]{0,1:T(1,128)}, u32[]{:S(2)}) %copy-start.12) | copy-done | bytes 4120
  6.7 0.0 copy-start
  6.7 0.0 copy-start.1
  6.7 2.8 %send.1 = (bf16[128,24,128]{2,1,0:T(8,128)(2,1)S(1)}, s32[8,1024]{1,0:T(8,128)S(1)}) custom-call(s32[1,2]{1,0:T(1,128)S(1)} %copy-done.13, bf16[1,2,16,8192]{3,2,1,0:T(8,128)(2,1)S(1)} %copy-done.3, f32[2,1024]{1,0:T(2,128)S(1)} %copy-done.10, f32[2,1024]{1,0:T(2,128)S(1)} %copy-done.11, s32[1,1024]{1,0:T(1,128)S(1)} %bitcast.3, s32[32,1]{1,0:T(8,128)S(1)} %copy.16.clip_ref, ...), custom_call_target="tpu_custom_call" | custom-call | tf_op jit(solution)/shard_map/send/pallas_call | solution.py:365
  9.5 0.0 copy-start.2
  9.5 0.9 %copy-done.2 = bf16[128,24,128]{2,1,0:T(8,128)(2,1)} copy-done((bf16[128,24,128]{2,1,0:T(8,128)(2,1)}, bf16[128,24,128]{2,1,0:T(8,128)(2,1)S(1)}, u32[]{:S(2)}) %copy-start.2) | copy-done | bytes 786456
  10.4 11.5 %all-to-all-start = ((bf16[128,24,128]{2,1,0:T(8,128)(2,1)}), bf16[128,24,128]{2,1,0:T(8,128)(2,1)S(1)}, u32[]{:S(2)}, u32[]{:S(2)}) async-start(bf16[128,24,128]{2,1,0:T(8,128)(2,1)} %copy-done.2), calls=%async_computation | async-start | bytes 1572864 | tf_op jit(solution)/shard_map/all_to_all | solution.py:381
  21.9 16.2 %all-to-all-done.got_ref = bf16[128,24,128]{2,1,0:T(8,128)(2,1)S(1)} async-done(((bf16[128,24,128]{2,1,0:T(8,128)(2,1)}), bf16[128,24,128]{2,1,0:T(8,128)(2,1)S(1)}, u32[]{:S(2)}, u32[]{:S(2)}) %all-to-all-start) | async-done | bytes 786464 | tf_op jit(solution)/shard_map/all_to_all | solution.py:381
  38.1 0.0 copy-done
  38.1 0.0 copy-done.1
  38.1 2.5 %owner.1 = bf16[128,24,128]{2,1,0:T(8,128)(2,1)S(1)} custom-call(s32[1]{0:T(128)} %bitcast.facet_ref, bf16[128,24,128]{2,1,0:T(8,128)(2,1)S(1)} %all-to-all-done.got_ref, bf16[4,256,512]{2,1,0:T(8,128)(2,1)S(1)} %copy-done.1, bf16[4,512,256]{2,1,0:T(8,128)(2,1)S(1)} %copy-done), custom_call_target="tpu_custom_call" | custom-call | tf_op jit(solution)/shard_map/owner/pallas_call | solution.py:384
  40.6 0.0 copy-start.4
  40.7 0.0 copy-start.6
  40.7 0.0 copy-start.8
  40.7 20.8 %all_to_all.10.got_ref = bf16[128,24,128]{2,1,0:T(8,128)(2,1)S(1)} all-to-all(bf16[128,24,128]{2,1,0:T(8,128)(2,1)S(1)} %owner.1), channel_id=1, replica_groups=mesh['facet'=4,'sub'=32] {'facet','sub'}, dimensions={0} | all-to-all | bytes 1572864 | tf_op jit(solution)/shard_map/all_to_all | solution.py:408
  61.5 0.0 copy-done.4
  61.5 0.0 copy-done.6
  61.5 0.0 copy-done.8
  61.5 3.2 %facet.1 = (f32[1,2,16,8192]{3,2,1,0:T(8,128)}, f32[2,1024]{1,0:T(2,128)}) custom-call(s32[1,2]{1,0:T(1,128)S(1)} %copy-done.13, bf16[128,24,128]{2,1,0:T(8,128)(2,1)S(1)} %all_to_all.10.got_ref, s32[8,1024]{1,0:T(8,128)S(1)} %get-tuple-element.5.meta_ref, bf16[256,32]{1,0:T(8,128)(2,1)S(1)} %copy-done.6, f32[2,128,128]{2,1,0:T(8,128)S(1)} %copy-done.4, ...), custom_call_target="tpu_custom_call" | custom-call | tf_op jit(solution)/shard_map/facet/pallas_call | solution.py:409
Async XLA Ops:
  0.6 0.8 %copy-start.7 = (bf16[128,128]{1,0:T(8,128)(2,1)S(1)}, bf16[128,128]{1,0:T(8,128)(2,1)}, u32[]{:S(2)}) copy-start(bf16[128,128]{1,0:T(8,128)(2,1)} %constant.22.clone.col_ref) | copy-start | bytes 98308
  1.4 0.7 %copy-start.13 = (s32[1,2]{1,0:T(1,128)S(1)}, s32[1,2]{1,0:T(1,128)}, u32[]{:S(2)}) copy-start(s32[1,2]{1,0:T(1,128)} %off_ref.3) | copy-start | bytes 28
  2.0 1.0 %copy-start.3 = (bf16[1,2,16,8192]{3,2,1,0:T(8,128)(2,1)S(1)}, bf16[1,2,16,8192]{3,2,1,0:T(8,128)(2,1)}, u32[]{:S(2)}) copy-start(bf16[1,2,16,8192]{3,2,1,0:T(8,128)(2,1)} %slab_ref.1) | copy-start | bytes 1572868
  3.1 0.8 %copy-start.5 = (f32[2,64,128]{2,1,0:T(8,128)S(1)}, f32[2,64,128]{2,1,0:T(8,128)}, u32[]{:S(2)}) copy-start(f32[2,64,128]{2,1,0:T(8,128)} %constant.24.clone.tw_ref) | copy-start | bytes 196612
  3.9 0.7 %copy-start.9 = (bf16[32,256]{1,0:T(8,128)(2,1)S(1)}, bf16[32,256]{1,0:T(8,128)(2,1)}, u32[]{:S(2)}) copy-start(bf16[32,256]{1,0:T(8,128)(2,1)} %constant.26.clone.coarse_ref) | copy-start | bytes 49156
  4.6 0.7 %copy-start.10 = (f32[2,1024]{1,0:T(2,128)S(1)}, f32[2,1024]{1,0:T(2,128)}, u32[]{:S(2)}) copy-start(f32[2,1024]{1,0:T(2,128)} %pos_ref.1) | copy-start | bytes 24580
  5.3 0.7 %copy-start.11 = (f32[2,1024]{1,0:T(2,128)S(1)}, f32[2,1024]{1,0:T(2,128)}, u32[]{:S(2)}) copy-start(f32[2,1024]{1,0:T(2,128)} %obs_ref.1) | copy-start | bytes 24580
  6.0 0.7 %copy-start.12 = (s32[1024,1]{0,1:T(1,128)S(1)}, s32[1024,1]{0,1:T(1,128)}, u32[]{:S(2)}) copy-start(s32[1024,1]{0,1:T(1,128)} %param.18) | copy-start | bytes 12292
  6.7 31.4 %copy-start = (bf16[4,512,256]{2,1,0:T(8,128)(2,1)S(1)}, bf16[4,512,256]{2,1,0:T(8,128)(2,1)}, u32[]{:S(2)}) copy-start(bf16[4,512,256]{2,1,0:T(8,128)(2,1)} %constant.29.clone.adj_ref) | copy-start | bytes 3145732
  6.7 31.4 %copy-start.1 = (bf16[4,256,512]{2,1,0:T(8,128)(2,1)S(1)}, bf16[4,256,512]{2,1,0:T(8,128)(2,1)}, u32[]{:S(2)}) copy-start(bf16[4,256,512]{2,1,0:T(8,128)(2,1)} %constant.28.clone.fwd_ref) | copy-start | bytes 3145732
  9.5 0.9 %copy-start.2 = (bf16[128,24,128]{2,1,0:T(8,128)(2,1)}, bf16[128,24,128]{2,1,0:T(8,128)(2,1)S(1)}, u32[]{:S(2)}) copy-start(bf16[128,24,128]{2,1,0:T(8,128)(2,1)S(1)} %get-tuple-element.4) | copy-start | bytes 2359300
  10.4 27.7 %all-to-all-start = ((bf16[128,24,128]{2,1,0:T(8,128)(2,1)}), bf16[128,24,128]{2,1,0:T(8,128)(2,1)S(1)}, u32[]{:S(2)}, u32[]{:S(2)}) async-start(bf16[128,24,128]{2,1,0:T(8,128)(2,1)} %copy-done.2), calls=%async_computation | async-start | bytes 1572864 | tf_op jit(solution)/shard_map/all_to_all | solution.py:381
  40.6 20.9 %copy-start.4 = (f32[2,128,128]{2,1,0:T(8,128)S(1)}, f32[2,128,128]{2,1,0:T(8,128)}, u32[]{:S(2)}) copy-start(f32[2,128,128]{2,1,0:T(8,128)} %constant.25.clone.tw_ref) | copy-start | bytes 393220
  40.7 20.8 %copy-start.6 = (bf16[256,32]{1,0:T(8,128)(2,1)S(1)}, bf16[256,32]{1,0:T(8,128)(2,1)}, u32[]{:S(2)}) copy-start(bf16[256,32]{1,0:T(8,128)(2,1)} %constant.27.clone.coarse_ref) | copy-start | bytes 49156
  40.7 20.8 %copy-start.8 = (bf16[128,128]{1,0:T(8,128)(2,1)S(1)}, bf16[128,128]{1,0:T(8,128)(2,1)}, u32[]{:S(2)}) copy-start(bf16[128,128]{1,0:T(8,128)(2,1)} %constant.23.clone.col_ref) | copy-start | bytes 98308

commit v2 on v1

v2 whole, which is shorter than its diff:
```python
import math

import jax
import jax.numpy as jnp
import numpy as np
from jax import lax
from jax.experimental import pallas as pl
from jax.experimental.pallas import tpu as pltpu
from jax.sharding import PartitionSpec as P

N_IMG = 32768
SUBG = 64
VIS_BLOCK = 32
LANES = 128
NQ = 32
NF = 4
NDEV = 128
RD = 16
NA = 64
NV = 1024
SLOT = 16
ROWS_MSG = 18
A_HIGH = 3 * 5 * SLOT
TWO_PI = 2.0 * math.pi
BF = jnp.bfloat16
F32 = jnp.float32
ALL = ("facet", "sub")


def unit(index, period):
    angle = TWO_PI * (np.asarray(index, np.int64) % period) / period
    return np.cos(angle), np.sin(angle)


def host_tables():
    block = np.arange(NA)
    lane = np.arange(LANES)
    fine = np.arange(SUBG)
    coarse = np.arange(NQ)
    c, s = unit(fine[:, None] * block[None, :], 256)
    c, s = c / 64.0, s / 64.0
    col_fwd = np.block([[c, s], [-s, c]])
    col_adj = np.block([[c.T, -s.T], [s.T, c.T]])
    tw_c, tw_s = unit(fine[:, None] * lane[None, :], N_IMG)
    twiddle_fwd = np.concatenate([tw_c, -tw_s], 0)
    twiddle_adj = np.stack([np.tile(tw_c.T, (1, 2)), np.tile(tw_s.T, (1, 2))])
    wc, ws = unit(coarse[:, None] * lane[None, :], 32)
    column = np.concatenate([col_fwd, wc, -ws], 0)
    coarse_adj = np.concatenate([wc.T, ws.T], 0)
    k_row = (np.arange(8)[:, None] * 4096 + fine[None, :]).reshape(NF, 2 * SUBG)
    rc, rs = unit(k_row[:, :, None] * np.arange(NQ * RD)[None, None, :], N_IMG)
    swapped = lambda x: x.reshape(NF, 2 * SUBG, NQ, RD).swapaxes(2, 3).reshape(x.shape) / 64.0
    rc, rs = swapped(rc), swapped(rs)
    row_fwd = np.concatenate([rc, -rs], 1)
    row_adj = np.ascontiguousarray(row_fwd.transpose(0, 2, 1))
    bf = lambda x: np.asarray(x, np.float32).astype(jnp.bfloat16)
    return dict(
        column=bf(column),
        col_adj=bf(col_adj),
        tw_fwd=np.asarray(twiddle_fwd, np.float32),
        tw_adj=np.asarray(twiddle_adj, np.float32),
        coarse_adj=bf(coarse_adj),
        row_fwd=bf(row_fwd),
        row_adj=bf(row_adj),
    )


def sincos_turn(turn):
    quarter = jnp.floor(turn * 4.0 + 0.5)
    y = (turn - quarter * 0.25) * TWO_PI
    y2 = y * y
    s = y * (1.0 + y2 * (-1.0 / 6 + y2 * (1.0 / 120 + y2 * (-1.0 / 5040 + y2 * (1.0 / 362880)))))
    c = 1.0 + y2 * (-0.5 + y2 * (1.0 / 24 + y2 * (-1.0 / 720 + y2 * (1.0 / 40320))))
    turns = quarter.astype(jnp.int32)
    odd = (turns & 1) == 1
    cos = jnp.where(odd, s, c)
    sin = jnp.where(odd, c, s)
    cos = jnp.where(((turns + 1) & 2) == 2, -cos, cos)
    sin = jnp.where((turns & 2) == 2, -sin, sin)
    return cos, sin


def phase_of(offset, frequency):
    index = (offset * frequency) & (N_IMG - 1)
    return sincos_turn(index.astype(F32) * (1.0 / N_IMG))


def swap(x):
    return pltpu.roll(x, SUBG, x.ndim - 1)


def iota(shape, dim):
    return lax.broadcasted_iota(jnp.int32, shape, dim)


def split3(x):
    high = x.astype(BF)
    rest = x - high.astype(F32)
    middle = rest.astype(BF)
    low = (rest - middle.astype(F32)).astype(BF)
    return high, middle, low


def lane_sign(rows):
    return jnp.where(iota((rows, LANES), 1) < SUBG, 1.0, -1.0).astype(F32)


def send_kernel(
    off_hbm, slab_hbm, pos_hbm, obs_hbm, ids_hbm, clip_hbm, table_hbm, tw_hbm,
    msg_ref, meta_ref, off_ref, slab_ref, pos_ref, obs_ref, ids_ref, clip_ref, table_ref, tw_ref,
    wide, flat, sems,
):
    pairs = [
        (ids_hbm, ids_ref), (clip_hbm, clip_ref), (pos_hbm, pos_ref), (obs_hbm, obs_ref),
        (off_hbm, off_ref), (slab_hbm, slab_ref), (table_hbm, table_ref), (tw_hbm, tw_ref),
    ]
    copies = [pltpu.make_async_copy(a, b, sems.at[i]) for i, (a, b) in enumerate(pairs)]
    for copy in copies:
        copy.start()

    copies[0].wait()
    ids = ids_ref[...]
    upper = jnp.where(iota((LANES, LANES), 0) < iota((LANES, LANES), 1), 1.0, 0.0).astype(BF)
    counter = jnp.concatenate([upper, jnp.ones((LANES, LANES), BF)], 1)
    before = jnp.zeros((2 * LANES, LANES), F32)
    ranks = []
    for b in range(NV // LANES):
        hot = iota((2 * LANES, LANES), 0) == ids[:, b * LANES:(b + 1) * LANES]
        hot_f = jnp.where(hot, 1.0, 0.0)
        count = jnp.dot(hot_f.astype(BF), counter, preferred_element_type=F32)
        ranks.append(jnp.sum(hot_f * (count[:, :LANES] + before), 0, keepdims=True))
        before = before + count[:, LANES:]
    rank = jnp.concatenate(ranks, 1).astype(jnp.int32)
    owner = (ids >> 6) * NQ + (ids & (NQ - 1))
    place = ((ids >> 5) & 1) * 8 + rank
    meta_ref[0:1, :] = owner
    meta_ref[1:2, :] = place
    here = iota((SLOT, NV), 0) == place
    copies[1].wait()
    n_block = NV // VIS_BLOCK
    clip = jnp.broadcast_to(clip_ref[...].astype(F32) * 0.25, (n_block, n_block))
    same = iota((n_block, n_block), 0) == iota((n_block, n_block), 1)
    clip = jnp.sum(jnp.where(same, clip, 0.0), 1, keepdims=True)
    block = iota((n_block, NV), 1) // VIS_BLOCK == iota((n_block, NV), 0)
    level = jnp.sum(jnp.where(block, clip, 0.0), 0, keepdims=True)
    copies[2].wait()
    copies[3].wait()
    values = [pos_ref[0:1, :], pos_ref[1:2, :], obs_ref[0:1, :], obs_ref[1:2, :], level]
    pieces = [split3(v) for v in values]
    own = jnp.where(iota((NDEV, NV), 0) == owner, 1.0, 0.0).astype(BF)
    table = jnp.concatenate(
        [jnp.where(here, p[part].astype(F32), 0.0).astype(BF) for part in range(3) for p in pieces]
        + [jnp.zeros((SLOT, NV), BF)], 0
    )
    copies[4].wait()
    meta_ref[2:3, :] = jnp.full((1, NV), off_ref[0, 1], jnp.int32)
    payload = lax.dot_general(own, table, (((1,), (1,)), ((), ())), preferred_element_type=F32)
    lane = iota((NDEV, LANES), 1)
    tail = payload[:, LANES:]
    tail = jnp.where(lane == A_HIGH - LANES, (off_ref[0, 0] >> 8).astype(F32), tail)
    tail = jnp.where(lane == A_HIGH + 1 - LANES, (off_ref[0, 0] & 255).astype(F32), tail)
    flat[pl.ds(RD, NDEV, stride=ROWS_MSG), :] = payload[:, :LANES]
    flat[pl.ds(RD + 1, NDEV, stride=ROWS_MSG), :] = tail

    freq = iota((NQ, LANES), 0) * (N_IMG // NQ) + (iota((NQ, LANES), 1) & (SUBG - 1))
    ph_c, ph_s = phase_of(off_ref[0, 1], freq)
    ph_s = ph_s * lane_sign(NQ)
    for copy in copies[5:]:
        copy.wait()
    for part in range(2):
        for a in range(NA):
            wide[part, a * RD:(a + 1) * RD, :] = slab_ref[
                0, part, :, a * LANES:(a + 1) * LANES
            ].astype(F32)
    tw_c, tw_s = tw_ref[:SUBG], tw_ref[SUBG:]
    col = table_ref[:LANES]
    coarse = jnp.concatenate([table_ref[LANES:LANES + NQ], table_ref[LANES + NQ:]], 1)
    group = 4
    for base in range(0, RD, group):
        cols = []
        for r in range(base, base + group):
            cols.append(
                jnp.concatenate(
                    [wide[0, pl.ds(r, NA, stride=RD), :], wide[1, pl.ds(r, NA, stride=RD), :]], 0
                ).astype(BF)
            )
        y = jnp.dot(col, jnp.concatenate(cols, 1), preferred_element_type=F32)
        stacked = []
        for i in range(group):
            yr = y[:SUBG, i * LANES:(i + 1) * LANES]
            yi = y[SUBG:, i * LANES:(i + 1) * LANES]
            zr = yr * tw_c - yi * tw_s
            zi = yr * tw_s + yi * tw_c
            stacked.append(jnp.concatenate([zr, -zi], 1).astype(BF))
            stacked.append(jnp.concatenate([zi, zr], 1).astype(BF))
        out = lax.dot_general(
            coarse, jnp.concatenate(stacked, 0), (((1,), (1,)), ((), ())),
            preferred_element_type=F32,
        )
        for i in range(group):
            piece = out[:, i * LANES:(i + 1) * LANES]
            piece = piece * ph_c + swap(piece) * ph_s
            for f in range(NF):
                flat[pl.ds(f * NQ * ROWS_MSG + base + i, NQ, stride=ROWS_MSG), :] = piece
    msg_ref[...] = flat[...].astype(BF)


def powers(turn):
    sub = iota((8, LANES), 0).astype(F32)
    low = sincos_turn(turn * sub)
    high = sincos_turn(turn * (sub * 8.0))
    re, im = [], []
    for a in range(8):
        hr, hi = high[0][a:a + 1, :], high[1][a:a + 1, :]
        re.append(hr * low[0] - hi * low[1])
        im.append(hr * low[1] + hi * low[0])
    return jnp.concatenate(re, 0), jnp.concatenate(im, 0)


def owner_kernel(
    got_ref, fwd_hbm, adj_hbm, msg_ref, fwd_ref, adj_ref, flat, left, inner, phasor, basis, sems,
):
    facet = lax.axis_index("facet")
    tables = [
        pltpu.make_async_copy(fwd_hbm.at[facet], fwd_ref, sems.at[0]),
        pltpu.make_async_copy(adj_hbm.at[facet], adj_ref, sems.at[1]),
    ]
    for copy in tables:
        copy.start()
    sign = lane_sign(2 * SUBG)
    flat[...] = got_ref[...].astype(F32)
    got = jnp.concatenate(
        [flat[pl.ds(RD, NDEV, stride=ROWS_MSG), :].T, flat[pl.ds(RD + 1, NDEV, stride=ROWS_MSG), :].T], 0
    )
    row = iota((2 * SUBG, LANES), 0)
    k_row = (facet * 2 + row // SUBG) * (N_IMG // 8) + (row & (SUBG - 1))
    offset = got[A_HIGH:A_HIGH + 1] * 256.0 + got[A_HIGH + 1:A_HIGH + 2]
    rho_c, rho_s = phase_of(offset.astype(jnp.int32), k_row)
    n = 5 * SLOT
    got = got[:n] + got[n:2 * n] + got[2 * n:3 * n]

    def rows_of(c, l):
        return got[c * SLOT + l * 8:c * SLOT + l * 8 + 8, :]

    for l in range(2):
        u, w = rows_of(0, l) * (1.0 / SUBG), rows_of(1, l) * (1.0 / SUBG)
        for k in range(8):
            at = slice(k * LANES, (k + 1) * LANES)
            cr, ci = powers(w[k:k + 1, :])
            basis[l, 0:SUBG, at] = (cr * 0.125).astype(BF)
            basis[l, SUBG:, at] = (ci * 0.125).astype(BF)
            lr, li = powers(u[k:k + 1, :])
            left[l, 0:SUBG, at] = lr * 0.125
            left[l, SUBG:, at] = li * 0.125

    tables[0].wait()
    real = jnp.zeros((2 * SUBG, LANES), F32)
    turned = jnp.zeros((2 * SUBG, LANES), F32)
    for f in range(NF):
        spectra = jnp.concatenate(
            [
                flat[pl.ds(f * NQ * ROWS_MSG + r, NQ, stride=ROWS_MSG), :].astype(BF)
                for r in range(RD)
            ], 0
        )
        both = jnp.dot(fwd_ref[...], spectra, preferred_element_type=F32)
        rc, rs = rho_c[:, f * NQ:f * NQ + 1], rho_s[:, f * NQ:f * NQ + 1]
        first, second = both[:2 * SUBG], both[2 * SUBG:]
        real = real + (rc * first + rs * second)
        turned = turned + (rc * second - rs * first)
    subgrids = (real - swap(turned) * sign).astype(BF).astype(F32)

    sums = []
    returned = [[None, None], [None, None]]
    for l in range(2):
        obs_r, obs_i, level = [rows_of(c, l) for c in range(2, 5)]
        sub = subgrids[l * SUBG:(l + 1) * SUBG]
        matrix = jnp.concatenate([sub * sign[:SUBG], swap(sub)], 0).astype(BF)
        inner[l] = jnp.dot(matrix, basis[l], preferred_element_type=F32)
        pred_r, pred_i = [], []
        for k in range(8):
            at = slice(k * LANES, (k + 1) * LANES)
            lr, li = left[l, 0:SUBG, at], left[l, SUBG:, at]
            ir, ii = inner[l, 0:SUBG, at], inner[l, SUBG:, at]
            pred_r.append(jnp.sum(lr * ir - li * ii, 0, keepdims=True))
            pred_i.append(jnp.sum(lr * ii + li * ir, 0, keepdims=True))
        mis_r = obs_r - jnp.concatenate(pred_r, 0)
        mis_i = obs_i - jnp.concatenate(pred_i, 0)
        live = level > 0.0
        threshold = jnp.where(live, level, 1.0)
        magnitude = jnp.sqrt(mis_r * mis_r + mis_i * mis_i)
        weight = jnp.where(live, threshold / jnp.maximum(magnitude, threshold), 0.0)
        wr, wi = weight * mis_r, weight * mis_i
        returned[0][l], returned[1][l] = wr, wi
        for k in range(8):
            at = slice(k * LANES, (k + 1) * LANES)
            lr, li = left[l, 0:SUBG, at], left[l, SUBG:, at]
            vr, vi = wr[k:k + 1, :], wi[k:k + 1, :]
            phasor[l, 0:SUBG, at] = (lr * vr + li * vi).astype(BF)
            phasor[l, SUBG:, at] = (lr * vi - li * vr).astype(BF)
        product = lax.dot_general(
            phasor[l], basis[l], (((1,), (1,)), ((), ())), preferred_element_type=F32
        )
        sums.append(product[:SUBG] * sign[:SUBG] + swap(product[SUBG:]))
    corrected = jnp.concatenate(sums, 0)
    corrected = corrected.astype(BF).astype(F32)
    cols = []
    for f in range(NF):
        rc, rs = rho_c[:, f * NQ:f * NQ + 1], rho_s[:, f * NQ:f * NQ + 1]
        d = corrected * rc - swap(corrected) * (sign * rs)
        cols.append(jnp.concatenate([d, swap(d) * sign], 0).astype(BF))
    tables[1].wait()
    images = jnp.dot(adj_ref[...], jnp.concatenate(cols, 1), preferred_element_type=F32)
    for f in range(NF):
        for r in range(RD):
            flat[pl.ds(f * NQ * ROWS_MSG + r, NQ, stride=ROWS_MSG), :] = images[
                r * NQ:(r + 1) * NQ, f * LANES:(f + 1) * LANES
            ]
    back = jnp.concatenate([returned[0][0], returned[0][1], returned[1][0], returned[1][1]], 0)
    back = [part.astype(F32) for part in split3(back)]
    back = jnp.concatenate(back + [jnp.zeros((2 * SLOT, LANES), F32)], 0).T
    flat[pl.ds(RD, NDEV, stride=ROWS_MSG), :] = back
    flat[pl.ds(RD + 1, NDEV, stride=ROWS_MSG), :] = jnp.zeros((NDEV, LANES), F32)
    msg_ref[...] = flat[...].astype(BF)


def facet_kernel(
    got_ref, meta_ref, coarse_ref, tw_ref, col_ref, out_hbm, res_ref, flat, turned, out_ref, sems,
):
    flat[...] = got_ref[...].astype(F32)
    freq = iota((NQ, LANES), 0) * (N_IMG // NQ) + (iota((NQ, LANES), 1) & (SUBG - 1))
    ph_c, ph_s = phase_of(meta_ref[2:3, :LANES], freq)
    ph_s = -ph_s * lane_sign(NQ)
    tw_c, tw_s = tw_ref[0], tw_ref[1]
    sign = lane_sign(LANES)
    group = 4
    copies = []
    for base in range(0, RD, group):
        images = []
        for r in range(base, base + group):
            image = flat[pl.ds(r, NQ, stride=ROWS_MSG), :]
            for f in range(1, NF):
                image = image + flat[pl.ds(f * NQ * ROWS_MSG + r, NQ, stride=ROWS_MSG), :]
            images.append((image * ph_c + swap(image) * ph_s).astype(BF))
        spread = jnp.dot(coarse_ref[...], jnp.concatenate(images, 1), preferred_element_type=F32)
        stacked = []
        for i in range(group):
            first = spread[:LANES, i * LANES:(i + 1) * LANES]
            second = spread[LANES:, i * LANES:(i + 1) * LANES]
            z = (tw_c * first - tw_s * second) - swap(tw_s * first + tw_c * second) * sign
            stacked.append(z.astype(BF))
        out = lax.dot_general(
            col_ref[...], jnp.concatenate(stacked, 0), (((1,), (1,)), ((), ())),
            preferred_element_type=F32,
        )
        for i in range(group):
            r = base + i
            for part in range(2):
                at = (part * 2 + r // 8) * NA * 8 + r % 8
                turned[pl.ds(at, NA, stride=8), :] = out[
                    part * NA:(part + 1) * NA, i * LANES:(i + 1) * LANES
                ]
        if (base + group) % 8 == 0:
            half = base // 8
            for part in range(2):
                where = slice(half * 8, half * 8 + 8)
                for a in range(NA):
                    at = ((part * 2 + half) * NA + a) * 8
                    out_ref[part, where, a * LANES:(a + 1) * LANES] = turned[at:at + 8, :]
                copy = pltpu.make_async_copy(
                    out_ref.at[part, where, :], out_hbm.at[0, part, where, :],
                    sems.at[half * 2 + part],
                )
                copy.start()
                copies.append(copy)

    n = 2 * SLOT
    back = flat[pl.ds(RD, NDEV, stride=ROWS_MSG), :].T[:3 * n]
    owner, place = meta_ref[0:1, :], meta_ref[1:2, :]
    own = jnp.where(iota((NDEV, NV), 0) == owner, 1.0, 0.0).astype(BF)
    found = jnp.dot(back.astype(BF), own, preferred_element_type=F32)
    found = found[:n] + found[n:2 * n] + found[2 * n:]
    here = iota((SLOT, NV), 0) == place
    for c in range(2):
        res_ref[c:c + 1, :] = jnp.sum(
            jnp.where(here, found[c * SLOT:(c + 1) * SLOT], 0.0), 0, keepdims=True
        )
    for copy in copies:
        copy.wait()


VMEM = pl.BlockSpec(memory_space=pltpu.VMEM)
HBM = pl.BlockSpec(memory_space=pltpu.MemorySpace.HBM)
TABLES = host_tables()


def in_place(arrays):
    return [pltpu.with_memory_space_constraint(x, pltpu.HBM) for x in arrays]


def exchange(message):
    pairs = message.reshape(NDEV * ROWS_MSG // 2, 2, LANES)
    return lax.all_to_all(pairs, ALL, split_axis=0, concat_axis=0, tiled=True).reshape(message.shape)


def on_device(slab, offsets, position, observed, subgrid_of, clip):
    t = {name: jnp.asarray(value) for name, value in TABLES.items()}
    limit = pltpu.CompilerParams(vmem_limit_bytes=32 << 20)
    message = jax.ShapeDtypeStruct((NDEV * ROWS_MSG, LANES), BF)
    flat = pltpu.VMEM((NDEV * ROWS_MSG, LANES), F32)
    inputs = (
        offsets, slab, position, observed, subgrid_of.reshape(1, NV),
        clip.reshape(1, NV // VIS_BLOCK), t["column"], t["tw_fwd"],
    )
    sent, meta = pl.pallas_call(
        send_kernel,
        out_shape=(message, jax.ShapeDtypeStruct((8, NV), jnp.int32)),
        in_specs=[HBM] * len(inputs),
        out_specs=(VMEM, VMEM),
        scratch_shapes=[pltpu.SMEM((1, 2), jnp.int32)]
        + [pltpu.VMEM(x.shape, x.dtype) for x in inputs[1:]]
        + [
            pltpu.VMEM((2, NA * RD, LANES), F32),
            flat,
            pltpu.SemaphoreType.DMA((len(inputs),)),
        ],
        compiler_params=limit,
        name="send",
    )(*in_place(inputs))
    got = exchange(sent)
    answer = pl.pallas_call(
        owner_kernel,
        out_shape=message,
        in_specs=[VMEM, HBM, HBM],
        out_specs=VMEM,
        scratch_shapes=[
            pltpu.VMEM((4 * SUBG, NQ * RD), BF),
            pltpu.VMEM((NQ * RD, 4 * SUBG), BF),
            flat,
            pltpu.VMEM((2, 2 * SUBG, NV), F32),
            pltpu.VMEM((2, 2 * SUBG, NV), F32),
            pltpu.VMEM((2, 2 * SUBG, NV), BF),
            pltpu.VMEM((2, 2 * SUBG, NV), BF),
            pltpu.SemaphoreType.DMA((2,)),
        ],
        compiler_params=limit,
        name="owner",
    )(got, *in_place((t["row_fwd"], t["row_adj"])))
    back = exchange(answer)
    facet_adjoint, residual = pl.pallas_call(
        facet_kernel,
        out_shape=(
            jax.ShapeDtypeStruct((1, 2, RD, NA * LANES), F32),
            jax.ShapeDtypeStruct((2, NV), F32),
        ),
        in_specs=[VMEM] * 5,
        out_specs=(HBM, VMEM),
        scratch_shapes=[
            flat,
            pltpu.VMEM((4 * NA * 8, LANES), F32),
            pltpu.VMEM((2, RD, NA * LANES), F32),
            pltpu.SemaphoreType.DMA((4,)),
        ],
        compiler_params=limit,
        name="facet",
    )(back, meta, t["coarse_adj"], t["tw_adj"], t["col_adj"])
    return (facet_adjoint, residual)


def solution(mesh):
    placed = (
        P("facet", None, "sub", None),
        P("facet", None),
        P(None, ALL),
        P(None, ALL),
        P(ALL, None),
        P(ALL),
    )
    return jax.shard_map(
        on_device,
        mesh=mesh,
        in_specs=placed,
        out_specs=(P("facet", None, "sub", None), P(None, ALL)),
        check_vma=False,
    )
```

time: 65.3 us -> 54.5 us (0.83)
  blocking collectives: 20.8 us -> 44.2 us
  waiting for transfers between devices: 16.2 us -> 0 us
  starting transfers between devices: 11.5 us -> 0 us
  local copies, waits for them, and re-layouts: 6.98 us -> 0.02 us
  Pallas kernels: 8.54 us -> 9.42 us
    all_to_all x1 -> x2, blocking collectives: 20.8 us -> 44.2 us  [exchange(): lax.all_to_all(pairs, ALL, split_axis=0, concat_axis=0, tiled=True)]
    all_to_all x1 -> x0, waiting for transfers between devices: 16.2 us -> none  [on_device(): got = lax.all_to_all(sent, ALL, split_axis=0, concat_axis=0, tiled=True)]
    all_to_all x1 -> x0, starting transfers between devices: 11.5 us -> none  [on_device(): got = lax.all_to_all(sent, ALL, split_axis=0, concat_axis=0, tiled=True)]
    unnamed x28 -> x6, local copies, waits for them, and re-layouts: 6.24 us -> 0.02 us
    reshape x1 -> x0, local copies, waits for them, and re-layouts: 0.74 us -> none  [on_device(): clip.reshape(NV // VIS_BLOCK, 1)]
  transfers between devices with their start and end apart: 1 -> 0, of which waited for: 1 -> 0; matrix products, arithmetic and copies ran while one was open for 0% -> 0% of each run, Pallas kernels for 0% -> 0%
where the time goes in v2:
time: 54.5 us; the launch traced here: 54.4 us
  blocking collectives  44.2 us (81%)
  Pallas kernels  9.42 us (17%)
  between operations  0.68 us (1%)
    all_to_all x2, blocking collectives, exchange(): lax.all_to_all(pairs, ALL, split_axis=0, concat_axis=0, tiled=True)  44.2 us
    pallas_call x1, Pallas kernels, on_device(): pl.pallas_call(send_kernel, out_shape=(message, jax.ShapeDtypeStruct((8,...  3.24 us
    pallas_call x1, Pallas kernels, on_device(): pl.pallas_call(facet_kernel, out_shape=(jax.ShapeDtypeStruct((1, 2, RD, N...  3.16 us
    pallas_call x1, Pallas kernels, on_device(): pl.pallas_call(owner_kernel, out_shape=message, in_specs=[VMEM, HBM, HBM]...  3.02 us

profile of v2, /device:TPU:1, one launch (start us, length us, event | category | flops | bytes accessed | tf_op | source)
XLA Modules:
  0.0 54.4 jit_solution(4075225329264663941)
XLA Ops:
  0.6 3.2 %send.1 = (bf16[2304,128]{1,0:T(8,128)(2,1)S(1)}, s32[8,1024]{1,0:T(8,128)S(1)}) custom-call(s32[1,2]{1,0:T(1,128)} %off_hbm.1, bf16[1,2,16,8192]{3,2,1,0:T(8,128)(2,1)} %slab_hbm.1, f32[2,1024]{1,0:T(2,128)} %pos_hbm.1, f32[2,1024]{1,0:T(2,128)} %obs_hbm.1, s32[1,1024]{1,0:T(1,128)} %bitcast.10, s32[1,32]{1,0:T(1,128)} %bitcast.11, ...), custom_call_target="tpu_custom_call" | custom-call | tf_op jit(solution)/shard_map/send/pallas_call | solution.py:415
  3.9 25.5 %all_to_all.10 = bf16[1152,2,128]{2,1,0:T(2,128)(2,1)S(1)} all-to-all(bf16[1152,2,128]{2,1,0:T(2,128)(2,1)S(1)} %bitcast.9), channel_id=1, replica_groups=mesh['facet'=4,'sub'=32] {'facet','sub'}, dimensions={0} | all-to-all | bytes 1179648 | tf_op jit(solution)/shard_map/all_to_all | solution.py:403
  29.4 3.0 %owner.1 = bf16[2304,128]{1,0:T(8,128)(2,1)S(1)} custom-call(bf16[2304,128]{1,0:T(8,128)(2,1)S(1)} %bitcast.6, bf16[4,256,512]{2,1,0:T(8,128)(2,1)} %constant.19.clone.fwd_hbm, bf16[4,512,256]{2,1,0:T(8,128)(2,1)} %constant.20.clone.adj_hbm), custom_call_target="tpu_custom_call" | custom-call | tf_op jit(solution)/shard_map/owner/pallas_call | solution.py:431
  32.4 0.0 copy-start
  32.4 0.0 copy-start.1
  32.4 0.0 copy-start.2
  32.4 18.8 %all_to_all.11 = bf16[1152,2,128]{2,1,0:T(2,128)(2,1)S(1)} all-to-all(bf16[1152,2,128]{2,1,0:T(2,128)(2,1)S(1)} %bitcast.7), channel_id=1, replica_groups=mesh['facet'=4,'sub'=32] {'facet','sub'}, dimensions={0} | all-to-all | bytes 1179648 | tf_op jit(solution)/shard_map/all_to_all | solution.py:403
  51.2 0.0 copy-done
  51.2 0.0 copy-done.1
  51.2 0.0 copy-done.2
  51.2 3.2 %facet.1 = (f32[1,2,16,8192]{3,2,1,0:T(8,128)}, f32[2,1024]{1,0:T(2,128)}) custom-call(bf16[2304,128]{1,0:T(8,128)(2,1)S(1)} %bitcast.8, s32[8,1024]{1,0:T(8,128)S(1)} %get-tuple-element.5.meta_ref, bf16[256,32]{1,0:T(8,128)(2,1)S(1)} %copy-done.1, f32[2,128,128]{2,1,0:T(8,128)S(1)} %copy-done, bf16[128,128]{1,0:T(8,128)(2,1)S(1)} %copy-done.2), custom_call_target="tpu_custom_call" | custom-call | tf_op jit(solution)/shard_map/facet/pallas_call | solution.py:450
Async XLA Ops:
  32.4 18.8 %copy-start = (f32[2,128,128]{2,1,0:T(8,128)S(1)}, f32[2,128,128]{2,1,0:T(8,128)}, u32[]{:S(2)}) copy-start(f32[2,128,128]{2,1,0:T(8,128)} %constant.17.clone.tw_ref) | copy-start | bytes 393220
  32.4 18.8 %copy-start.1 = (bf16[256,32]{1,0:T(8,128)(2,1)S(1)}, bf16[256,32]{1,0:T(8,128)(2,1)}, u32[]{:S(2)}) copy-start(bf16[256,32]{1,0:T(8,128)(2,1)} %constant.18.clone.coarse_ref) | copy-start | bytes 49156
  32.4 18.8 %copy-start.2 = (bf16[128,128]{1,0:T(8,128)(2,1)S(1)}, bf16[128,128]{1,0:T(8,128)(2,1)}, u32[]{:S(2)}) copy-start(bf16[128,128]{1,0:T(8,128)(2,1)} %constant.15.clone.col_ref) | copy-start | bytes 98308

commit v3 on v2

v3 whole, which is shorter than its diff:
```python
import math

import jax
import jax.numpy as jnp
import numpy as np
from jax import lax
from jax.experimental import pallas as pl
from jax.experimental.pallas import tpu as pltpu
from jax.sharding import PartitionSpec as P

N_IMG = 32768
SUBG = 64
HALF = 32
VIS_BLOCK = 32
LANES = 128
NQ = 32
NF = 4
NDEV = 128
RD = 16
NR2 = 8
NA = 64
NV = 1024
SLOT = 16
MSG = 10
A_HIGH = 3 * 5 * SLOT
TWO_PI = 2.0 * math.pi
BF = jnp.bfloat16
F32 = jnp.float32
ALL = ("facet", "sub")


def unit(index, period):
    angle = TWO_PI * (np.asarray(index, np.int64) % period) / period
    return np.cos(angle), np.sin(angle)


def host_tables():
    block = np.arange(NA)
    lane = np.arange(LANES)
    fine = np.arange(SUBG)
    coarse = np.arange(NQ)
    c, s = unit(fine[:, None] * block[None, :], 256)
    c, s = c / 64.0, s / 64.0
    col_fwd = np.block([[c, s], [-s, c]])
    col_adj = np.block([[c.T, -s.T], [s.T, c.T]])
    tw_c, tw_s = unit(fine[:, None] * lane[None, :], N_IMG)
    twiddle_fwd = np.concatenate([tw_c, -tw_s], 0)
    twiddle_adj = np.stack([np.tile(tw_c.T, (1, 2)), np.tile(tw_s.T, (1, 2))])
    wc, ws = unit(coarse[:, None] * lane[None, :], 32)
    column = np.concatenate([col_fwd, wc, ws, -ws, wc], 0)
    coarse_adj = np.concatenate([wc.T, ws.T], 0)
    k_row = (np.arange(8)[:, None] * 4096 + fine[None, :]).reshape(2, 4 * SUBG)
    r = np.arange(NQ * RD).reshape(NQ, 2, NR2).transpose(1, 2, 0).reshape(-1)
    rc, rs = unit(k_row[:, :, None] * r[None, None, :], N_IMG)
    row_fwd = np.concatenate([rc, -rs], 1) / 64.0
    row_adj = np.ascontiguousarray(row_fwd.transpose(0, 2, 1))
    bf = lambda x: np.asarray(x, np.float32).astype(jnp.bfloat16)
    return dict(
        column=bf(column),
        col_adj=bf(col_adj),
        tw_fwd=np.asarray(twiddle_fwd, np.float32),
        tw_adj=np.asarray(twiddle_adj, np.float32),
        coarse_adj=bf(coarse_adj),
        row_fwd=bf(row_fwd),
        row_adj=bf(row_adj),
    )


def sincos_turn(turn):
    quarter = jnp.floor(turn * 4.0 + 0.5)
    y = (turn - quarter * 0.25) * TWO_PI
    y2 = y * y
    s = y * (1.0 + y2 * (-1.0 / 6 + y2 * (1.0 / 120 + y2 * (-1.0 / 5040 + y2 * (1.0 / 362880)))))
    c = 1.0 + y2 * (-0.5 + y2 * (1.0 / 24 + y2 * (-1.0 / 720 + y2 * (1.0 / 40320))))
    turns = quarter.astype(jnp.int32)
    odd = (turns & 1) == 1
    cos = jnp.where(odd, s, c)
    sin = jnp.where(odd, c, s)
    cos = jnp.where(((turns + 1) & 2) == 2, -cos, cos)
    sin = jnp.where((turns & 2) == 2, -sin, sin)
    return cos, sin


def phase_of(offset, frequency):
    index = (offset * frequency) & (N_IMG - 1)
    return sincos_turn(index.astype(F32) * (1.0 / N_IMG))


def iota(shape, dim):
    return lax.broadcasted_iota(jnp.int32, shape, dim)


def roll(x, shift):
    return pltpu.roll(x, shift, x.ndim - 1)


def lane_sign(rows, width):
    return jnp.where((iota((rows, LANES), 1) & width) == 0, 1.0, -1.0).astype(F32)


def lower(shape):
    return iota(shape, len(shape) - 1) < SUBG


def split3(x):
    high = x.astype(BF)
    rest = x - high.astype(F32)
    middle = rest.astype(BF)
    low = (rest - middle.astype(F32)).astype(BF)
    return high, middle, low


def send_kernel(
    off_hbm, slab_hbm, pos_hbm, obs_hbm, ids_hbm, clip_hbm, table_hbm, tw_hbm, fwd_hbm, adj_hbm,
    msg_ref, meta_ref, fwd_ref, adj_ref, off_ref, slab_ref, pos_ref, obs_ref, ids_ref, clip_ref, table_ref, tw_ref,
    wide, flat, sems,
):
    pairs = [
        (ids_hbm, ids_ref), (clip_hbm, clip_ref), (pos_hbm, pos_ref), (obs_hbm, obs_ref),
        (off_hbm, off_ref), (slab_hbm, slab_ref), (table_hbm, table_ref), (tw_hbm, tw_ref),
    ]
    copies = [pltpu.make_async_copy(a, b, sems.at[i]) for i, (a, b) in enumerate(pairs)]
    four = lax.axis_index("facet") // 2
    later = [
        pltpu.make_async_copy(fwd_hbm.at[four], fwd_ref, sems.at[len(pairs)]),
        pltpu.make_async_copy(adj_hbm.at[four], adj_ref, sems.at[len(pairs) + 1]),
    ]
    for copy in copies + later:
        copy.start()

    copies[0].wait()
    ids = ids_ref[...]
    upper = jnp.where(iota((LANES, LANES), 0) < iota((LANES, LANES), 1), 1.0, 0.0).astype(BF)
    counter = jnp.concatenate([upper, jnp.ones((LANES, LANES), BF)], 1)
    before = jnp.zeros((2 * LANES, LANES), F32)
    ranks = []
    for b in range(NV // LANES):
        hot = iota((2 * LANES, LANES), 0) == ids[:, b * LANES:(b + 1) * LANES]
        hot_f = jnp.where(hot, 1.0, 0.0)
        count = jnp.dot(hot_f.astype(BF), counter, preferred_element_type=F32)
        ranks.append(jnp.sum(hot_f * (count[:, :LANES] + before), 0, keepdims=True))
        before = before + count[:, LANES:]
    rank = jnp.concatenate(ranks, 1).astype(jnp.int32)
    owner = (ids >> 7) * (2 * NQ) + (ids & (NQ - 1)) * 2 + ((ids >> 6) & 1)
    place = ((ids >> 5) & 1) * 8 + rank
    meta_ref[0:1, :] = owner
    meta_ref[1:2, :] = place
    here = iota((SLOT, NV), 0) == place
    copies[1].wait()
    n_block = NV // VIS_BLOCK
    clip = jnp.broadcast_to(clip_ref[...].astype(F32) * 0.25, (n_block, n_block))
    same = iota((n_block, n_block), 0) == iota((n_block, n_block), 1)
    clip = jnp.sum(jnp.where(same, clip, 0.0), 1, keepdims=True)
    block = iota((n_block, NV), 1) // VIS_BLOCK == iota((n_block, NV), 0)
    level = jnp.sum(jnp.where(block, clip, 0.0), 0, keepdims=True)
    copies[2].wait()
    copies[3].wait()
    values = [pos_ref[0:1, :], pos_ref[1:2, :], obs_ref[0:1, :], obs_ref[1:2, :], level]
    pieces = [split3(v) for v in values]
    own = jnp.where(iota((NDEV, NV), 0) == owner, 1.0, 0.0).astype(BF)
    table = jnp.concatenate(
        [jnp.where(here, p[part].astype(F32), 0.0).astype(BF) for part in range(3) for p in pieces]
        + [jnp.zeros((SLOT, NV), BF)], 0
    )
    copies[4].wait()
    meta_ref[2:3, :] = jnp.full((1, NV), off_ref[0, 1], jnp.int32)
    payload = lax.dot_general(own, table, (((1,), (1,)), ((), ())), preferred_element_type=F32)
    lane = iota((NDEV, LANES), 1)
    tail = payload[:, LANES:]
    tail = jnp.where(lane == A_HIGH - LANES, (off_ref[0, 0] >> 8).astype(F32), tail)
    tail = jnp.where(lane == A_HIGH + 1 - LANES, (off_ref[0, 0] & 255).astype(F32), tail)
    flat[pl.ds(NR2, NDEV, stride=MSG), :] = payload[:, :LANES]
    flat[pl.ds(NR2 + 1, NDEV, stride=MSG), :] = tail

    lane1 = iota((NQ, LANES), 1)
    phases = []
    for c in range(2):
        freq = iota((NQ, LANES), 0) * (N_IMG // NQ) + (lane1 & (HALF - 1)) + c * HALF
        phases.append(phase_of(off_ref[0, 1], freq))
    for copy in copies[5:]:
        copy.wait()
    for part in range(2):
        for a in range(NA):
            wide[part, a * RD:(a + 1) * RD, :] = slab_ref[
                0, part, :, a * LANES:(a + 1) * LANES
            ].astype(F32)
    tw_c, tw_s = tw_ref[:SUBG], tw_ref[SUBG:]
    col = table_ref[:LANES]
    coarse = jnp.concatenate(
        [
            jnp.concatenate([table_ref[LANES:LANES + NQ], table_ref[LANES + 2 * NQ:LANES + 3 * NQ]], 1),
            jnp.concatenate([table_ref[LANES + NQ:LANES + 2 * NQ], table_ref[LANES + 3 * NQ:]], 1),
        ], 0
    )
    for base in range(0, NR2, 2):
        which = [base, base + NR2, base + 1, base + 1 + NR2]
        cols = [
            jnp.concatenate(
                [wide[0, pl.ds(r, NA, stride=RD), :], wide[1, pl.ds(r, NA, stride=RD), :]], 0
            ).astype(BF)
            for r in which
        ]
        y = jnp.dot(col, jnp.concatenate(cols, 1), preferred_element_type=F32)
        real, imag = [], []
        for i in range(4):
            yr = y[:SUBG, i * LANES:(i + 1) * LANES]
            yi = y[SUBG:, i * LANES:(i + 1) * LANES]
            zr = yr * tw_c - yi * tw_s
            zi = yr * tw_s + yi * tw_c
            real.append(jnp.concatenate([zr, -zi], 1).astype(BF))
            imag.append(jnp.concatenate([zi, zr], 1).astype(BF))
        stacked = []
        for pair in range(2):
            for c in range(2):
                for i in (2 * pair, 2 * pair + 1):
                    stacked.append(real[i][c * HALF:(c + 1) * HALF])
                    stacked.append(imag[i][c * HALF:(c + 1) * HALF])
        out = lax.dot_general(
            coarse, jnp.concatenate(stacked, 0), (((1,), (1,)), ((), ())),
            preferred_element_type=F32,
        )
        for pair in range(2):
            for c in range(2):
                at = (pair * 2 + c) * LANES
                piece = out[:NQ, at:at + LANES] * phases[c][0] - out[NQ:, at:at + LANES] * phases[c][1]
                for g in range(2):
                    row = (2 * NQ * g + c) * MSG + base + pair
                    flat[pl.ds(row, NQ, stride=2 * MSG), :] = piece
    msg_ref[...] = flat[...].astype(BF)
    for copy in later:
        copy.wait()


def rows_kernel(got_ref, fwd_ref, keep_ref, give_ref, vis_ref, rho_ref, flat, halves):
    flat[...] = got_ref[...].astype(F32)
    got = jnp.concatenate(
        [flat[pl.ds(NR2, NDEV, stride=MSG), :].T, flat[pl.ds(NR2 + 1, NDEV, stride=MSG), :].T], 0
    )
    n = 5 * SLOT
    vis_ref[...] = got[:n] + got[n:2 * n] + got[2 * n:3 * n]
    four = lax.axis_index("facet") // 2
    start = (got[A_HIGH:A_HIGH + 1] * 256.0 + got[A_HIGH + 1:A_HIGH + 2]).astype(jnp.int32)
    low = lower((1, LANES))
    starts = [
        jnp.where(low, start[:, 2 * t * NQ:2 * t * NQ + 1], start[:, (2 * t + 1) * NQ:(2 * t + 1) * NQ + 1])
        for t in range(2)
    ]
    eight = iota((8, LANES), 0)
    turn_c, turn_s = phase_of(
        jnp.where(eight < 4, starts[0], starts[1]), (four * 4 + (eight & 3)) * (N_IMG // 8)
    )
    for t in range(2):
        fine_c, fine_s = phase_of(starts[t], iota((SUBG, LANES), 0))
        for p in range(4):
            tc, ts = turn_c[t * 4 + p:t * 4 + p + 1], turn_s[t * 4 + p:t * 4 + p + 1]
            rho_ref[t, 0, p * SUBG:(p + 1) * SUBG, :] = fine_c * tc - fine_s * ts
            rho_ref[t, 1, p * SUBG:(p + 1) * SUBG, :] = fine_s * tc + fine_c * ts
    low = lower((NQ, LANES))
    first, second = [], []
    for row in range(NR2):
        x = [flat[pl.ds(f * NQ * MSG + row, NQ, stride=MSG), :] for f in range(NF)]
        y = [roll(v, SUBG) for v in x]
        first.append(jnp.concatenate([jnp.where(low, x[0], y[1]), jnp.where(low, x[2], y[3])], 1).astype(BF))
        second.append(jnp.concatenate([jnp.where(low, y[0], x[1]), jnp.where(low, y[2], x[3])], 1).astype(BF))
    both = jnp.dot(fwd_ref[...], jnp.concatenate(first + second, 0), preferred_element_type=F32)
    m = 4 * SUBG
    real, turned = 0.0, 0.0
    for t in range(2):
        rc, rs = rho_ref[t, 0], rho_ref[t, 1]
        a, b = both[:m, t * LANES:(t + 1) * LANES], both[m:, t * LANES:(t + 1) * LANES]
        real = real + (rc * a + rs * b)
        turned = turned + (rc * b - rs * a)
    real = real + roll(real, SUBG)
    turned = turned + roll(turned, SUBG)
    halves[...] = real - roll(turned, HALF) * lane_sign(m, HALF)
    core = lax.axis_index("sub") & 1
    keep_ref[...] = halves[pl.ds(core * LANES, LANES), :].astype(BF)
    give_ref[...] = halves[pl.ds((1 - core) * LANES, LANES), :].astype(BF)


def times(a, b):
    return a[0] * b[0] - a[1] * b[1], a[0] * b[1] + a[1] * b[0]


def tables_kernel(vis_ref, left, basis, small):
    slot = 0
    for l in range(2):
        for which in range(2):
            turn = vis_ref[which * SLOT + l * 8:which * SLOT + l * 8 + 8, :] * (1.0 / SUBG)
            p1 = sincos_turn(turn)
            ones = jnp.ones_like(turn)

            def ladder(p, unit):
                p2 = times(p, p)
                p3 = times(p2, p)
                p4 = times(p2, p2)
                return [unit, p, p2, p3, p4, times(p4, p), times(p3, p3), times(p4, p3)], p4

            low, p4 = ladder(p1, (ones, jnp.zeros_like(turn)))
            high, _ = ladder(times(p4, p4), (ones, jnp.zeros_like(turn)))
            for i in range(8):
                for part in range(2):
                    small[slot, part, i * 8:i * 8 + 8, :] = low[i][part]
                    small[slot, 2 + part, i * 8:i * 8 + 8, :] = high[i][part] * 0.125
            for k in range(8):
                at = slice(k * LANES, (k + 1) * LANES)
                br, bi, ar, ai = [small[slot, part, pl.ds(k, 8, stride=8), :] for part in range(4)]
                re, im = [], []
                for a in range(8):
                    hr, hi = ar[a:a + 1, :], ai[a:a + 1, :]
                    re.append(hr * br - hi * bi)
                    im.append(hr * bi + hi * br)
                if which == 0:
                    left[l, 0:SUBG, at] = jnp.concatenate(re, 0)
                    left[l, SUBG:, at] = jnp.concatenate(im, 0)
                else:
                    for h in range(2):
                        base = h * SUBG
                        basis[l, base:base + HALF, at] = jnp.concatenate(re[h * 4:h * 4 + 4], 0).astype(BF)
                        basis[l, base + HALF:base + SUBG, at] = jnp.concatenate(im[h * 4:h * 4 + 4], 0).astype(BF)
            slot += 1


def swap_half(x):
    return jnp.where((iota(x.shape, 1) & HALF) == 0, roll(x, LANES - HALF), roll(x, HALF))


def visibility_kernel(keep_ref, other_ref, vis_ref, left, basis, corrected_ref, back_ref, inner, phasor):
    upper_core = (lax.axis_index("sub") & 1) == 1
    keep, other = keep_ref[...].astype(F32), other_ref[...].astype(F32)
    halves = jnp.where(upper_core, other, keep), jnp.where(upper_core, keep, other)
    subgrids = jnp.where(lower((LANES, LANES)), halves[0], halves[1])
    sign = lane_sign(SUBG, HALF)
    sums = []
    returned = [[None, None], [None, None]]
    for l in range(2):
        obs_r, obs_i, level = [vis_ref[c * SLOT + l * 8:c * SLOT + l * 8 + 8, :] for c in range(2, 5)]
        sub = subgrids[l * SUBG:(l + 1) * SUBG]
        matrix = jnp.concatenate([sub * sign, swap_half(sub)], 0).astype(BF)
        inner[l] = jnp.dot(matrix, basis[l], preferred_element_type=F32)
        pred_r, pred_i = [], []
        for k in range(8):
            at = slice(k * LANES, (k + 1) * LANES)
            lr, li = left[l, 0:SUBG, at], left[l, SUBG:, at]
            ir, ii = inner[l, 0:SUBG, at], inner[l, SUBG:, at]
            pred_r.append(jnp.sum(lr * ir - li * ii, 0, keepdims=True))
            pred_i.append(jnp.sum(lr * ii + li * ir, 0, keepdims=True))
        mis_r = obs_r - jnp.concatenate(pred_r, 0)
        mis_i = obs_i - jnp.concatenate(pred_i, 0)
        live = level > 0.0
        threshold = jnp.where(live, level, 1.0)
        magnitude = jnp.sqrt(mis_r * mis_r + mis_i * mis_i)
        weight = jnp.where(live, threshold / jnp.maximum(magnitude, threshold), 0.0)
        wr, wi = weight * mis_r, weight * mis_i
        returned[0][l], returned[1][l] = wr, wi
        for k in range(8):
            at = slice(k * LANES, (k + 1) * LANES)
            lr, li = left[l, 0:SUBG, at], left[l, SUBG:, at]
            vr, vi = wr[k:k + 1, :], wi[k:k + 1, :]
            phasor[l, 0:SUBG, at] = (lr * vr + li * vi).astype(BF)
            phasor[l, SUBG:, at] = (lr * vi - li * vr).astype(BF)
        product = lax.dot_general(
            phasor[l], basis[l], (((1,), (1,)), ((), ())), preferred_element_type=F32
        )
        sums.append(product[:SUBG] * sign + swap_half(product[SUBG:]))
    corrected_ref[...] = jnp.concatenate(sums, 0).astype(BF)
    back = jnp.concatenate([returned[0][0], returned[0][1], returned[1][0], returned[1][1]], 0)
    back = [part.astype(F32) for part in split3(back)]
    back_ref[...] = jnp.concatenate(back + [jnp.zeros((2 * SLOT, LANES), F32)], 0)


def images_kernel(mine_ref, other_ref, back_ref, rho_ref, adj_ref, msg_ref, flat):
    upper_core = (lax.axis_index("sub") & 1) == 1
    mine, other = mine_ref[...].astype(F32), other_ref[...].astype(F32)
    low = lower((LANES, LANES))
    rows = []
    for x in (jnp.where(upper_core, other, mine), jnp.where(upper_core, mine, other)):
        y = roll(x, SUBG)
        rows.append(jnp.where(low != upper_core, x, y))
    corrected = jnp.concatenate(rows, 0)
    turned = roll(corrected, HALF) * -lane_sign(4 * SUBG, HALF)
    cols = []
    for t in range(2):
        rc, rs = rho_ref[t, 0], rho_ref[t, 1]
        cols.append(
            jnp.concatenate(
                [(corrected * rc + turned * rs).astype(BF), (corrected * rs - turned * rc).astype(BF)], 0
            )
        )
    images = jnp.dot(adj_ref[...], jnp.concatenate(cols, 1), preferred_element_type=F32)
    low = lower((NQ, LANES))
    for row in range(NR2):
        for t in range(2):
            at = slice(t * LANES, (t + 1) * LANES)
            a = images[row * NQ:(row + 1) * NQ, at]
            b = images[(NR2 + row) * NQ:(NR2 + row + 1) * NQ, at]
            flat[pl.ds(2 * t * NQ * MSG + row, NQ, stride=MSG), :] = jnp.where(low, a, roll(b, SUBG))
            flat[pl.ds((2 * t + 1) * NQ * MSG + row, NQ, stride=MSG), :] = jnp.where(low, roll(a, SUBG), b)
    flat[pl.ds(NR2, NDEV, stride=MSG), :] = back_ref[...].T
    flat[pl.ds(NR2 + 1, NDEV, stride=MSG), :] = jnp.zeros((NDEV, LANES), F32)
    msg_ref[...] = flat[...].astype(BF)


def facet_kernel(
    got_ref, meta_ref, coarse_ref, tw_ref, col_ref, out_hbm, res_hbm, flat, turned, out_ref, res_ref, sems,
):
    flat[...] = got_ref[...].astype(F32)
    n = 2 * SLOT
    back = flat[pl.ds(NR2, NDEV, stride=MSG), :].T[:3 * n]
    owner, place = meta_ref[0:1, :], meta_ref[1:2, :]
    own = jnp.where(iota((NDEV, NV), 0) == owner, 1.0, 0.0).astype(BF)
    found = jnp.dot(back.astype(BF), own, preferred_element_type=F32)
    found = found[:n] + found[n:2 * n] + found[2 * n:]
    here = iota((SLOT, NV), 0) == place
    for c in range(2):
        res_ref[c:c + 1, :] = jnp.sum(
            jnp.where(here, found[c * SLOT:(c + 1) * SLOT], 0.0), 0, keepdims=True
        )
    copies = [pltpu.make_async_copy(res_ref, res_hbm, sems.at[4])]
    copies[0].start()

    freq = iota((NQ, LANES), 0) * (N_IMG // NQ) + (iota((NQ, LANES), 1) & (SUBG - 1))
    ph_c, ph_s = phase_of(meta_ref[2:3, :LANES], freq)
    ph_s = -ph_s * lane_sign(NQ, SUBG)
    tw_c, tw_s = tw_ref[0], tw_ref[1]
    sign = lane_sign(LANES, SUBG)
    quarter = iota((NQ, LANES), 1) // HALF
    images = [None] * RD
    for row in range(NR2):
        x = []
        for c in range(2):
            image = flat[pl.ds(c * MSG + row, NQ, stride=2 * MSG), :]
            x.append(image + flat[pl.ds((2 * NQ + c) * MSG + row, NQ, stride=2 * MSG), :])
        r32, r64, r96 = [[roll(v, k * HALF) for v in x] for k in (1, 2, 3)]
        choose = lambda *v: jnp.where(
            quarter < 2, jnp.where(quarter == 0, v[0], v[1]), jnp.where(quarter == 2, v[2], v[3])
        )
        for h, image in enumerate(
            (choose(x[0], r32[1], r32[0], r64[1]), choose(r64[0], r96[1], r96[0], x[1]))
        ):
            images[row + h * NR2] = (image * ph_c + roll(image, SUBG) * ph_s).astype(BF)
    group = 4
    for base in range(0, RD, group):
        spread = jnp.dot(
            coarse_ref[...], jnp.concatenate(images[base:base + group], 1), preferred_element_type=F32
        )
        stacked = []
        for i in range(group):
            first = spread[:LANES, i * LANES:(i + 1) * LANES]
            second = spread[LANES:, i * LANES:(i + 1) * LANES]
            z = (tw_c * first - tw_s * second) - roll(tw_s * first + tw_c * second, SUBG) * sign
            stacked.append(z.astype(BF))
        out = lax.dot_general(
            col_ref[...], jnp.concatenate(stacked, 0), (((1,), (1,)), ((), ())),
            preferred_element_type=F32,
        )
        for i in range(group):
            r = base + i
            for part in range(2):
                at = (part * 2 + r // 8) * NA * 8 + r % 8
                turned[pl.ds(at, NA, stride=8), :] = out[
                    part * NA:(part + 1) * NA, i * LANES:(i + 1) * LANES
                ]
        if (base + group) % 8 == 0:
            half = base // 8
            for part in range(2):
                where = slice(half * 8, half * 8 + 8)
                for a in range(NA):
                    at = ((part * 2 + half) * NA + a) * 8
                    out_ref[part, where, a * LANES:(a + 1) * LANES] = turned[at:at + 8, :]
                copy = pltpu.make_async_copy(
                    out_ref.at[part, where, :], out_hbm.at[0, part, where, :],
                    sems.at[half * 2 + part],
                )
                copy.start()
                copies.append(copy)
    for copy in copies:
        copy.wait()


VMEM = pl.BlockSpec(memory_space=pltpu.VMEM)
HBM = pl.BlockSpec(memory_space=pltpu.MemorySpace.HBM)
TABLES = host_tables()


def in_place(arrays):
    return [pltpu.with_memory_space_constraint(x, pltpu.HBM) for x in arrays]


def exchange(message):
    pairs = message.reshape(NDEV * MSG // 2, 2, LANES)
    return lax.all_to_all(pairs, ALL, split_axis=0, concat_axis=0, tiled=True).reshape(message.shape)


def other_core(x):
    return lax.ppermute(x, "sub", [(i, i ^ 1) for i in range(NQ)])


def on_device(slab, offsets, position, observed, subgrid_of, clip):
    t = {name: jnp.asarray(value) for name, value in TABLES.items()}
    limit = pltpu.CompilerParams(vmem_limit_bytes=32 << 20)
    shape = jax.ShapeDtypeStruct
    message = shape((NDEV * MSG, LANES), BF)
    table = shape((8 * SUBG, NQ * RD), BF)
    square = shape((LANES, LANES), BF)
    flat = pltpu.VMEM((NDEV * MSG, LANES), F32)

    def call(kernel, name, inputs, outs, scratch, in_specs=None, out_specs=None, flops=1 << 20):
        return pl.pallas_call(
            kernel,
            out_shape=outs,
            in_specs=in_specs or [VMEM] * len(inputs),
            out_specs=out_specs or (VMEM,) * len(outs),
            scratch_shapes=scratch,
            compiler_params=limit,
            cost_estimate=pl.CostEstimate(flops=flops, bytes_accessed=1 << 21, transcendentals=0),
            name=name,
        )(*inputs)

    inputs = (
        offsets, slab, position, observed, subgrid_of.reshape(1, NV),
        clip.reshape(1, NV // VIS_BLOCK), t["column"], t["tw_fwd"],
    )
    sent, meta, fwd, adj = call(
        send_kernel, "send", in_place(inputs + (t["row_fwd"], t["row_adj"])),
        (message, shape((8, NV), jnp.int32), table, table),
        [pltpu.SMEM((1, 2), jnp.int32)]
        + [pltpu.VMEM(x.shape, x.dtype) for x in inputs[1:]]
        + [
            pltpu.VMEM((2, NA * RD, LANES), F32),
            flat,
            pltpu.SemaphoreType.DMA((len(inputs) + 2,)),
        ],
        in_specs=[HBM] * (len(inputs) + 2),
    )
    got = exchange(sent)
    keep, give, vis, rho = call(
        rows_kernel, "rows", (got, fwd),
        (square, square, shape((5 * SLOT, LANES), F32), shape((2, 2, 4 * SUBG, LANES), F32)),
        [flat, pltpu.VMEM((4 * SUBG, LANES), F32)],
    )
    other = other_core(give)
    left, basis = call(
        tables_kernel, "tables", (vis,),
        (shape((2, 2 * SUBG, NV), F32), shape((2, 2 * SUBG, NV), BF)),
        [pltpu.VMEM((4, 4, SUBG, LANES), F32)],
    )
    corrected, back = call(
        visibility_kernel, "visibilities", (keep, other, vis, left, basis),
        (square, shape((LANES, LANES), F32)),
        [pltpu.VMEM((2, 2 * SUBG, NV), F32), pltpu.VMEM((2, 2 * SUBG, NV), BF)],
    )
    (answer,) = call(
        images_kernel, "images", (corrected, other_core(corrected), back, rho, adj), (message,), [flat]
    )
    facet_adjoint, residual = call(
        facet_kernel, "facet",
        (exchange(answer), meta, t["coarse_adj"], t["tw_adj"], t["col_adj"]),
        (shape((1, 2, RD, NA * LANES), F32), shape((2, NV), F32)),
        [
            flat,
            pltpu.VMEM((4 * NA * 8, LANES), F32),
            pltpu.VMEM((2, RD, NA * LANES), F32),
            pltpu.VMEM((2, NV), F32),
            pltpu.SemaphoreType.DMA((5,)),
        ],
        out_specs=(HBM, HBM),
    )
    return (facet_adjoint, residual)


def solution(mesh):
    placed = (
        P("facet", None, "sub", None),
        P("facet", None),
        P(None, ALL),
        P(None, ALL),
        P(ALL, None),
        P(ALL),
    )
    return jax.shard_map(
        on_device,
        mesh=mesh,
        in_specs=placed,
        out_specs=(P("facet", None, "sub", None), P(None, ALL)),
        check_vma=False,
    )
```

time: 54.5 us -> 50.5 us (0.927)
  blocking collectives: 44.2 us -> 37.9 us
  starting transfers between devices: 0 us -> 1.62 us
  waiting for transfers between devices: 0 us -> 1.22 us
  Pallas kernels: 9.42 us -> 8.81 us
    all_to_all x2, blocking collectives: 44.2 us -> 37.9 us  [exchange(): lax.all_to_all(pairs, ALL, split_axis=0, concat_axis=0, tiled=True)]
    ppermute x0 -> x2, starting transfers between devices: none -> 1.62 us  [other_core(): return lax.ppermute(x, 'sub', [(i, i ^ 1) for i in range(NQ)])]
    ppermute x0 -> x2, waiting for transfers between devices: none -> 1.22 us  [other_core(): return lax.ppermute(x, 'sub', [(i, i ^ 1) for i in range(NQ)])]
    pallas_call x3 -> x6, Pallas kernels: 9.42 us -> 8.81 us  [call(): pl.pallas_call(kernel, out_shape=outs, in_specs=in_specs or [VMEM] * len(...]
  transfers between devices with their start and end apart: 0 -> 2, of which waited for: 0 -> 2; matrix products, arithmetic and copies ran while one was open for 0% -> 0% of each run, Pallas kernels for 0% -> 1%
where the time goes in v3:
time: 50.5 us; the launch traced here: 50.3 us
  blocking collectives  37.9 us (75%)
  Pallas kernels  8.81 us (17%)
  starting transfers between devices  1.62 us (3%)
  waiting for transfers between devices  1.22 us (2%)
  between operations  0.69 us (1%)
    all_to_all x2, blocking collectives, exchange(): lax.all_to_all(pairs, ALL, split_axis=0, concat_axis=0, tiled=True)  37.9 us
    pallas_call x6, Pallas kernels, call(): pl.pallas_call(kernel, out_shape=outs, in_specs=in_specs or [VMEM] * len(...  8.81 us
    ppermute x2, starting transfers between devices, other_core(): return lax.ppermute(x, 'sub', [(i, i ^ 1) for i in range(NQ)])  1.62 us
    ppermute x2, waiting for transfers between devices, other_core(): return lax.ppermute(x, 'sub', [(i, i ^ 1) for i in range(NQ)])  1.22 us
  transfers between devices with their start and end apart: 2, of which 2 were waited for; matrix products, arithmetic and copies ran while one was open for 0% of the time, Pallas kernels for 1%

profile of v3, /device:TPU:1, one launch (start us, length us, event | category | flops | bytes accessed | tf_op | source)
XLA Modules:
  0.0 50.3 jit_solution(14739895818205837624)
XLA Ops:
  0.6 3.2 %send.1 = (bf16[1280,128]{1,0:T(8,128)(2,1)S(1)}, s32[8,1024]{1,0:T(8,128)S(1)}, bf16[512,512]{1,0:T(8,128)(2,1)S(1)}, bf16[512,512]{1,0:T(8,128)(2,1)S(1)}) custom-call(s32[1,2]{1,0:T(1,128)} %off_hbm.1, bf16[1,2,16,8192]{3,2,1,0:T(8,128)(2,1)} %slab_hbm.1, f32[2,1024]{1,0:T(2,128)} %pos_hbm.1, f32[2,1024]{1,0:T(2,128)} %obs_hbm.1, s32[1,1024]{1,0:T(1,128)} %bitcast.10, ...), custom_call_target="tpu_custom_call" | custom-call | flops 1048576 | bytes 2097152 | tf_op jit(solution)/shard_map/send/pallas_call | solution.py:509
  3.8 22.7 %all_to_all.10 = bf16[640,2,128]{2,1,0:T(2,128)(2,1)S(1)} all-to-all(bf16[640,2,128]{2,1,0:T(2,128)(2,1)S(1)} %bitcast.9), channel_id=1, replica_groups=mesh['facet'=4,'sub'=32] {'facet','sub'}, dimensions={0} | all-to-all | bytes 655360 | tf_op jit(solution)/shard_map/all_to_all | solution.py:492
  26.5 0.8 %rows.1 = (bf16[128,128]{1,0:T(8,128)(2,1)S(1)}, bf16[128,128]{1,0:T(8,128)(2,1)S(1)}, f32[80,128]{1,0:T(8,128)S(1)}, f32[2,2,256,128]{3,2,1,0:T(8,128)S(1)}) custom-call(bf16[1280,128]{1,0:T(8,128)(2,1)S(1)} %bitcast.7, bf16[512,512]{1,0:T(8,128)(2,1)S(1)} %get-tuple-element.15.fwd_ref), custom_call_target="tpu_custom_call" | custom-call | flops 1048576 | bytes 2097152 | tf_op jit(solution)/shard_map/rows/pallas_call | solution.py:509
  27.3 1.2 %collective-permute-start = (bf16[128,128]{1,0:T(8,128)(2,1)S(1)}, bf16[128,128]{1,0:T(8,128)(2,1)S(1)}, u32[]{:S(2)}, u32[]{:S(2)}) collective-permute-start(bf16[128,128]{1,0:T(8,128)(2,1)S(1)} %get-tuple-element.17), channel_id=1, source_target_pairs={{0,1},{1,0},{2,3},{3,2},{4,5},{5,4},{6,7},{7,6},{8,9},{9,8},{10,11... | collective-permute-start | bytes 98312 | tf_op jit(solution)/shard_map/ppermute | solution.py:496
  28.5 0.5 tables.1
  29.0 0.4 collective-permute-done.other_ref
  29.4 1.0 %visibilities.1 = (bf16[128,128]{1,0:T(8,128)(2,1)S(1)}, f32[128,128]{1,0:T(8,128)S(1)}) custom-call(bf16[128,128]{1,0:T(8,128)(2,1)S(1)} %get-tuple-element.16.keep_ref, bf16[128,128]{1,0:T(8,128)(2,1)S(1)} %collective-permute-done.other_ref, f32[80,128]{1,0:T(8,128)S(1)} %get-tuple-element.18.vis_ref, f32[2,128,1024]{2,1,0:T(8,128)S(1)} %get-tuple-element.19.left, ...), custom_call_target="tpu_custom_call" | custom-call | flops 1048576 | bytes 2097152 | tf_op jit(solution)/shard_map/visibilities/pallas_call | solution.py:509
  30.4 0.4 collective-permute-start.1
  30.8 0.9 %collective-permute-done.1.other_ref = bf16[128,128]{1,0:T(8,128)(2,1)S(1)} collective-permute-done((bf16[128,128]{1,0:T(8,128)(2,1)S(1)}, bf16[128,128]{1,0:T(8,128)(2,1)S(1)}, u32[]{:S(2)}, u32[]{:S(2)}) %collective-permute-start.1) | collective-permute-done | bytes 32800 | tf_op jit(solution)/shard_map/ppermute | solution.py:496
  31.7 0.6 %images.1 = bf16[1280,128]{1,0:T(8,128)(2,1)S(1)} custom-call(bf16[128,128]{1,0:T(8,128)(2,1)S(1)} %get-tuple-element.21.mine_ref, bf16[128,128]{1,0:T(8,128)(2,1)S(1)} %collective-permute-done.1.other_ref, f32[128,128]{1,0:T(8,128)S(1)} %get-tuple-element.22.back_ref, f32[2,2,256,128]{3,2,1,0:T(8,128)S(1)} %get-tuple-element.23.rho_ref, ...), custom_call_target="tpu_custom_call" | custom-call | flops 1048576 | bytes 2097152 | tf_op jit(solution)/shard_map/images/pallas_call | solution.py:509
  32.3 0.0 copy-start
  32.3 0.0 copy-start.1
  32.3 0.0 copy-start.2
  32.3 15.2 %all_to_all.11 = bf16[640,2,128]{2,1,0:T(2,128)(2,1)S(1)} all-to-all(bf16[640,2,128]{2,1,0:T(2,128)(2,1)S(1)} %bitcast.8), channel_id=1, replica_groups=mesh['facet'=4,'sub'=32] {'facet','sub'}, dimensions={0} | all-to-all | bytes 655360 | tf_op jit(solution)/shard_map/all_to_all | solution.py:492
  47.6 0.0 copy-done
  47.6 0.0 copy-done.1
  47.6 0.0 copy-done.2
  47.6 2.7 %facet.1 = (f32[1,2,16,8192]{3,2,1,0:T(8,128)}, f32[2,1024]{1,0:T(2,128)}) custom-call(bf16[1280,128]{1,0:T(8,128)(2,1)S(1)} %bitcast.6, s32[8,1024]{1,0:T(8,128)S(1)} %get-tuple-element.25.meta_ref, bf16[256,32]{1,0:T(8,128)(2,1)S(1)} %copy-done.1, f32[2,128,128]{2,1,0:T(8,128)S(1)} %copy-done, bf16[128,128]{1,0:T(8,128)(2,1)S(1)} %copy-done.2), custom_call_target="tpu_custom_call" | custom-call | flops 1048576 | bytes 2097152 | tf_op jit(solution)/shard_map/facet/pallas_call | solution.py:509
Async XLA Ops:
  27.3 2.0 %collective-permute-start = (bf16[128,128]{1,0:T(8,128)(2,1)S(1)}, bf16[128,128]{1,0:T(8,128)(2,1)S(1)}, u32[]{:S(2)}, u32[]{:S(2)}) collective-permute-start(bf16[128,128]{1,0:T(8,128)(2,1)S(1)} %get-tuple-element.17), channel_id=1, source_target_pairs={{0,1},{1,0},{2,3},{3,2},{4,5},{5,4},{6,7},{7,6},{8,9},{9,8},{10,11... | collective-permute-start | bytes 98312 | tf_op jit(solution)/shard_map/ppermute | solution.py:496
  30.4 1.3 %collective-permute-start.1 = (bf16[128,128]{1,0:T(8,128)(2,1)S(1)}, bf16[128,128]{1,0:T(8,128)(2,1)S(1)}, u32[]{:S(2)}, u32[]{:S(2)}) collective-permute-start(bf16[128,128]{1,0:T(8,128)(2,1)S(1)} %get-tuple-element.21.mine_ref), channel_id=1, source_target_pairs={{0,1},{1,0},{2,3},{3,2},{4,5},{5,4},{6,7},{7,6},{8,9},{9,8},{10,11... | collective-permute-start | bytes 98312 | tf_op jit(solution)/shard_map/ppermute | solution.py:496
  32.3 15.3 %copy-start = (f32[2,128,128]{2,1,0:T(8,128)S(1)}, f32[2,128,128]{2,1,0:T(8,128)}, u32[]{:S(2)}) copy-start(f32[2,128,128]{2,1,0:T(8,128)} %constant.17.clone.tw_ref) | copy-start | bytes 393220
  32.3 15.3 %copy-start.1 = (bf16[256,32]{1,0:T(8,128)(2,1)S(1)}, bf16[256,32]{1,0:T(8,128)(2,1)}, u32[]{:S(2)}) copy-start(bf16[256,32]{1,0:T(8,128)(2,1)} %constant.18.clone.coarse_ref) | copy-start | bytes 49156
  32.3 15.3 %copy-start.2 = (bf16[128,128]{1,0:T(8,128)(2,1)S(1)}, bf16[128,128]{1,0:T(8,128)(2,1)}, u32[]{:S(2)}) copy-start(bf16[128,128]{1,0:T(8,128)(2,1)} %constant.15.clone.col_ref) | copy-start | bytes 98308

commit v4 on v3

--- a/solution.py
+++ b/solution.py
@@ -45,15 +45,18 @@
     col_adj = np.block([[c.T, -s.T], [s.T, c.T]])
     tw_c, tw_s = unit(fine[:, None] * lane[None, :], N_IMG)
     twiddle_fwd = np.concatenate([tw_c, -tw_s], 0)
-    twiddle_adj = np.stack([np.tile(tw_c.T, (1, 2)), np.tile(tw_s.T, (1, 2))])
+    orders = [fine, fine ^ HALF]
+    twiddle_adj = np.stack([np.tile(x.T[:, o], (1, 2)) for o in orders for x in (tw_c, tw_s)])
+    col_adj = np.concatenate([col_adj[:, np.concatenate([o, o + SUBG])] for o in orders], 0)
     wc, ws = unit(coarse[:, None] * lane[None, :], 32)
     column = np.concatenate([col_fwd, wc, ws, -ws, wc], 0)
-    coarse_adj = np.concatenate([wc.T, ws.T], 0)
+    coarse_adj = np.block([[wc.T, ws.T], [-ws.T, wc.T]])
     k_row = (np.arange(8)[:, None] * 4096 + fine[None, :]).reshape(2, 4 * SUBG)
     r = np.arange(NQ * RD).reshape(NQ, 2, NR2).transpose(1, 2, 0).reshape(-1)
     rc, rs = unit(k_row[:, :, None] * r[None, None, :], N_IMG)
-    row_fwd = np.concatenate([rc, -rs], 1) / 64.0
-    row_adj = np.ascontiguousarray(row_fwd.transpose(0, 2, 1))
+    pairs = lambda x: x.reshape(2, 2, 2 * SUBG, NQ * RD) / 64.0
+    row_fwd = np.concatenate([pairs(rc), -pairs(rs)], 2)
+    row_adj = np.ascontiguousarray(row_fwd.transpose(0, 1, 3, 2))
     bf = lambda x: np.asarray(x, np.float32).astype(jnp.bfloat16)
     return dict(
         column=bf(column),
@@ -173,10 +176,8 @@
     flat[pl.ds(NR2 + 1, NDEV, stride=MSG), :] = tail
 
     lane1 = iota((NQ, LANES), 1)
-    phases = []
-    for c in range(2):
-        freq = iota((NQ, LANES), 0) * (N_IMG // NQ) + (lane1 & (HALF - 1)) + c * HALF
-        phases.append(phase_of(off_ref[0, 1], freq))
+    freq = iota((NQ, LANES), 0) * (N_IMG // NQ) + (lane1 & (HALF - 1)) + lane1 // SUBG * HALF
+    ph_c, ph_s = phase_of(off_ref[0, 1], freq)
     for copy in copies[5:]:
         copy.wait()
     for part in range(2):
@@ -188,10 +189,11 @@
     col = table_ref[:LANES]
     coarse = jnp.concatenate(
         [
-            jnp.concatenate([table_ref[LANES:LANES + NQ], table_ref[LANES + 2 * NQ:LANES + 3 * NQ]], 1),
-            jnp.concatenate([table_ref[LANES + NQ:LANES + 2 * NQ], table_ref[LANES + 3 * NQ:]], 1),
+            jnp.concatenate([table_ref[LANES:LANES + NQ], table_ref[LANES + NQ:LANES + 2 * NQ]], 1),
+            jnp.concatenate([table_ref[LANES + 2 * NQ:LANES + 3 * NQ], table_ref[LANES + 3 * NQ:]], 1),
         ], 0
     )
+    low = lower((NQ, LANES))
     for base in range(0, NR2, 2):
         which = [base, base + NR2, base + 1, base + 1 + NR2]
         cols = [
@@ -201,50 +203,62 @@
             for r in which
         ]
         y = jnp.dot(col, jnp.concatenate(cols, 1), preferred_element_type=F32)
-        real, imag = [], []
+        both = []
         for i in range(4):
             yr = y[:SUBG, i * LANES:(i + 1) * LANES]
             yi = y[SUBG:, i * LANES:(i + 1) * LANES]
             zr = yr * tw_c - yi * tw_s
             zi = yr * tw_s + yi * tw_c
-            real.append(jnp.concatenate([zr, -zi], 1).astype(BF))
-            imag.append(jnp.concatenate([zi, zr], 1).astype(BF))
-        stacked = []
-        for pair in range(2):
-            for c in range(2):
-                for i in (2 * pair, 2 * pair + 1):
-                    stacked.append(real[i][c * HALF:(c + 1) * HALF])
-                    stacked.append(imag[i][c * HALF:(c + 1) * HALF])
+            both.append(jnp.concatenate([zr, zi], 1).astype(BF))
+        stacked = [
+            both[2 * pair + i][c * HALF:(c + 1) * HALF]
+            for pair in range(2) for c in range(2) for i in range(2)
+        ]
         out = lax.dot_general(
             coarse, jnp.concatenate(stacked, 0), (((1,), (1,)), ((), ())),
             preferred_element_type=F32,
         )
         for pair in range(2):
+            at = pair * LANES
+            x, y = out[:NQ, at:at + LANES], out[NQ:, at:at + LANES]
+            re, im = x * ph_c + y * ph_s, y * ph_c - x * ph_s
+            pieces = [jnp.where(low, re, roll(im, SUBG)), jnp.where(low, roll(re, SUBG), im)]
             for c in range(2):
-                at = (pair * 2 + c) * LANES
-                piece = out[:NQ, at:at + LANES] * phases[c][0] - out[NQ:, at:at + LANES] * phases[c][1]
                 for g in range(2):
                     row = (2 * NQ * g + c) * MSG + base + pair
-                    flat[pl.ds(row, NQ, stride=2 * MSG), :] = piece
+                    flat[pl.ds(row, NQ, stride=2 * MSG), :] = pieces[c]
     msg_ref[...] = flat[...].astype(BF)
     for copy in later:
         copy.wait()
 
 
-def rows_kernel(got_ref, fwd_ref, keep_ref, give_ref, vis_ref, rho_ref, flat, halves):
+def quarter_low(shape):
+    return (iota(shape, len(shape) - 1) & HALF) == 0
+
+
+def combine(both, rho):
+    real, turned = 0.0, 0.0
+    for t in range(2):
+        rc, rs = rho[t, 0], rho[t, 1]
+        a, b = both[:LANES, t * LANES:(t + 1) * LANES], both[LANES:, t * LANES:(t + 1) * LANES]
+        real = real + (rc * a + rs * b)
+        turned = turned + (rc * b - rs * a)
+    real = real + roll(real, HALF)
+    turned = turned + roll(turned, HALF)
+    return (real - roll(turned, SUBG) * lane_sign(LANES, SUBG)).astype(BF)
+
+
+def rows_kernel(got_ref, fwd_ref, give_ref, rhs_ref, rho_ref, raw_ref, flat):
     flat[...] = got_ref[...].astype(F32)
-    got = jnp.concatenate(
-        [flat[pl.ds(NR2, NDEV, stride=MSG), :].T, flat[pl.ds(NR2 + 1, NDEV, stride=MSG), :].T], 0
-    )
-    n = 5 * SLOT
-    vis_ref[...] = got[:n] + got[n:2 * n] + got[2 * n:3 * n]
+    core = lax.axis_index("sub") & 1
     four = lax.axis_index("facet") // 2
-    start = (got[A_HIGH:A_HIGH + 1] * 256.0 + got[A_HIGH + 1:A_HIGH + 2]).astype(jnp.int32)
-    low = lower((1, LANES))
-    starts = [
-        jnp.where(low, start[:, 2 * t * NQ:2 * t * NQ + 1], start[:, (2 * t + 1) * NQ:(2 * t + 1) * NQ + 1])
-        for t in range(2)
-    ]
+    low = quarter_low((1, LANES))
+    start = []
+    for f in range(NF):
+        row = f * NQ * MSG + NR2 + 1
+        at = A_HIGH - LANES
+        start.append((flat[row:row + 1, at:at + 1] * 256.0 + flat[row:row + 1, at + 1:at + 2]).astype(jnp.int32))
+    starts = [jnp.where(low, start[2 * t], start[2 * t + 1]) for t in range(2)]
     eight = iota((8, LANES), 0)
     turn_c, turn_s = phase_of(
         jnp.where(eight < 4, starts[0], starts[1]), (four * 4 + (eight & 3)) * (N_IMG // 8)
@@ -253,36 +267,36 @@
         fine_c, fine_s = phase_of(starts[t], iota((SUBG, LANES), 0))
         for p in range(4):
             tc, ts = turn_c[t * 4 + p:t * 4 + p + 1], turn_s[t * 4 + p:t * 4 + p + 1]
-            rho_ref[t, 0, p * SUBG:(p + 1) * SUBG, :] = fine_c * tc - fine_s * ts
-            rho_ref[t, 1, p * SUBG:(p + 1) * SUBG, :] = fine_s * tc + fine_c * ts
-    low = lower((NQ, LANES))
-    first, second = [], []
+            at = slice((p & 1) * SUBG, (p & 1) * SUBG + SUBG)
+            rho_ref[p // 2, t, 0, at, :] = fine_c * tc - fine_s * ts
+            rho_ref[p // 2, t, 1, at, :] = fine_s * tc + fine_c * ts
+    low = quarter_low((NQ, LANES))
     for row in range(NR2):
         x = [flat[pl.ds(f * NQ * MSG + row, NQ, stride=MSG), :] for f in range(NF)]
-        y = [roll(v, SUBG) for v in x]
-        first.append(jnp.concatenate([jnp.where(low, x[0], y[1]), jnp.where(low, x[2], y[3])], 1).astype(BF))
-        second.append(jnp.concatenate([jnp.where(low, y[0], x[1]), jnp.where(low, y[2], x[3])], 1).astype(BF))
-    both = jnp.dot(fwd_ref[...], jnp.concatenate(first + second, 0), preferred_element_type=F32)
-    m = 4 * SUBG
-    real, turned = 0.0, 0.0
-    for t in range(2):
-        rc, rs = rho_ref[t, 0], rho_ref[t, 1]
-        a, b = both[:m, t * LANES:(t + 1) * LANES], both[m:, t * LANES:(t + 1) * LANES]
-        real = real + (rc * a + rs * b)
-        turned = turned + (rc * b - rs * a)
-    real = real + roll(real, SUBG)
-    turned = turned + roll(turned, SUBG)
-    halves[...] = real - roll(turned, HALF) * lane_sign(m, HALF)
-    core = lax.axis_index("sub") & 1
-    keep_ref[...] = halves[pl.ds(core * LANES, LANES), :].astype(BF)
-    give_ref[...] = halves[pl.ds((1 - core) * LANES, LANES), :].astype(BF)
+        for t in range(2):
+            at = slice(t * LANES, (t + 1) * LANES)
+            a, b = x[2 * t], x[2 * t + 1]
+            rhs_ref[row * NQ:(row + 1) * NQ, at] = jnp.where(low, a, roll(b, HALF)).astype(BF)
+            rhs_ref[(NR2 + row) * NQ:(NR2 + row + 1) * NQ, at] = jnp.where(
+                low, roll(a, LANES - HALF), b
+            ).astype(BF)
+    both = jnp.dot(fwd_ref[1 - core], rhs_ref[...], preferred_element_type=F32)
+    give_ref[...] = combine(both, rho_ref.at[1 - core])
+    raw_ref[0] = flat[pl.ds(NR2, NDEV, stride=MSG), :]
+    raw_ref[1] = flat[pl.ds(NR2 + 1, NDEV, stride=MSG), :]
 
 
 def times(a, b):
     return a[0] * b[0] - a[1] * b[1], a[0] * b[1] + a[1] * b[0]
 
 
-def tables_kernel(vis_ref, left, basis, small):
+def tables_kernel(raw_ref, fwd_ref, rhs_ref, rho_ref, keep_ref, vis_ref, left, basis, small):
+    core = lax.axis_index("sub") & 1
+    got = jnp.concatenate([raw_ref[0].T, raw_ref[1].T], 0)
+    n = 5 * SLOT
+    vis_ref[...] = got[:n] + got[n:2 * n] + got[2 * n:3 * n]
+    both = jnp.dot(fwd_ref[core], rhs_ref[...], preferred_element_type=F32)
+    keep_ref[...] = combine(both, rho_ref.at[core])
     slot = 0
     for l in range(2):
         for which in range(2):
@@ -314,29 +328,23 @@
                     left[l, 0:SUBG, at] = jnp.concatenate(re, 0)
                     left[l, SUBG:, at] = jnp.concatenate(im, 0)
                 else:
-                    for h in range(2):
-                        base = h * SUBG
-                        basis[l, base:base + HALF, at] = jnp.concatenate(re[h * 4:h * 4 + 4], 0).astype(BF)
-                        basis[l, base + HALF:base + SUBG, at] = jnp.concatenate(im[h * 4:h * 4 + 4], 0).astype(BF)
+                    basis[l, 0:SUBG, at] = jnp.concatenate(re, 0).astype(BF)
+                    basis[l, SUBG:, at] = jnp.concatenate(im, 0).astype(BF)
             slot += 1
-
-
-def swap_half(x):
-    return jnp.where((iota(x.shape, 1) & HALF) == 0, roll(x, LANES - HALF), roll(x, HALF))
 
 
 def visibility_kernel(keep_ref, other_ref, vis_ref, left, basis, corrected_ref, back_ref, inner, phasor):
     upper_core = (lax.axis_index("sub") & 1) == 1
     keep, other = keep_ref[...].astype(F32), other_ref[...].astype(F32)
     halves = jnp.where(upper_core, other, keep), jnp.where(upper_core, keep, other)
-    subgrids = jnp.where(lower((LANES, LANES)), halves[0], halves[1])
-    sign = lane_sign(SUBG, HALF)
+    subgrids = jnp.where(quarter_low((LANES, LANES)), roll(halves[0], LANES - HALF), halves[1])
+    sign = lane_sign(SUBG, SUBG)
     sums = []
     returned = [[None, None], [None, None]]
     for l in range(2):
         obs_r, obs_i, level = [vis_ref[c * SLOT + l * 8:c * SLOT + l * 8 + 8, :] for c in range(2, 5)]
         sub = subgrids[l * SUBG:(l + 1) * SUBG]
-        matrix = jnp.concatenate([sub * sign, swap_half(sub)], 0).astype(BF)
+        matrix = jnp.concatenate([sub * sign, roll(sub, SUBG)], 0).astype(BF)
         inner[l] = jnp.dot(matrix, basis[l], preferred_element_type=F32)
         pred_r, pred_i = [], []
         for k in range(8):
@@ -362,40 +370,52 @@
         product = lax.dot_general(
             phasor[l], basis[l], (((1,), (1,)), ((), ())), preferred_element_type=F32
         )
-        sums.append(product[:SUBG] * sign + swap_half(product[SUBG:]))
+        sums.append(product[:SUBG] * sign + roll(product[SUBG:], SUBG))
     corrected_ref[...] = jnp.concatenate(sums, 0).astype(BF)
     back = jnp.concatenate([returned[0][0], returned[0][1], returned[1][0], returned[1][1]], 0)
     back = [part.astype(F32) for part in split3(back)]
     back_ref[...] = jnp.concatenate(back + [jnp.zeros((2 * SLOT, LANES), F32)], 0)
 
 
-def images_kernel(mine_ref, other_ref, back_ref, rho_ref, adj_ref, msg_ref, flat):
-    upper_core = (lax.axis_index("sub") & 1) == 1
-    mine, other = mine_ref[...].astype(F32), other_ref[...].astype(F32)
-    low = lower((LANES, LANES))
-    rows = []
-    for x in (jnp.where(upper_core, other, mine), jnp.where(upper_core, mine, other)):
-        y = roll(x, SUBG)
-        rows.append(jnp.where(low != upper_core, x, y))
-    corrected = jnp.concatenate(rows, 0)
-    turned = roll(corrected, HALF) * -lane_sign(4 * SUBG, HALF)
+def partial_images(x, pair, rho_ref, adj_ref):
+    core = lax.axis_index("sub") & 1
+    x = x.astype(F32)
+    moved = jnp.where(core == 1, roll(x, LANES - HALF), roll(x, HALF))
+    x = jnp.where(quarter_low(x.shape) != (core == 1), x, moved)
+    turned = roll(x, SUBG) * -lane_sign(LANES, SUBG)
     cols = []
     for t in range(2):
-        rc, rs = rho_ref[t, 0], rho_ref[t, 1]
+        rc, rs = rho_ref[pair, t, 0], rho_ref[pair, t, 1]
         cols.append(
-            jnp.concatenate(
-                [(corrected * rc + turned * rs).astype(BF), (corrected * rs - turned * rc).astype(BF)], 0
-            )
+            jnp.concatenate([(x * rc + turned * rs).astype(BF), (x * rs - turned * rc).astype(BF)], 0)
         )
-    images = jnp.dot(adj_ref[...], jnp.concatenate(cols, 1), preferred_element_type=F32)
-    low = lower((NQ, LANES))
+    half = NQ * NR2
+    table = jnp.concatenate(
+        [
+            adj_ref[pair, pl.ds(pl.multiple_of(core * half, half), half), :],
+            adj_ref[pair, pl.ds(pl.multiple_of((1 - core) * half, half), half), :],
+        ], 0
+    )
+    return jnp.dot(table, jnp.concatenate(cols, 1), preferred_element_type=F32)
+
+
+def mine_kernel(corrected_ref, rho_ref, adj_ref, part_ref):
+    part_ref[...] = partial_images(corrected_ref[...], lax.axis_index("sub") & 1, rho_ref, adj_ref)
+
+
+def images_kernel(part_ref, other_ref, back_ref, rho_ref, adj_ref, msg_ref, flat):
+    pair = 1 - (lax.axis_index("sub") & 1)
+    images = part_ref[...] + partial_images(other_ref[...], pair, rho_ref, adj_ref)
+    low = quarter_low((NQ, LANES))
     for row in range(NR2):
         for t in range(2):
             at = slice(t * LANES, (t + 1) * LANES)
             a = images[row * NQ:(row + 1) * NQ, at]
             b = images[(NR2 + row) * NQ:(NR2 + row + 1) * NQ, at]
-            flat[pl.ds(2 * t * NQ * MSG + row, NQ, stride=MSG), :] = jnp.where(low, a, roll(b, SUBG))
-            flat[pl.ds((2 * t + 1) * NQ * MSG + row, NQ, stride=MSG), :] = jnp.where(low, roll(a, SUBG), b)
+            flat[pl.ds(2 * t * NQ * MSG + row, NQ, stride=MSG), :] = jnp.where(low, a, roll(b, HALF))
+            flat[pl.ds((2 * t + 1) * NQ * MSG + row, NQ, stride=MSG), :] = jnp.where(
+                low, roll(a, LANES - HALF), b
+            )
     flat[pl.ds(NR2, NDEV, stride=MSG), :] = back_ref[...].T
     flat[pl.ds(NR2 + 1, NDEV, stride=MSG), :] = jnp.zeros((NDEV, LANES), F32)
     msg_ref[...] = flat[...].astype(BF)
@@ -416,42 +436,39 @@
         res_ref[c:c + 1, :] = jnp.sum(
             jnp.where(here, found[c * SLOT:(c + 1) * SLOT], 0.0), 0, keepdims=True
         )
-    copies = [pltpu.make_async_copy(res_ref, res_hbm, sems.at[4])]
+    copies = [pltpu.make_async_copy(res_ref, res_hbm, sems.at[8])]
     copies[0].start()
 
-    freq = iota((NQ, LANES), 0) * (N_IMG // NQ) + (iota((NQ, LANES), 1) & (SUBG - 1))
-    ph_c, ph_s = phase_of(meta_ref[2:3, :LANES], freq)
-    ph_s = -ph_s * lane_sign(NQ, SUBG)
-    tw_c, tw_s = tw_ref[0], tw_ref[1]
-    sign = lane_sign(LANES, SUBG)
-    quarter = iota((NQ, LANES), 1) // HALF
-    images = [None] * RD
-    for row in range(NR2):
-        x = []
-        for c in range(2):
-            image = flat[pl.ds(c * MSG + row, NQ, stride=2 * MSG), :]
-            x.append(image + flat[pl.ds((2 * NQ + c) * MSG + row, NQ, stride=2 * MSG), :])
-        r32, r64, r96 = [[roll(v, k * HALF) for v in x] for k in (1, 2, 3)]
-        choose = lambda *v: jnp.where(
-            quarter < 2, jnp.where(quarter == 0, v[0], v[1]), jnp.where(quarter == 2, v[2], v[3])
-        )
-        for h, image in enumerate(
-            (choose(x[0], r32[1], r32[0], r64[1]), choose(r64[0], r96[1], r96[0], x[1]))
-        ):
-            images[row + h * NR2] = (image * ph_c + roll(image, SUBG) * ph_s).astype(BF)
+    sign = -lane_sign(NQ, SUBG)
+    low = quarter_low((NQ, LANES))
     group = 4
     for base in range(0, RD, group):
-        spread = jnp.dot(
-            coarse_ref[...], jnp.concatenate(images[base:base + group], 1), preferred_element_type=F32
-        )
+        h = base // NR2
+        if base % NR2 == 0:
+            lane1 = iota((NQ, LANES), 1)
+            freq = iota((NQ, LANES), 0) * (N_IMG // NQ) + ((lane1 & (SUBG - 1)) ^ (h * HALF))
+            ph_c, ph_s = phase_of(meta_ref[2:3, :LANES], freq)
+        images = []
+        for i in range(group):
+            row = (base + i) % NR2
+            x = [
+                flat[pl.ds(c * MSG + row, NQ, stride=2 * MSG), :]
+                + flat[pl.ds((2 * NQ + c) * MSG + row, NQ, stride=2 * MSG), :]
+                for c in range(2)
+            ]
+            image = jnp.where(low, x[h], x[1 - h])
+            turn = roll(image, SUBG) * sign
+            images.append(
+                jnp.concatenate([image * ph_c + turn * ph_s, turn * ph_c - image * ph_s], 0).astype(BF)
+            )
+        spread = jnp.dot(coarse_ref[...], jnp.concatenate(images, 1), preferred_element_type=F32)
+        tw_c, tw_s = tw_ref[2 * h], tw_ref[2 * h + 1]
         stacked = []
         for i in range(group):
-            first = spread[:LANES, i * LANES:(i + 1) * LANES]
-            second = spread[LANES:, i * LANES:(i + 1) * LANES]
-            z = (tw_c * first - tw_s * second) - roll(tw_s * first + tw_c * second, SUBG) * sign
-            stacked.append(z.astype(BF))
+            at = slice(i * LANES, (i + 1) * LANES)
+            stacked.append((tw_c * spread[:LANES, at] + tw_s * spread[LANES:, at]).astype(BF))
         out = lax.dot_general(
-            col_ref[...], jnp.concatenate(stacked, 0), (((1,), (1,)), ((), ())),
+            col_ref[h * LANES:(h + 1) * LANES], jnp.concatenate(stacked, 0), (((1,), (1,)), ((), ())),
             preferred_element_type=F32,
         )
         for i in range(group):
@@ -465,15 +482,17 @@
             half = base // 8
             for part in range(2):
                 where = slice(half * 8, half * 8 + 8)
-                for a in range(NA):
-                    at = ((part * 2 + half) * NA + a) * 8
-                    out_ref[part, where, a * LANES:(a + 1) * LANES] = turned[at:at + 8, :]
-                copy = pltpu.make_async_copy(
-                    out_ref.at[part, where, :], out_hbm.at[0, part, where, :],
-                    sems.at[half * 2 + part],
-                )
-                copy.start()
-                copies.append(copy)
+                for piece in range(2):
+                    for a in range(piece * NA // 2, (piece + 1) * NA // 2):
+                        at = ((part * 2 + half) * NA + a) * 8
+                        out_ref[part, where, a * LANES:(a + 1) * LANES] = turned[at:at + 8, :]
+                    wide = slice(piece * NA // 2 * LANES, (piece + 1) * NA // 2 * LANES)
+                    copy = pltpu.make_async_copy(
+                        out_ref.at[part, where, wide], out_hbm.at[0, part, where, wide],
+                        sems.at[(half * 2 + part) * 2 + piece],
+                    )
+                    copy.start()
+                    copies.append(copy)
     for copy in copies:
         copy.wait()
 
@@ -501,7 +520,8 @@
     limit = pltpu.CompilerParams(vmem_limit_bytes=32 << 20)
     shape = jax.ShapeDtypeStruct
     message = shape((NDEV * MSG, LANES), BF)
-    table = shape((8 * SUBG, NQ * RD), BF)
+    fwd_table = shape((2, 4 * SUBG, NQ * RD), BF)
+    adj_table = shape((2, NQ * RD, 4 * SUBG), BF)
     square = shape((LANES, LANES), BF)
     flat = pltpu.VMEM((NDEV * MSG, LANES), F32)
 
@@ -523,7 +543,7 @@
     )
     sent, meta, fwd, adj = call(
         send_kernel, "send", in_place(inputs + (t["row_fwd"], t["row_adj"])),
-        (message, shape((8, NV), jnp.int32), table, table),
+        (message, shape((8, NV), jnp.int32), fwd_table, adj_table),
         [pltpu.SMEM((1, 2), jnp.int32)]
         + [pltpu.VMEM(x.shape, x.dtype) for x in inputs[1:]]
         + [
@@ -534,15 +554,21 @@
         in_specs=[HBM] * (len(inputs) + 2),
     )
     got = exchange(sent)
-    keep, give, vis, rho = call(
+    give, rhs, rho, raw = call(
         rows_kernel, "rows", (got, fwd),
-        (square, square, shape((5 * SLOT, LANES), F32), shape((2, 2, 4 * SUBG, LANES), F32)),
-        [flat, pltpu.VMEM((4 * SUBG, LANES), F32)],
+        (
+            square, shape((NQ * RD, 2 * LANES), BF), shape((2, 2, 2, LANES, LANES), F32),
+            shape((2, NDEV, LANES), F32),
+        ),
+        [flat],
     )
     other = other_core(give)
-    left, basis = call(
-        tables_kernel, "tables", (vis,),
-        (shape((2, 2 * SUBG, NV), F32), shape((2, 2 * SUBG, NV), BF)),
+    keep, vis, left, basis = call(
+        tables_kernel, "tables", (raw, fwd, rhs, rho),
+        (
+            square, shape((5 * SLOT, LANES), F32), shape((2, 2 * SUBG, NV), F32),
+            shape((2, 2 * SUBG, NV), BF),
+        ),
         [pltpu.VMEM((4, 4, SUBG, LANES), F32)],
     )
     corrected, back = call(
@@ -550,9 +576,11 @@
         (square, shape((LANES, LANES), F32)),
         [pltpu.VMEM((2, 2 * SUBG, NV), F32), pltpu.VMEM((2, 2 * SUBG, NV), BF)],
     )
-    (answer,) = call(
-        images_kernel, "images", (corrected, other_core(corrected), back, rho, adj), (message,), [flat]
-    )
+    other = other_core(corrected)
+    (part,) = call(
+        mine_kernel, "mine", (corrected, rho, adj), (shape((NQ * RD, 2 * LANES), F32),), []
+    )
+    (answer,) = call(images_kernel, "images", (part, other, back, rho, adj), (message,), [flat])
     facet_adjoint, residual = call(
         facet_kernel, "facet",
         (exchange(answer), meta, t["coarse_adj"], t["tw_adj"], t["col_adj"]),
@@ -562,7 +590,7 @@
             pltpu.VMEM((4 * NA * 8, LANES), F32),
             pltpu.VMEM((2, RD, NA * LANES), F32),
             pltpu.VMEM((2, NV), F32),
-            pltpu.SemaphoreType.DMA((5,)),
+            pltpu.SemaphoreType.DMA((9,)),
         ],
         out_specs=(HBM, HBM),
     )

time: 50.5 us -> 49.7 us (0.984)
  waiting for transfers between devices: 1.22 us -> 0.54 us
    ppermute x2, waiting for transfers between devices: 1.22 us -> 0.54 us  [other_core(): return lax.ppermute(x, 'sub', [(i, i ^ 1) for i in range(NQ)])]
    pallas_call x6 -> x7, Pallas kernels: 8.81 us -> 8.72 us  [call(): pl.pallas_call(kernel, out_shape=outs, in_specs=in_specs or [VMEM] * len(...]
  transfers between devices with their start and end apart: 2 -> 2, of which waited for: 2 -> 2; matrix products, arithmetic and copies ran while one was open for 0% -> 0% of each run, Pallas kernels for 1% -> 2%
where the time goes in v4:
time: 49.7 us; the launch traced here: 49.5 us
  blocking collectives  37.9 us (76%)
  Pallas kernels  8.72 us (18%)
  starting transfers between devices  1.62 us (3%)
  between operations  0.71 us (1%)
  waiting for transfers between devices  0.54 us (1%)
    all_to_all x2, blocking collectives, exchange(): lax.all_to_all(pairs, ALL, split_axis=0, concat_axis=0, tiled=True)  37.9 us
    pallas_call x7, Pallas kernels, call(): pl.pallas_call(kernel, out_shape=outs, in_specs=in_specs or [VMEM] * len(...  8.72 us
    ppermute x2, starting transfers between devices, other_core(): return lax.ppermute(x, 'sub', [(i, i ^ 1) for i in range(NQ)])  1.62 us
  transfers between devices with their start and end apart: 2, of which 2 were waited for; matrix products, arithmetic and copies ran while one was open for 0% of the time, Pallas kernels for 2%

profile of v4, /device:TPU:1, one launch (start us, length us, event | category | flops | bytes accessed | tf_op | source)
XLA Modules:
  0.0 49.5 jit_solution(4972688826758106518)
XLA Ops:
  0.6 3.0 %send.1 = (bf16[1280,128]{1,0:T(8,128)(2,1)S(1)}, s32[8,1024]{1,0:T(8,128)S(1)}, bf16[2,256,512]{2,1,0:T(8,128)(2,1)S(1)}, bf16[2,512,256]{2,1,0:T(8,128)(2,1)S(1)}) custom-call(s32[1,2]{1,0:T(1,128)} %off_hbm.1, bf16[1,2,16,8192]{3,2,1,0:T(8,128)(2,1)} %slab_hbm.1, f32[2,1024]{1,0:T(2,128)} %pos_hbm.1, f32[2,1024]{1,0:T(2,128)} %obs_hbm.1, ...), custom_call_target="tpu_custom_call" | custom-call | flops 1048576 | bytes 2097152 | tf_op jit(solution)/shard_map/send/pallas_call | solution.py:529
  3.7 22.7 %all_to_all.10 = bf16[640,2,128]{2,1,0:T(2,128)(2,1)S(1)} all-to-all(bf16[640,2,128]{2,1,0:T(2,128)(2,1)S(1)} %bitcast.9), channel_id=1, replica_groups=mesh['facet'=4,'sub'=32] {'facet','sub'}, dimensions={0} | all-to-all | bytes 655360 | tf_op jit(solution)/shard_map/all_to_all | solution.py:511
  26.4 0.7 %rows.1 = (bf16[128,128]{1,0:T(8,128)(2,1)S(1)}, bf16[512,256]{1,0:T(8,128)(2,1)S(1)}, f32[2,2,2,128,128]{4,3,2,1,0:T(8,128)S(1)}, f32[2,128,128]{2,1,0:T(8,128)S(1)}) custom-call(bf16[1280,128]{1,0:T(8,128)(2,1)S(1)} %bitcast.7, bf16[2,256,512]{2,1,0:T(8,128)(2,1)S(1)} %get-tuple-element.17.fwd_ref), custom_call_target="tpu_custom_call" | custom-call | flops 1048576 | bytes 2097152 | tf_op jit(solution)/shard_map/rows/pallas_call | solution.py:529
  27.1 1.2 %collective-permute-start = (bf16[128,128]{1,0:T(8,128)(2,1)S(1)}, bf16[128,128]{1,0:T(8,128)(2,1)S(1)}, u32[]{:S(2)}, u32[]{:S(2)}) collective-permute-start(bf16[128,128]{1,0:T(8,128)(2,1)S(1)} %get-tuple-element.22), channel_id=1, source_target_pairs={{0,1},{1,0},{2,3},{3,2},{4,5},{5,4},{6,7},{7,6},{8,9},{9,8},{10,11... | collective-permute-start | bytes 98312 | tf_op jit(solution)/shard_map/ppermute | solution.py:515
  28.3 0.8 %tables.1 = (bf16[128,128]{1,0:T(8,128)(2,1)S(1)}, f32[80,128]{1,0:T(8,128)S(1)}, f32[2,128,1024]{2,1,0:T(8,128)S(1)}, bf16[2,128,1024]{2,1,0:T(8,128)(2,1)S(1)}) custom-call(f32[2,128,128]{2,1,0:T(8,128)S(1)} %get-tuple-element.18.raw_ref, bf16[2,256,512]{2,1,0:T(8,128)(2,1)S(1)} %get-tuple-element.17.fwd_ref, ...), custom_call_target="tpu_custom_call" | custom-call | flops 1048576 | bytes 2097152 | tf_op jit(solution)/shard_map/tables/pallas_call | solution.py:529
  29.1 0.1 collective-permute-done.other_ref
  29.1 1.1 %visibilities.1 = (bf16[128,128]{1,0:T(8,128)(2,1)S(1)}, f32[128,128]{1,0:T(8,128)S(1)}) custom-call(bf16[128,128]{1,0:T(8,128)(2,1)S(1)} %get-tuple-element.21.keep_ref, bf16[128,128]{1,0:T(8,128)(2,1)S(1)} %collective-permute-done.other_ref, f32[80,128]{1,0:T(8,128)S(1)} %get-tuple-element.23.vis_ref, f32[2,128,1024]{2,1,0:T(8,128)S(1)} %get-tuple-element.24.left, ...), custom_call_target="tpu_custom_call" | custom-call | flops 1048576 | bytes 2097152 | tf_op jit(solution)/shard_map/visibilities/pallas_call | solution.py:529
  30.2 0.4 collective-permute-start.1
  30.7 0.4 mine.1.part_ref
  31.0 0.5 collective-permute-done.1.other_ref
  31.5 0.6 %images.1 = bf16[1280,128]{1,0:T(8,128)(2,1)S(1)} custom-call(f32[512,256]{1,0:T(8,128)S(1)} %mine.1.part_ref, bf16[128,128]{1,0:T(8,128)(2,1)S(1)} %collective-permute-done.1.other_ref, f32[128,128]{1,0:T(8,128)S(1)} %get-tuple-element.28.back_ref, f32[2,2,2,128,128]{4,3,2,1,0:T(8,128)S(1)} %get-tuple-element.20.rho_ref, ...), custom_call_target="tpu_custom_call" | custom-call | flops 1048576 | bytes 2097152 | tf_op jit(solution)/shard_map/images/pallas_call | solution.py:529
  32.1 0.0 copy-start
  32.1 0.0 copy-start.1
  32.1 0.0 copy-start.2
  32.1 15.2 %all_to_all.11 = bf16[640,2,128]{2,1,0:T(2,128)(2,1)S(1)} all-to-all(bf16[640,2,128]{2,1,0:T(2,128)(2,1)S(1)} %bitcast.8), channel_id=1, replica_groups=mesh['facet'=4,'sub'=32] {'facet','sub'}, dimensions={0} | all-to-all | bytes 655360 | tf_op jit(solution)/shard_map/all_to_all | solution.py:511
  47.4 0.0 copy-done
  47.4 0.0 copy-done.1
  47.4 0.0 copy-done.2
  47.4 2.1 %facet.1 = (f32[1,2,16,8192]{3,2,1,0:T(8,128)}, f32[2,1024]{1,0:T(2,128)}) custom-call(bf16[1280,128]{1,0:T(8,128)(2,1)S(1)} %bitcast.6, s32[8,1024]{1,0:T(8,128)S(1)} %get-tuple-element.29.meta_ref, bf16[256,64]{1,0:T(8,128)(2,1)S(1)} %copy-done.1, f32[4,128,128]{2,1,0:T(8,128)S(1)} %copy-done, bf16[256,128]{1,0:T(8,128)(2,1)S(1)} %copy-done.2), custom_call_target="tpu_custom_call" | custom-call | flops 1048576 | bytes 2097152 | tf_op jit(solution)/shard_map/facet/pallas_call | solution.py:529
Async XLA Ops:
  27.1 2.1 %collective-permute-start = (bf16[128,128]{1,0:T(8,128)(2,1)S(1)}, bf16[128,128]{1,0:T(8,128)(2,1)S(1)}, u32[]{:S(2)}, u32[]{:S(2)}) collective-permute-start(bf16[128,128]{1,0:T(8,128)(2,1)S(1)} %get-tuple-element.22), channel_id=1, source_target_pairs={{0,1},{1,0},{2,3},{3,2},{4,5},{5,4},{6,7},{7,6},{8,9},{9,8},{10,11... | collective-permute-start | bytes 98312 | tf_op jit(solution)/shard_map/ppermute | solution.py:515
  30.2 1.3 %collective-permute-start.1 = (bf16[128,128]{1,0:T(8,128)(2,1)S(1)}, bf16[128,128]{1,0:T(8,128)(2,1)S(1)}, u32[]{:S(2)}, u32[]{:S(2)}) collective-permute-start(bf16[128,128]{1,0:T(8,128)(2,1)S(1)} %get-tuple-element.26.corrected_ref), channel_id=1, source_target_pairs={{0,1},{1,0},{2,3},{3,2},{4,5},{5,4},{6,7},{7,6},{8,9},{9,8},{10,11... | collective-permute-start | bytes 98312 | tf_op jit(solution)/shard_map/ppermute | solution.py:515
  32.1 15.3 %copy-start = (f32[4,128,128]{2,1,0:T(8,128)S(1)}, f32[4,128,128]{2,1,0:T(8,128)}, u32[]{:S(2)}) copy-start(f32[4,128,128]{2,1,0:T(8,128)} %constant.17.clone.tw_ref) | copy-start | bytes 786436
  32.1 15.3 %copy-start.1 = (bf16[256,64]{1,0:T(8,128)(2,1)S(1)}, bf16[256,64]{1,0:T(8,128)(2,1)}, u32[]{:S(2)}) copy-start(bf16[256,64]{1,0:T(8,128)(2,1)} %constant.18.clone.coarse_ref) | copy-start | bytes 98308
  32.1 15.3 %copy-start.2 = (bf16[256,128]{1,0:T(8,128)(2,1)S(1)}, bf16[256,128]{1,0:T(8,128)(2,1)}, u32[]{:S(2)}) copy-start(bf16[256,128]{1,0:T(8,128)(2,1)} %constant.15.clone.col_ref) | copy-start | bytes 196612

commit v5 on v4

--- a/solution.py
+++ b/solution.py
@@ -116,7 +116,7 @@
 def send_kernel(
     off_hbm, slab_hbm, pos_hbm, obs_hbm, ids_hbm, clip_hbm, table_hbm, tw_hbm, fwd_hbm, adj_hbm,
     msg_ref, meta_ref, fwd_ref, adj_ref, off_ref, slab_ref, pos_ref, obs_ref, ids_ref, clip_ref, table_ref, tw_ref,
-    wide, flat, sems,
+    wide, flat, y_ref, z_ref, sems,
 ):
     pairs = [
         (ids_hbm, ids_ref), (clip_hbm, clip_ref), (pos_hbm, pos_ref), (obs_hbm, obs_ref),
@@ -194,39 +194,35 @@
         ], 0
     )
     low = lower((NQ, LANES))
-    for base in range(0, NR2, 2):
-        which = [base, base + NR2, base + 1, base + 1 + NR2]
-        cols = [
-            jnp.concatenate(
-                [wide[0, pl.ds(r, NA, stride=RD), :], wide[1, pl.ds(r, NA, stride=RD), :]], 0
-            ).astype(BF)
-            for r in which
-        ]
-        y = jnp.dot(col, jnp.concatenate(cols, 1), preferred_element_type=F32)
+    cols = [
+        jnp.concatenate(
+            [wide[0, pl.ds(r, NA, stride=RD), :], wide[1, pl.ds(r, NA, stride=RD), :]], 0
+        ).astype(BF)
+        for r in range(RD)
+    ]
+    y_ref[...] = jnp.dot(col, jnp.concatenate(cols, 1), preferred_element_type=F32)
+    for row in range(NR2):
         both = []
-        for i in range(4):
-            yr = y[:SUBG, i * LANES:(i + 1) * LANES]
-            yi = y[SUBG:, i * LANES:(i + 1) * LANES]
+        for r in (row, row + NR2):
+            at = slice(r * LANES, (r + 1) * LANES)
+            yr, yi = y_ref[:SUBG, at], y_ref[SUBG:, at]
             zr = yr * tw_c - yi * tw_s
             zi = yr * tw_s + yi * tw_c
             both.append(jnp.concatenate([zr, zi], 1).astype(BF))
-        stacked = [
-            both[2 * pair + i][c * HALF:(c + 1) * HALF]
-            for pair in range(2) for c in range(2) for i in range(2)
-        ]
-        out = lax.dot_general(
-            coarse, jnp.concatenate(stacked, 0), (((1,), (1,)), ((), ())),
-            preferred_element_type=F32,
-        )
-        for pair in range(2):
-            at = pair * LANES
-            x, y = out[:NQ, at:at + LANES], out[NQ:, at:at + LANES]
-            re, im = x * ph_c + y * ph_s, y * ph_c - x * ph_s
-            pieces = [jnp.where(low, re, roll(im, SUBG)), jnp.where(low, roll(re, SUBG), im)]
-            for c in range(2):
-                for g in range(2):
-                    row = (2 * NQ * g + c) * MSG + base + pair
-                    flat[pl.ds(row, NQ, stride=2 * MSG), :] = pieces[c]
+        for i, (c, h) in enumerate(((0, 0), (0, 1), (1, 0), (1, 1))):
+            at = row * LANES + i * HALF
+            z_ref[at:at + HALF, :] = both[h][c * HALF:(c + 1) * HALF]
+    out = lax.dot_general(
+        coarse, z_ref[...], (((1,), (1,)), ((), ())), preferred_element_type=F32
+    )
+    for row in range(NR2):
+        at = slice(row * LANES, (row + 1) * LANES)
+        x, y = out[:NQ, at], out[NQ:, at]
+        re, im = x * ph_c + y * ph_s, y * ph_c - x * ph_s
+        pieces = [jnp.where(low, re, roll(im, SUBG)), jnp.where(low, roll(re, SUBG), im)]
+        for c in range(2):
+            for g in range(2):
+                flat[pl.ds((2 * NQ * g + c) * MSG + row, NQ, stride=2 * MSG), :] = pieces[c]
     msg_ref[...] = flat[...].astype(BF)
     for copy in later:
         copy.wait()
@@ -248,28 +244,30 @@
     return (real - roll(turned, SUBG) * lane_sign(LANES, SUBG)).astype(BF)
 
 
+def row_phases(tails, pair, rho_ref):
+    first = (lax.axis_index("facet") // 2) * 4 + pair * 2
+    low = quarter_low((1, LANES))
+    start = [(v[:, 0:1] * 256.0 + v[:, 1:2]).astype(jnp.int32) for v in tails]
+    starts = [jnp.where(low, start[2 * t], start[2 * t + 1]) for t in range(2)]
+    eight = iota((8, LANES), 0)
+    turn_c, turn_s = phase_of(
+        jnp.where(eight < 4, starts[0], starts[1]), (first + (eight & 1)) * (N_IMG // 8)
+    )
+    for t in range(2):
+        fine_c, fine_s = phase_of(starts[t], iota((SUBG, LANES), 0))
+        for p in range(2):
+            tc, ts = turn_c[t * 4 + p:t * 4 + p + 1], turn_s[t * 4 + p:t * 4 + p + 1]
+            at = slice(p * SUBG, (p + 1) * SUBG)
+            rho_ref[t, 0, at, :] = fine_c * tc - fine_s * ts
+            rho_ref[t, 1, at, :] = fine_s * tc + fine_c * ts
+
+
 def rows_kernel(got_ref, fwd_ref, give_ref, rhs_ref, rho_ref, raw_ref, flat):
     flat[...] = got_ref[...].astype(F32)
     core = lax.axis_index("sub") & 1
-    four = lax.axis_index("facet") // 2
-    low = quarter_low((1, LANES))
-    start = []
-    for f in range(NF):
-        row = f * NQ * MSG + NR2 + 1
-        at = A_HIGH - LANES
-        start.append((flat[row:row + 1, at:at + 1] * 256.0 + flat[row:row + 1, at + 1:at + 2]).astype(jnp.int32))
-    starts = [jnp.where(low, start[2 * t], start[2 * t + 1]) for t in range(2)]
-    eight = iota((8, LANES), 0)
-    turn_c, turn_s = phase_of(
-        jnp.where(eight < 4, starts[0], starts[1]), (four * 4 + (eight & 3)) * (N_IMG // 8)
-    )
-    for t in range(2):
-        fine_c, fine_s = phase_of(starts[t], iota((SUBG, LANES), 0))
-        for p in range(4):
-            tc, ts = turn_c[t * 4 + p:t * 4 + p + 1], turn_s[t * 4 + p:t * 4 + p + 1]
-            at = slice((p & 1) * SUBG, (p & 1) * SUBG + SUBG)
-            rho_ref[p // 2, t, 0, at, :] = fine_c * tc - fine_s * ts
-            rho_ref[p // 2, t, 1, at, :] = fine_s * tc + fine_c * ts
+    at = A_HIGH - LANES
+    tails = [flat[f * NQ * MSG + NR2 + 1:f * NQ * MSG + NR2 + 2, at:at + 2] for f in range(NF)]
+    row_phases(tails, 1 - core, rho_ref)
     low = quarter_low((NQ, LANES))
     for row in range(NR2):
         x = [flat[pl.ds(f * NQ * MSG + row, NQ, stride=MSG), :] for f in range(NF)]
@@ -281,7 +279,7 @@
                 low, roll(a, LANES - HALF), b
             ).astype(BF)
     both = jnp.dot(fwd_ref[1 - core], rhs_ref[...], preferred_element_type=F32)
-    give_ref[...] = combine(both, rho_ref.at[1 - core])
+    give_ref[...] = combine(both, rho_ref)
     raw_ref[0] = flat[pl.ds(NR2, NDEV, stride=MSG), :]
     raw_ref[1] = flat[pl.ds(NR2 + 1, NDEV, stride=MSG), :]
 
@@ -290,13 +288,15 @@
     return a[0] * b[0] - a[1] * b[1], a[0] * b[1] + a[1] * b[0]
 
 
-def tables_kernel(raw_ref, fwd_ref, rhs_ref, rho_ref, keep_ref, vis_ref, left, basis, small):
+def tables_kernel(raw_ref, fwd_ref, rhs_ref, keep_ref, vis_ref, rho_ref, left, basis, small):
     core = lax.axis_index("sub") & 1
+    at = A_HIGH - LANES
+    row_phases([raw_ref[1, f * NQ:f * NQ + 1, at:at + 2] for f in range(NF)], core, rho_ref)
     got = jnp.concatenate([raw_ref[0].T, raw_ref[1].T], 0)
     n = 5 * SLOT
     vis_ref[...] = got[:n] + got[n:2 * n] + got[2 * n:3 * n]
     both = jnp.dot(fwd_ref[core], rhs_ref[...], preferred_element_type=F32)
-    keep_ref[...] = combine(both, rho_ref.at[core])
+    keep_ref[...] = combine(both, rho_ref)
     slot = 0
     for l in range(2):
         for which in range(2):
@@ -339,40 +339,42 @@
     halves = jnp.where(upper_core, other, keep), jnp.where(upper_core, keep, other)
     subgrids = jnp.where(quarter_low((LANES, LANES)), roll(halves[0], LANES - HALF), halves[1])
     sign = lane_sign(SUBG, SUBG)
-    sums = []
-    returned = [[None, None], [None, None]]
     for l in range(2):
-        obs_r, obs_i, level = [vis_ref[c * SLOT + l * 8:c * SLOT + l * 8 + 8, :] for c in range(2, 5)]
         sub = subgrids[l * SUBG:(l + 1) * SUBG]
         matrix = jnp.concatenate([sub * sign, roll(sub, SUBG)], 0).astype(BF)
         inner[l] = jnp.dot(matrix, basis[l], preferred_element_type=F32)
-        pred_r, pred_i = [], []
+    predicted = [[], [], [], []]
+    for l in range(2):
         for k in range(8):
             at = slice(k * LANES, (k + 1) * LANES)
             lr, li = left[l, 0:SUBG, at], left[l, SUBG:, at]
             ir, ii = inner[l, 0:SUBG, at], inner[l, SUBG:, at]
-            pred_r.append(jnp.sum(lr * ir - li * ii, 0, keepdims=True))
-            pred_i.append(jnp.sum(lr * ii + li * ir, 0, keepdims=True))
-        mis_r = obs_r - jnp.concatenate(pred_r, 0)
-        mis_i = obs_i - jnp.concatenate(pred_i, 0)
-        live = level > 0.0
-        threshold = jnp.where(live, level, 1.0)
-        magnitude = jnp.sqrt(mis_r * mis_r + mis_i * mis_i)
-        weight = jnp.where(live, threshold / jnp.maximum(magnitude, threshold), 0.0)
-        wr, wi = weight * mis_r, weight * mis_i
-        returned[0][l], returned[1][l] = wr, wi
+            predicted[l].append(jnp.sum(lr * ir - li * ii, 0, keepdims=True))
+            predicted[2 + l].append(jnp.sum(lr * ii + li * ir, 0, keepdims=True))
+    rows_of = lambda c: vis_ref[c * SLOT:(c + 1) * SLOT, :]
+    mis_r = rows_of(2) - jnp.concatenate(predicted[0] + predicted[1], 0)
+    mis_i = rows_of(3) - jnp.concatenate(predicted[2] + predicted[3], 0)
+    level = rows_of(4)
+    live = level > 0.0
+    threshold = jnp.where(live, level, 1.0)
+    magnitude = jnp.sqrt(mis_r * mis_r + mis_i * mis_i)
+    weight = jnp.where(live, threshold / jnp.maximum(magnitude, threshold), 0.0)
+    wr, wi = weight * mis_r, weight * mis_i
+    for l in range(2):
         for k in range(8):
             at = slice(k * LANES, (k + 1) * LANES)
             lr, li = left[l, 0:SUBG, at], left[l, SUBG:, at]
-            vr, vi = wr[k:k + 1, :], wi[k:k + 1, :]
+            vr, vi = wr[l * 8 + k:l * 8 + k + 1, :], wi[l * 8 + k:l * 8 + k + 1, :]
             phasor[l, 0:SUBG, at] = (lr * vr + li * vi).astype(BF)
             phasor[l, SUBG:, at] = (lr * vi - li * vr).astype(BF)
+    sums = []
+    for l in range(2):
         product = lax.dot_general(
             phasor[l], basis[l], (((1,), (1,)), ((), ())), preferred_element_type=F32
         )
         sums.append(product[:SUBG] * sign + roll(product[SUBG:], SUBG))
     corrected_ref[...] = jnp.concatenate(sums, 0).astype(BF)
-    back = jnp.concatenate([returned[0][0], returned[0][1], returned[1][0], returned[1][1]], 0)
+    back = jnp.concatenate([wr, wi], 0)
     back = [part.astype(F32) for part in split3(back)]
     back_ref[...] = jnp.concatenate(back + [jnp.zeros((2 * SLOT, LANES), F32)], 0)
 
@@ -385,7 +387,7 @@
     turned = roll(x, SUBG) * -lane_sign(LANES, SUBG)
     cols = []
     for t in range(2):
-        rc, rs = rho_ref[pair, t, 0], rho_ref[pair, t, 1]
+        rc, rs = rho_ref[t, 0], rho_ref[t, 1]
         cols.append(
             jnp.concatenate([(x * rc + turned * rs).astype(BF), (x * rs - turned * rc).astype(BF)], 0)
         )
@@ -422,7 +424,7 @@
 
 
 def facet_kernel(
-    got_ref, meta_ref, coarse_ref, tw_ref, col_ref, out_hbm, res_hbm, flat, turned, out_ref, res_ref, sems,
+    got_ref, meta_ref, coarse_ref, tw_ref, col_ref, out_hbm, res_hbm, flat, spread, z_ref, turned, out_ref, res_ref, sems,
 ):
     flat[...] = got_ref[...].astype(F32)
     n = 2 * SLOT
@@ -441,16 +443,12 @@
 
     sign = -lane_sign(NQ, SUBG)
     low = quarter_low((NQ, LANES))
-    group = 4
-    for base in range(0, RD, group):
-        h = base // NR2
-        if base % NR2 == 0:
-            lane1 = iota((NQ, LANES), 1)
-            freq = iota((NQ, LANES), 0) * (N_IMG // NQ) + ((lane1 & (SUBG - 1)) ^ (h * HALF))
-            ph_c, ph_s = phase_of(meta_ref[2:3, :LANES], freq)
+    for h in range(2):
+        lane1 = iota((NQ, LANES), 1)
+        freq = iota((NQ, LANES), 0) * (N_IMG // NQ) + ((lane1 & (SUBG - 1)) ^ (h * HALF))
+        ph_c, ph_s = phase_of(meta_ref[2:3, :LANES], freq)
         images = []
-        for i in range(group):
-            row = (base + i) % NR2
+        for row in range(NR2):
             x = [
                 flat[pl.ds(c * MSG + row, NQ, stride=2 * MSG), :]
                 + flat[pl.ds((2 * NQ + c) * MSG + row, NQ, stride=2 * MSG), :]
@@ -461,38 +459,34 @@
             images.append(
                 jnp.concatenate([image * ph_c + turn * ph_s, turn * ph_c - image * ph_s], 0).astype(BF)
             )
-        spread = jnp.dot(coarse_ref[...], jnp.concatenate(images, 1), preferred_element_type=F32)
+        spread[h] = jnp.dot(coarse_ref[...], jnp.concatenate(images, 1), preferred_element_type=F32)
+    for h in range(2):
         tw_c, tw_s = tw_ref[2 * h], tw_ref[2 * h + 1]
-        stacked = []
-        for i in range(group):
-            at = slice(i * LANES, (i + 1) * LANES)
-            stacked.append((tw_c * spread[:LANES, at] + tw_s * spread[LANES:, at]).astype(BF))
+        for row in range(NR2):
+            at = slice(row * LANES, (row + 1) * LANES)
+            z_ref[h, at, :] = (tw_c * spread[h, :LANES, at] + tw_s * spread[h, LANES:, at]).astype(BF)
         out = lax.dot_general(
-            col_ref[h * LANES:(h + 1) * LANES], jnp.concatenate(stacked, 0), (((1,), (1,)), ((), ())),
+            col_ref[h * LANES:(h + 1) * LANES], z_ref[h], (((1,), (1,)), ((), ())),
             preferred_element_type=F32,
         )
-        for i in range(group):
-            r = base + i
-            for part in range(2):
-                at = (part * 2 + r // 8) * NA * 8 + r % 8
-                turned[pl.ds(at, NA, stride=8), :] = out[
-                    part * NA:(part + 1) * NA, i * LANES:(i + 1) * LANES
+        for part in range(2):
+            for row in range(NR2):
+                turned[h, part, pl.ds(row, NA, stride=NR2), :] = out[
+                    part * NA:(part + 1) * NA, row * LANES:(row + 1) * LANES
                 ]
-        if (base + group) % 8 == 0:
-            half = base // 8
-            for part in range(2):
-                where = slice(half * 8, half * 8 + 8)
-                for piece in range(2):
-                    for a in range(piece * NA // 2, (piece + 1) * NA // 2):
-                        at = ((part * 2 + half) * NA + a) * 8
-                        out_ref[part, where, a * LANES:(a + 1) * LANES] = turned[at:at + 8, :]
-                    wide = slice(piece * NA // 2 * LANES, (piece + 1) * NA // 2 * LANES)
-                    copy = pltpu.make_async_copy(
-                        out_ref.at[part, where, wide], out_hbm.at[0, part, where, wide],
-                        sems.at[(half * 2 + part) * 2 + piece],
-                    )
-                    copy.start()
-                    copies.append(copy)
+            where = slice(h * NR2, (h + 1) * NR2)
+            for piece in range(2):
+                for a in range(piece * NA // 2, (piece + 1) * NA // 2):
+                    out_ref[part, where, a * LANES:(a + 1) * LANES] = turned[
+                        h, part, a * NR2:(a + 1) * NR2, :
+                    ]
+                wide = slice(piece * NA // 2 * LANES, (piece + 1) * NA // 2 * LANES)
+                copy = pltpu.make_async_copy(
+                    out_ref.at[part, where, wide], out_hbm.at[0, part, where, wide],
+                    sems.at[(h * 2 + part) * 2 + piece],
+                )
+                copy.start()
+                copies.append(copy)
     for copy in copies:
         copy.wait()
 
@@ -523,6 +517,7 @@
     fwd_table = shape((2, 4 * SUBG, NQ * RD), BF)
     adj_table = shape((2, NQ * RD, 4 * SUBG), BF)
     square = shape((LANES, LANES), BF)
+    phases = shape((2, 2, LANES, LANES), F32)
     flat = pltpu.VMEM((NDEV * MSG, LANES), F32)
 
     def call(kernel, name, inputs, outs, scratch, in_specs=None, out_specs=None, flops=1 << 20):
@@ -549,24 +544,25 @@
         + [
             pltpu.VMEM((2, NA * RD, LANES), F32),
             flat,
+            pltpu.VMEM((LANES, RD * LANES), F32),
+            pltpu.VMEM((NR2 * LANES, 2 * LANES), BF),
             pltpu.SemaphoreType.DMA((len(inputs) + 2,)),
         ],
         in_specs=[HBM] * (len(inputs) + 2),
     )
     got = exchange(sent)
-    give, rhs, rho, raw = call(
+    give, rhs, other_rho, raw = call(
         rows_kernel, "rows", (got, fwd),
         (
-            square, shape((NQ * RD, 2 * LANES), BF), shape((2, 2, 2, LANES, LANES), F32),
-            shape((2, NDEV, LANES), F32),
+            square, shape((NQ * RD, 2 * LANES), BF), phases, shape((2, NDEV, LANES), F32),
         ),
         [flat],
     )
     other = other_core(give)
-    keep, vis, left, basis = call(
-        tables_kernel, "tables", (raw, fwd, rhs, rho),
+    keep, vis, rho, left, basis = call(
+        tables_kernel, "tables", (raw, fwd, rhs),
         (
-            square, shape((5 * SLOT, LANES), F32), shape((2, 2 * SUBG, NV), F32),
+            square, shape((5 * SLOT, LANES), F32), phases, shape((2, 2 * SUBG, NV), F32),
             shape((2, 2 * SUBG, NV), BF),
         ),
         [pltpu.VMEM((4, 4, SUBG, LANES), F32)],
@@ -580,14 +576,16 @@
     (part,) = call(
         mine_kernel, "mine", (corrected, rho, adj), (shape((NQ * RD, 2 * LANES), F32),), []
     )
-    (answer,) = call(images_kernel, "images", (part, other, back, rho, adj), (message,), [flat])
+    (answer,) = call(images_kernel, "images", (part, other, back, other_rho, adj), (message,), [flat])
     facet_adjoint, residual = call(
         facet_kernel, "facet",
         (exchange(answer), meta, t["coarse_adj"], t["tw_adj"], t["col_adj"]),
         (shape((1, 2, RD, NA * LANES), F32), shape((2, NV), F32)),
         [
             flat,
-            pltpu.VMEM((4 * NA * 8, LANES), F32),
+            pltpu.VMEM((2, 2 * LANES, NR2 * LANES), F32),
+            pltpu.VMEM((2, NR2 * LANES, LANES), BF),
+            pltpu.VMEM((2, 2, NA * NR2, LANES), F32),
             pltpu.VMEM((2, RD, NA * LANES), F32),
             pltpu.VMEM((2, NV), F32),
             pltpu.SemaphoreType.DMA((9,)),

time: 49.7 us -> 48.8 us (0.982)
  Pallas kernels: 8.72 us -> 8.02 us
    pallas_call x7, Pallas kernels: 8.72 us -> 8.02 us  [call(): pl.pallas_call(kernel, out_shape=outs, in_specs=in_specs or [VMEM] * len(...]
  transfers between devices with their start and end apart: 2 -> 2, of which waited for: 2 -> 1; matrix products, arithmetic and copies ran while one was open for 0% -> 0% of each run, Pallas kernels for 2% -> 3%
where the time goes in v5:
time: 48.8 us; the launch traced here: 48.7 us
  blocking collectives  37.8 us (77%)
  Pallas kernels  8.02 us (16%)
  starting transfers between devices  1.5 us (3%)
  between operations  0.71 us (1%)
  waiting for transfers between devices  0.61 us (1%)
    all_to_all x2, blocking collectives, exchange(): lax.all_to_all(pairs, ALL, split_axis=0, concat_axis=0, tiled=True)  37.8 us
    pallas_call x7, Pallas kernels, call(): pl.pallas_call(kernel, out_shape=outs, in_specs=in_specs or [VMEM] * len(...  8.02 us
    ppermute x2, starting transfers between devices, other_core(): return lax.ppermute(x, 'sub', [(i, i ^ 1) for i in range(NQ)])  1.5 us
  transfers between devices with their start and end apart: 2, of which 1 were waited for; matrix products, arithmetic and copies ran while one was open for 0% of the time, Pallas kernels for 3%

profile of v5, /device:TPU:1, one launch (start us, length us, event | category | flops | bytes accessed | tf_op | source)
XLA Modules:
  0.0 48.7 jit_solution(5176053317576419702)
XLA Ops:
  0.6 2.8 %send.1 = (bf16[1280,128]{1,0:T(8,128)(2,1)S(1)}, s32[8,1024]{1,0:T(8,128)S(1)}, bf16[2,256,512]{2,1,0:T(8,128)(2,1)S(1)}, bf16[2,512,256]{2,1,0:T(8,128)(2,1)S(1)}) custom-call(s32[1,2]{1,0:T(1,128)} %off_hbm.1, bf16[1,2,16,8192]{3,2,1,0:T(8,128)(2,1)} %slab_hbm.1, f32[2,1024]{1,0:T(2,128)} %pos_hbm.1, f32[2,1024]{1,0:T(2,128)} %obs_hbm.1, ...), custom_call_target="tpu_custom_call" | custom-call | flops 1048576 | bytes 2097152 | tf_op jit(solution)/shard_map/send/pallas_call | solution.py:524
  3.4 22.7 %all_to_all.10 = bf16[640,2,128]{2,1,0:T(2,128)(2,1)S(1)} all-to-all(bf16[640,2,128]{2,1,0:T(2,128)(2,1)S(1)} %bitcast.9), channel_id=1, replica_groups=mesh['facet'=4,'sub'=32] {'facet','sub'}, dimensions={0} | all-to-all | bytes 655360 | tf_op jit(solution)/shard_map/all_to_all | solution.py:505
  26.1 0.6 %rows.1 = (bf16[128,128]{1,0:T(8,128)(2,1)S(1)}, bf16[512,256]{1,0:T(8,128)(2,1)S(1)}, f32[2,2,128,128]{3,2,1,0:T(8,128)S(1)}, f32[2,128,128]{2,1,0:T(8,128)S(1)}) custom-call(bf16[1280,128]{1,0:T(8,128)(2,1)S(1)} %bitcast.7, bf16[2,256,512]{2,1,0:T(8,128)(2,1)S(1)} %get-tuple-element.18.fwd_ref), custom_call_target="tpu_custom_call" | custom-call | flops 1048576 | bytes 2097152 | tf_op jit(solution)/shard_map/rows/pallas_call | solution.py:524
  26.7 1.2 %collective-permute-start = (bf16[128,128]{1,0:T(8,128)(2,1)S(1)}, bf16[128,128]{1,0:T(8,128)(2,1)S(1)}, u32[]{:S(2)}, u32[]{:S(2)}) collective-permute-start(bf16[128,128]{1,0:T(8,128)(2,1)S(1)} %get-tuple-element.22), channel_id=1, source_target_pairs={{0,1},{1,0},{2,3},{3,2},{4,5},{5,4},{6,7},{7,6},{8,9},{9,8},{10,11... | collective-permute-start | bytes 98312 | tf_op jit(solution)/shard_map/ppermute | solution.py:509
  27.9 0.9 %tables.1 = (bf16[128,128]{1,0:T(8,128)(2,1)S(1)}, f32[80,128]{1,0:T(8,128)S(1)}, f32[2,2,128,128]{3,2,1,0:T(8,128)S(1)}, f32[2,128,1024]{2,1,0:T(8,128)S(1)}, bf16[2,128,1024]{2,1,0:T(8,128)(2,1)S(1)}) custom-call(f32[2,128,128]{2,1,0:T(8,128)S(1)} %get-tuple-element.19.raw_ref, bf16[2,256,512]{2,1,0:T(8,128)(2,1)S(1)} %get-tuple-element.18.fwd_ref, ...), custom_call_target="tpu_custom_call" | custom-call | flops 1048576 | bytes 2097152 | tf_op jit(solution)/shard_map/tables/pallas_call | solution.py:524
  28.9 0.0 collective-permute-done.other_ref
  28.9 1.0 %visibilities.1 = (bf16[128,128]{1,0:T(8,128)(2,1)S(1)}, f32[128,128]{1,0:T(8,128)S(1)}) custom-call(bf16[128,128]{1,0:T(8,128)(2,1)S(1)} %get-tuple-element.21.keep_ref, bf16[128,128]{1,0:T(8,128)(2,1)S(1)} %collective-permute-done.other_ref, f32[80,128]{1,0:T(8,128)S(1)} %get-tuple-element.23.vis_ref, f32[2,128,1024]{2,1,0:T(8,128)S(1)} %get-tuple-element.24.left, ...), custom_call_target="tpu_custom_call" | custom-call | flops 1048576 | bytes 2097152 | tf_op jit(solution)/shard_map/visibilities/pallas_call | solution.py:524
  29.9 0.3 collective-permute-start.1
  30.2 0.4 mine.1.part_ref
  30.6 0.6 %collective-permute-done.1.other_ref = bf16[128,128]{1,0:T(8,128)(2,1)S(1)} collective-permute-done((bf16[128,128]{1,0:T(8,128)(2,1)S(1)}, bf16[128,128]{1,0:T(8,128)(2,1)S(1)}, u32[]{:S(2)}, u32[]{:S(2)}) %collective-permute-start.1) | collective-permute-done | bytes 32800 | tf_op jit(solution)/shard_map/ppermute | solution.py:509
  31.2 0.6 %images.1 = bf16[1280,128]{1,0:T(8,128)(2,1)S(1)} custom-call(f32[512,256]{1,0:T(8,128)S(1)} %mine.1.part_ref, bf16[128,128]{1,0:T(8,128)(2,1)S(1)} %collective-permute-done.1.other_ref, f32[128,128]{1,0:T(8,128)S(1)} %get-tuple-element.29.back_ref, f32[2,2,128,128]{3,2,1,0:T(8,128)S(1)} %get-tuple-element.30.rho_ref, ...), custom_call_target="tpu_custom_call" | custom-call | flops 1048576 | bytes 2097152 | tf_op jit(solution)/shard_map/images/pallas_call | solution.py:524
  31.8 0.0 copy-start
  31.8 0.0 copy-start.1
  31.8 0.0 copy-start.2
  31.8 15.1 %all_to_all.11 = bf16[640,2,128]{2,1,0:T(2,128)(2,1)S(1)} all-to-all(bf16[640,2,128]{2,1,0:T(2,128)(2,1)S(1)} %bitcast.8), channel_id=1, replica_groups=mesh['facet'=4,'sub'=32] {'facet','sub'}, dimensions={0} | all-to-all | bytes 655360 | tf_op jit(solution)/shard_map/all_to_all | solution.py:505
  46.9 0.0 copy-done
  46.9 0.0 copy-done.1
  46.9 0.0 copy-done.2
  46.9 1.7 %facet.1 = (f32[1,2,16,8192]{3,2,1,0:T(8,128)}, f32[2,1024]{1,0:T(2,128)}) custom-call(bf16[1280,128]{1,0:T(8,128)(2,1)S(1)} %bitcast.6, s32[8,1024]{1,0:T(8,128)S(1)} %get-tuple-element.31.meta_ref, bf16[256,64]{1,0:T(8,128)(2,1)S(1)} %copy-done.1, f32[4,128,128]{2,1,0:T(8,128)S(1)} %copy-done, bf16[256,128]{1,0:T(8,128)(2,1)S(1)} %copy-done.2), custom_call_target="tpu_custom_call" | custom-call | flops 1048576 | bytes 2097152 | tf_op jit(solution)/shard_map/facet/pallas_call | solution.py:524
Async XLA Ops:
  26.7 2.1 %collective-permute-start = (bf16[128,128]{1,0:T(8,128)(2,1)S(1)}, bf16[128,128]{1,0:T(8,128)(2,1)S(1)}, u32[]{:S(2)}, u32[]{:S(2)}) collective-permute-start(bf16[128,128]{1,0:T(8,128)(2,1)S(1)} %get-tuple-element.22), channel_id=1, source_target_pairs={{0,1},{1,0},{2,3},{3,2},{4,5},{5,4},{6,7},{7,6},{8,9},{9,8},{10,11... | collective-permute-start | bytes 98312 | tf_op jit(solution)/shard_map/ppermute | solution.py:509
  29.9 1.3 %collective-permute-start.1 = (bf16[128,128]{1,0:T(8,128)(2,1)S(1)}, bf16[128,128]{1,0:T(8,128)(2,1)S(1)}, u32[]{:S(2)}, u32[]{:S(2)}) collective-permute-start(bf16[128,128]{1,0:T(8,128)(2,1)S(1)} %get-tuple-element.26.corrected_ref), channel_id=1, source_target_pairs={{0,1},{1,0},{2,3},{3,2},{4,5},{5,4},{6,7},{7,6},{8,9},{9,8},{10,11... | collective-permute-start | bytes 98312 | tf_op jit(solution)/shard_map/ppermute | solution.py:509
  31.8 15.2 %copy-start = (f32[4,128,128]{2,1,0:T(8,128)S(1)}, f32[4,128,128]{2,1,0:T(8,128)}, u32[]{:S(2)}) copy-start(f32[4,128,128]{2,1,0:T(8,128)} %constant.17.clone.tw_ref) | copy-start | bytes 786436
  31.8 15.1 %copy-start.1 = (bf16[256,64]{1,0:T(8,128)(2,1)S(1)}, bf16[256,64]{1,0:T(8,128)(2,1)}, u32[]{:S(2)}) copy-start(bf16[256,64]{1,0:T(8,128)(2,1)} %constant.18.clone.coarse_ref) | copy-start | bytes 98308
  31.8 15.1 %copy-start.2 = (bf16[256,128]{1,0:T(8,128)(2,1)S(1)}, bf16[256,128]{1,0:T(8,128)(2,1)}, u32[]{:S(2)}) copy-start(bf16[256,128]{1,0:T(8,128)(2,1)} %constant.15.clone.col_ref) | copy-start | bytes 196612

commit v6 on v5

--- a/solution.py
+++ b/solution.py
@@ -114,12 +114,12 @@
 
 
 def send_kernel(
-    off_hbm, slab_hbm, pos_hbm, obs_hbm, ids_hbm, clip_hbm, table_hbm, tw_hbm, fwd_hbm, adj_hbm,
-    msg_ref, meta_ref, fwd_ref, adj_ref, off_ref, slab_ref, pos_ref, obs_ref, ids_ref, clip_ref, table_ref, tw_ref,
+    off_hbm, slab_hbm, pos_hbm, obs_hbm, ids_hbm, ids8_hbm, clip_hbm, table_hbm, tw_hbm, fwd_hbm, adj_hbm,
+    msg_ref, meta_ref, fwd_ref, adj_ref, off_ref, slab_ref, pos_ref, obs_ref, ids_ref, ids8_ref, clip_ref, table_ref, tw_ref,
     wide, flat, y_ref, z_ref, sems,
 ):
     pairs = [
-        (ids_hbm, ids_ref), (clip_hbm, clip_ref), (pos_hbm, pos_ref), (obs_hbm, obs_ref),
+        (ids_hbm, ids_ref), (ids8_hbm, ids8_ref), (clip_hbm, clip_ref), (pos_hbm, pos_ref), (obs_hbm, obs_ref),
         (off_hbm, off_ref), (slab_hbm, slab_ref), (table_hbm, table_ref), (tw_hbm, tw_ref),
     ]
     copies = [pltpu.make_async_copy(a, b, sems.at[i]) for i, (a, b) in enumerate(pairs)]
@@ -132,40 +132,56 @@
         copy.start()
 
     copies[0].wait()
+    copies[1].wait()
     ids = ids_ref[...]
-    upper = jnp.where(iota((LANES, LANES), 0) < iota((LANES, LANES), 1), 1.0, 0.0).astype(BF)
-    counter = jnp.concatenate([upper, jnp.ones((LANES, LANES), BF)], 1)
-    before = jnp.zeros((2 * LANES, LANES), F32)
+    n_tile = NV // LANES
+    column = ids8_ref[...].astype(F32).T
+    row_ids = ids.astype(F32).astype(BF)
+    zero, one = jnp.zeros((), BF), jnp.ones((), BF)
+    above = iota((LANES, LANES), 0) < iota((LANES, LANES), 1)
+    above = jnp.where(above, 1.0, 0.0).astype(BF)
+    counts = [None] * n_tile
+    for b in range(n_tile):
+        mine = jnp.broadcast_to(column[:, b:b + 1], (LANES, LANES)).astype(BF)
+        for c in range(b, n_tile):
+            other = jnp.broadcast_to(row_ids[:, c * LANES:(c + 1) * LANES], (LANES, LANES))
+            same = jnp.where(mine == other, above if b == c else one, zero)
+            counts[c] = same if b == 0 else counts[c] + same
     ranks = []
-    for b in range(NV // LANES):
-        hot = iota((2 * LANES, LANES), 0) == ids[:, b * LANES:(b + 1) * LANES]
-        hot_f = jnp.where(hot, 1.0, 0.0)
-        count = jnp.dot(hot_f.astype(BF), counter, preferred_element_type=F32)
-        ranks.append(jnp.sum(hot_f * (count[:, :LANES] + before), 0, keepdims=True))
-        before = before + count[:, LANES:]
+    for c in range(n_tile):
+        part = counts[c]
+        while part.shape[0] > 16:
+            half = part.shape[0] // 2
+            part = part[:half] + part[half:]
+        ranks.append(jnp.sum(part.astype(F32), 0, keepdims=True))
     rank = jnp.concatenate(ranks, 1).astype(jnp.int32)
     owner = (ids >> 7) * (2 * NQ) + (ids & (NQ - 1)) * 2 + ((ids >> 6) & 1)
     place = ((ids >> 5) & 1) * 8 + rank
     meta_ref[0:1, :] = owner
     meta_ref[1:2, :] = place
-    here = iota((SLOT, NV), 0) == place
-    copies[1].wait()
+    here = iota((SLOT, NV), 0).astype(F32).astype(BF) == place.astype(F32).astype(BF)
+    copies[2].wait()
     n_block = NV // VIS_BLOCK
     clip = jnp.broadcast_to(clip_ref[...].astype(F32) * 0.25, (n_block, n_block))
     same = iota((n_block, n_block), 0) == iota((n_block, n_block), 1)
     clip = jnp.sum(jnp.where(same, clip, 0.0), 1, keepdims=True)
     block = iota((n_block, NV), 1) // VIS_BLOCK == iota((n_block, NV), 0)
     level = jnp.sum(jnp.where(block, clip, 0.0), 0, keepdims=True)
-    copies[2].wait()
     copies[3].wait()
+    copies[4].wait()
     values = [pos_ref[0:1, :], pos_ref[1:2, :], obs_ref[0:1, :], obs_ref[1:2, :], level]
     pieces = [split3(v) for v in values]
-    own = jnp.where(iota((NDEV, NV), 0) == owner, 1.0, 0.0).astype(BF)
+    own = jnp.where(
+        iota((NDEV, NV), 0).astype(F32).astype(BF) == owner.astype(F32).astype(BF), one, zero
+    )
     table = jnp.concatenate(
-        [jnp.where(here, p[part].astype(F32), 0.0).astype(BF) for part in range(3) for p in pieces]
+        [
+            jnp.where(here, jnp.broadcast_to(p[part], (SLOT, NV)), zero)
+            for part in range(3) for p in pieces
+        ]
         + [jnp.zeros((SLOT, NV), BF)], 0
     )
-    copies[4].wait()
+    copies[5].wait()
     meta_ref[2:3, :] = jnp.full((1, NV), off_ref[0, 1], jnp.int32)
     payload = lax.dot_general(own, table, (((1,), (1,)), ((), ())), preferred_element_type=F32)
     lane = iota((NDEV, LANES), 1)
@@ -178,7 +194,7 @@
     lane1 = iota((NQ, LANES), 1)
     freq = iota((NQ, LANES), 0) * (N_IMG // NQ) + (lane1 & (HALF - 1)) + lane1 // SUBG * HALF
     ph_c, ph_s = phase_of(off_ref[0, 1], freq)
-    for copy in copies[5:]:
+    for copy in copies[6:]:
         copy.wait()
     for part in range(2):
         for a in range(NA):
@@ -254,12 +270,16 @@
         jnp.where(eight < 4, starts[0], starts[1]), (first + (eight & 1)) * (N_IMG // 8)
     )
     for t in range(2):
-        fine_c, fine_s = phase_of(starts[t], iota((SUBG, LANES), 0))
+        low_c, low_s = phase_of(starts[t], eight)
+        high_c, high_s = phase_of(starts[t], eight * 8)
         for p in range(2):
             tc, ts = turn_c[t * 4 + p:t * 4 + p + 1], turn_s[t * 4 + p:t * 4 + p + 1]
-            at = slice(p * SUBG, (p + 1) * SUBG)
-            rho_ref[t, 0, at, :] = fine_c * tc - fine_s * ts
-            rho_ref[t, 1, at, :] = fine_s * tc + fine_c * ts
+            hc, hs = high_c * tc - high_s * ts, high_s * tc + high_c * ts
+            for a in range(8):
+                at = slice(p * SUBG + a * 8, p * SUBG + a * 8 + 8)
+                ac, asin = hc[a:a + 1], hs[a:a + 1]
+                rho_ref[t, 0, at, :] = low_c * ac - low_s * asin
+                rho_ref[t, 1, at, :] = low_s * ac + low_c * asin
 
 
 def rows_kernel(got_ref, fwd_ref, give_ref, rhs_ref, rho_ref, raw_ref, flat):
@@ -374,9 +394,7 @@
         )
         sums.append(product[:SUBG] * sign + roll(product[SUBG:], SUBG))
     corrected_ref[...] = jnp.concatenate(sums, 0).astype(BF)
-    back = jnp.concatenate([wr, wi], 0)
-    back = [part.astype(F32) for part in split3(back)]
-    back_ref[...] = jnp.concatenate(back + [jnp.zeros((2 * SLOT, LANES), F32)], 0)
+    back_ref[...] = jnp.concatenate([wr, wi], 0)
 
 
 def partial_images(x, pair, rho_ref, adj_ref):
@@ -401,11 +419,13 @@
     return jnp.dot(table, jnp.concatenate(cols, 1), preferred_element_type=F32)
 
 
-def mine_kernel(corrected_ref, rho_ref, adj_ref, part_ref):
+def mine_kernel(corrected_ref, back_ref, rho_ref, adj_ref, part_ref, tail_ref):
+    back = [part.astype(F32) for part in split3(back_ref[...])]
+    tail_ref[...] = jnp.concatenate(back + [jnp.zeros((2 * SLOT, LANES), F32)], 0).T
     part_ref[...] = partial_images(corrected_ref[...], lax.axis_index("sub") & 1, rho_ref, adj_ref)
 
 
-def images_kernel(part_ref, other_ref, back_ref, rho_ref, adj_ref, msg_ref, flat):
+def images_kernel(part_ref, other_ref, tail_ref, rho_ref, adj_ref, msg_ref, flat):
     pair = 1 - (lax.axis_index("sub") & 1)
     images = part_ref[...] + partial_images(other_ref[...], pair, rho_ref, adj_ref)
     low = quarter_low((NQ, LANES))
@@ -418,7 +438,7 @@
             flat[pl.ds((2 * t + 1) * NQ * MSG + row, NQ, stride=MSG), :] = jnp.where(
                 low, roll(a, LANES - HALF), b
             )
-    flat[pl.ds(NR2, NDEV, stride=MSG), :] = back_ref[...].T
+    flat[pl.ds(NR2, NDEV, stride=MSG), :] = tail_ref[...]
     flat[pl.ds(NR2 + 1, NDEV, stride=MSG), :] = jnp.zeros((NDEV, LANES), F32)
     msg_ref[...] = flat[...].astype(BF)
 
@@ -533,7 +553,7 @@
         )(*inputs)
 
     inputs = (
-        offsets, slab, position, observed, subgrid_of.reshape(1, NV),
+        offsets, slab, position, observed, subgrid_of.reshape(1, NV), subgrid_of.reshape(8, LANES),
         clip.reshape(1, NV // VIS_BLOCK), t["column"], t["tw_fwd"],
     )
     sent, meta, fwd, adj = call(
@@ -569,14 +589,15 @@
     )
     corrected, back = call(
         visibility_kernel, "visibilities", (keep, other, vis, left, basis),
-        (square, shape((LANES, LANES), F32)),
+        (square, shape((2 * SLOT, LANES), F32)),
         [pltpu.VMEM((2, 2 * SUBG, NV), F32), pltpu.VMEM((2, 2 * SUBG, NV), BF)],
     )
     other = other_core(corrected)
-    (part,) = call(
-        mine_kernel, "mine", (corrected, rho, adj), (shape((NQ * RD, 2 * LANES), F32),), []
-    )
-    (answer,) = call(images_kernel, "images", (part, other, back, other_rho, adj), (message,), [flat])
+    part, tail = call(
+        mine_kernel, "mine", (corrected, back, rho, adj),
+        (shape((NQ * RD, 2 * LANES), F32), shape((LANES, LANES), F32)), [],
+    )
+    (answer,) = call(images_kernel, "images", (part, other, tail, other_rho, adj), (message,), [flat])
     facet_adjoint, residual = call(
         facet_kernel, "facet",
         (exchange(answer), meta, t["coarse_adj"], t["tw_adj"], t["col_adj"]),

time: 48.8 us -> 48.6 us (level)
  no operation moved by 1% of the time
where the time goes in v6:
time: 48.6 us; the launch traced here: 48.4 us
  blocking collectives  37.9 us (78%)
  Pallas kernels  7.71 us (16%)
  starting transfers between devices  1.57 us (3%)
  between operations  0.71 us (1%)
  waiting for transfers between devices  0.53 us (1%)
    all_to_all x2, blocking collectives, exchange(): lax.all_to_all(pairs, ALL, split_axis=0, concat_axis=0, tiled=True)  37.9 us
    pallas_call x7, Pallas kernels, call(): pl.pallas_call(kernel, out_shape=outs, in_specs=in_specs or [VMEM] * len(...  7.71 us
    ppermute x2, starting transfers between devices, other_core(): return lax.ppermute(x, 'sub', [(i, i ^ 1) for i in range(NQ)])  1.57 us
  transfers between devices with their start and end apart: 2, of which 1 were waited for; matrix products, arithmetic and copies ran while one was open for 0% of the time, Pallas kernels for 3%

profile of v6, /device:TPU:1, one launch (start us, length us, event | category | flops | bytes accessed | tf_op | source)
XLA Modules:
  0.0 48.4 jit_solution(16454227029933608693)
XLA Ops:
  0.6 2.7 %send.1 = (bf16[1280,128]{1,0:T(8,128)(2,1)S(1)}, s32[8,1024]{1,0:T(8,128)S(1)}, bf16[2,256,512]{2,1,0:T(8,128)(2,1)S(1)}, bf16[2,512,256]{2,1,0:T(8,128)(2,1)S(1)}) custom-call(s32[1,2]{1,0:T(1,128)} %off_hbm.1, bf16[1,2,16,8192]{3,2,1,0:T(8,128)(2,1)} %slab_hbm.1, f32[2,1024]{1,0:T(2,128)} %pos_hbm.1, f32[2,1024]{1,0:T(2,128)} %obs_hbm.1, ...), custom_call_target="tpu_custom_call" | custom-call | flops 1048576 | bytes 2097152 | tf_op jit(solution)/shard_map/send/pallas_call | solution.py:544
  3.3 22.7 %all_to_all.10 = bf16[640,2,128]{2,1,0:T(2,128)(2,1)S(1)} all-to-all(bf16[640,2,128]{2,1,0:T(2,128)(2,1)S(1)} %bitcast.10), channel_id=1, replica_groups=mesh['facet'=4,'sub'=32] {'facet','sub'}, dimensions={0} | all-to-all | bytes 655360 | tf_op jit(solution)/shard_map/all_to_all | solution.py:525
  26.0 0.6 %rows.1 = (bf16[128,128]{1,0:T(8,128)(2,1)S(1)}, bf16[512,256]{1,0:T(8,128)(2,1)S(1)}, f32[2,2,128,128]{3,2,1,0:T(8,128)S(1)}, f32[2,128,128]{2,1,0:T(8,128)S(1)}) custom-call(bf16[1280,128]{1,0:T(8,128)(2,1)S(1)} %bitcast.8, bf16[2,256,512]{2,1,0:T(8,128)(2,1)S(1)} %get-tuple-element.20.fwd_ref), custom_call_target="tpu_custom_call" | custom-call | flops 1048576 | bytes 2097152 | tf_op jit(solution)/shard_map/rows/pallas_call | solution.py:544
  26.5 1.2 %collective-permute-start = (bf16[128,128]{1,0:T(8,128)(2,1)S(1)}, bf16[128,128]{1,0:T(8,128)(2,1)S(1)}, u32[]{:S(2)}, u32[]{:S(2)}) collective-permute-start(bf16[128,128]{1,0:T(8,128)(2,1)S(1)} %get-tuple-element.24), channel_id=1, source_target_pairs={{0,1},{1,0},{2,3},{3,2},{4,5},{5,4},{6,7},{7,6},{8,9},{9,8},{10,11... | collective-permute-start | bytes 98312 | tf_op jit(solution)/shard_map/ppermute | solution.py:529
  27.7 0.9 %tables.1 = (bf16[128,128]{1,0:T(8,128)(2,1)S(1)}, f32[80,128]{1,0:T(8,128)S(1)}, f32[2,2,128,128]{3,2,1,0:T(8,128)S(1)}, f32[2,128,1024]{2,1,0:T(8,128)S(1)}, bf16[2,128,1024]{2,1,0:T(8,128)(2,1)S(1)}) custom-call(f32[2,128,128]{2,1,0:T(8,128)S(1)} %get-tuple-element.21.raw_ref, bf16[2,256,512]{2,1,0:T(8,128)(2,1)S(1)} %get-tuple-element.20.fwd_ref, ...), custom_call_target="tpu_custom_call" | custom-call | flops 1048576 | bytes 2097152 | tf_op jit(solution)/shard_map/tables/pallas_call | solution.py:544
  28.6 0.0 collective-permute-done.other_ref
  28.6 1.0 %visibilities.1 = (bf16[128,128]{1,0:T(8,128)(2,1)S(1)}, f32[32,128]{1,0:T(8,128)S(1)}) custom-call(bf16[128,128]{1,0:T(8,128)(2,1)S(1)} %get-tuple-element.23.keep_ref, bf16[128,128]{1,0:T(8,128)(2,1)S(1)} %collective-permute-done.other_ref, f32[80,128]{1,0:T(8,128)S(1)} %get-tuple-element.25.vis_ref, f32[2,128,1024]{2,1,0:T(8,128)S(1)} %get-tuple-element.26.left, ...), custom_call_target="tpu_custom_call" | custom-call | flops 1048576 | bytes 2097152 | tf_op jit(solution)/shard_map/visibilities/pallas_call | solution.py:544
  29.6 0.4 collective-permute-start.1
  30.0 0.4 mine.1
  30.4 0.5 %collective-permute-done.1.other_ref = bf16[128,128]{1,0:T(8,128)(2,1)S(1)} collective-permute-done((bf16[128,128]{1,0:T(8,128)(2,1)S(1)}, bf16[128,128]{1,0:T(8,128)(2,1)S(1)}, u32[]{:S(2)}, u32[]{:S(2)}) %collective-permute-start.1) | collective-permute-done | bytes 32800 | tf_op jit(solution)/shard_map/ppermute | solution.py:529
  30.9 0.5 %images.1 = bf16[1280,128]{1,0:T(8,128)(2,1)S(1)} custom-call(f32[512,256]{1,0:T(8,128)S(1)} %get-tuple-element.32.part_ref, bf16[128,128]{1,0:T(8,128)(2,1)S(1)} %collective-permute-done.1.other_ref, f32[128,128]{1,0:T(8,128)S(1)} %get-tuple-element.33.tail_ref, f32[2,2,128,128]{3,2,1,0:T(8,128)S(1)} %get-tuple-element.34.rho_ref, ...), custom_call_target="tpu_custom_call" | custom-call | flops 1048576 | bytes 2097152 | tf_op jit(solution)/shard_map/images/pallas_call | solution.py:544
  31.4 0.0 copy-start
  31.5 0.0 copy-start.1
  31.5 0.0 copy-start.2
  31.5 15.2 %all_to_all.11 = bf16[640,2,128]{2,1,0:T(2,128)(2,1)S(1)} all-to-all(bf16[640,2,128]{2,1,0:T(2,128)(2,1)S(1)} %bitcast.9), channel_id=1, replica_groups=mesh['facet'=4,'sub'=32] {'facet','sub'}, dimensions={0} | all-to-all | bytes 655360 | tf_op jit(solution)/shard_map/all_to_all | solution.py:525
  46.7 0.0 copy-done
  46.7 0.0 copy-done.1
  46.7 0.0 copy-done.2
  46.7 1.7 %facet.1 = (f32[1,2,16,8192]{3,2,1,0:T(8,128)}, f32[2,1024]{1,0:T(2,128)}) custom-call(bf16[1280,128]{1,0:T(8,128)(2,1)S(1)} %bitcast.7, s32[8,1024]{1,0:T(8,128)S(1)} %get-tuple-element.35.meta_ref, bf16[256,64]{1,0:T(8,128)(2,1)S(1)} %copy-done.1, f32[4,128,128]{2,1,0:T(8,128)S(1)} %copy-done, bf16[256,128]{1,0:T(8,128)(2,1)S(1)} %copy-done.2), custom_call_target="tpu_custom_call" | custom-call | flops 1048576 | bytes 2097152 | tf_op jit(solution)/shard_map/facet/pallas_call | solution.py:544
Async XLA Ops:
  26.5 2.1 %collective-permute-start = (bf16[128,128]{1,0:T(8,128)(2,1)S(1)}, bf16[128,128]{1,0:T(8,128)(2,1)S(1)}, u32[]{:S(2)}, u32[]{:S(2)}) collective-permute-start(bf16[128,128]{1,0:T(8,128)(2,1)S(1)} %get-tuple-element.24), channel_id=1, source_target_pairs={{0,1},{1,0},{2,3},{3,2},{4,5},{5,4},{6,7},{7,6},{8,9},{9,8},{10,11... | collective-permute-start | bytes 98312 | tf_op jit(solution)/shard_map/ppermute | solution.py:529
  29.6 1.3 %collective-permute-start.1 = (bf16[128,128]{1,0:T(8,128)(2,1)S(1)}, bf16[128,128]{1,0:T(8,128)(2,1)S(1)}, u32[]{:S(2)}, u32[]{:S(2)}) collective-permute-start(bf16[128,128]{1,0:T(8,128)(2,1)S(1)} %get-tuple-element.28.corrected_ref), channel_id=1, source_target_pairs={{0,1},{1,0},{2,3},{3,2},{4,5},{5,4},{6,7},{7,6},{8,9},{9,8},{10,11... | collective-permute-start | bytes 98312 | tf_op jit(solution)/shard_map/ppermute | solution.py:529
  31.4 15.2 %copy-start = (f32[4,128,128]{2,1,0:T(8,128)S(1)}, f32[4,128,128]{2,1,0:T(8,128)}, u32[]{:S(2)}) copy-start(f32[4,128,128]{2,1,0:T(8,128)} %constant.17.clone.tw_ref) | copy-start | bytes 786436
  31.5 15.2 %copy-start.1 = (bf16[256,64]{1,0:T(8,128)(2,1)S(1)}, bf16[256,64]{1,0:T(8,128)(2,1)}, u32[]{:S(2)}) copy-start(bf16[256,64]{1,0:T(8,128)(2,1)} %constant.18.clone.coarse_ref) | copy-start | bytes 98308
  31.5 15.2 %copy-start.2 = (bf16[256,128]{1,0:T(8,128)(2,1)S(1)}, bf16[256,128]{1,0:T(8,128)(2,1)}, u32[]{:S(2)}) copy-start(bf16[256,128]{1,0:T(8,128)(2,1)} %constant.15.clone.col_ref) | copy-start | bytes 196612

commit v7 on v6

--- a/solution.py
+++ b/solution.py
@@ -447,20 +447,7 @@
     got_ref, meta_ref, coarse_ref, tw_ref, col_ref, out_hbm, res_hbm, flat, spread, z_ref, turned, out_ref, res_ref, sems,
 ):
     flat[...] = got_ref[...].astype(F32)
-    n = 2 * SLOT
-    back = flat[pl.ds(NR2, NDEV, stride=MSG), :].T[:3 * n]
-    owner, place = meta_ref[0:1, :], meta_ref[1:2, :]
-    own = jnp.where(iota((NDEV, NV), 0) == owner, 1.0, 0.0).astype(BF)
-    found = jnp.dot(back.astype(BF), own, preferred_element_type=F32)
-    found = found[:n] + found[n:2 * n] + found[2 * n:]
-    here = iota((SLOT, NV), 0) == place
-    for c in range(2):
-        res_ref[c:c + 1, :] = jnp.sum(
-            jnp.where(here, found[c * SLOT:(c + 1) * SLOT], 0.0), 0, keepdims=True
-        )
-    copies = [pltpu.make_async_copy(res_ref, res_hbm, sems.at[8])]
-    copies[0].start()
-
+    copies = []
     sign = -lane_sign(NQ, SUBG)
     low = quarter_low((NQ, LANES))
     for h in range(2):
@@ -507,6 +494,20 @@
                 )
                 copy.start()
                 copies.append(copy)
+    n = 2 * SLOT
+    back = flat[pl.ds(NR2, NDEV, stride=MSG), :].T[:3 * n]
+    owner, place = meta_ref[0:1, :], meta_ref[1:2, :]
+    own = jnp.where(iota((NDEV, NV), 0) == owner, 1.0, 0.0).astype(BF)
+    found = jnp.dot(back.astype(BF), own, preferred_element_type=F32)
+    found = found[:n] + found[n:2 * n] + found[2 * n:]
+    here = iota((SLOT, NV), 0) == place
+    for c in range(2):
+        res_ref[c:c + 1, :] = jnp.sum(
+            jnp.where(here, found[c * SLOT:(c + 1) * SLOT], 0.0), 0, keepdims=True
+        )
+    copies.append(pltpu.make_async_copy(res_ref, res_hbm, sems.at[8]))
+    copies[-1].start()
+
     for copy in copies:
         copy.wait()
 

time: 48.6 us -> 48.6 us (level)
  no operation moved by 1% of the time
where the time goes in v7:
time: 48.6 us; the launch traced here: 48.4 us
  blocking collectives  37.9 us (78%)
  Pallas kernels  7.7 us (16%)
  starting transfers between devices  1.57 us (3%)
  between operations  0.71 us (1%)
  waiting for transfers between devices  0.53 us (1%)
    all_to_all x2, blocking collectives, exchange(): lax.all_to_all(pairs, ALL, split_axis=0, concat_axis=0, tiled=True)  37.9 us
    pallas_call x7, Pallas kernels, call(): pl.pallas_call(kernel, out_shape=outs, in_specs=in_specs or [VMEM] * len(...  7.7 us
    ppermute x2, starting transfers between devices, other_core(): return lax.ppermute(x, 'sub', [(i, i ^ 1) for i in range(NQ)])  1.57 us
  transfers between devices with their start and end apart: 2, of which 1 were waited for; matrix products, arithmetic and copies ran while one was open for 0% of the time, Pallas kernels for 3%

profile of v7, /device:TPU:1, one launch (start us, length us, event | category | flops | bytes accessed | tf_op | source)
XLA Modules:
  0.0 48.4 jit_solution(4962611221918095731)
XLA Ops:
  0.6 2.7 %send.1 = (bf16[1280,128]{1,0:T(8,128)(2,1)S(1)}, s32[8,1024]{1,0:T(8,128)S(1)}, bf16[2,256,512]{2,1,0:T(8,128)(2,1)S(1)}, bf16[2,512,256]{2,1,0:T(8,128)(2,1)S(1)}) custom-call(s32[1,2]{1,0:T(1,128)} %off_hbm.1, bf16[1,2,16,8192]{3,2,1,0:T(8,128)(2,1)} %slab_hbm.1, f32[2,1024]{1,0:T(2,128)} %pos_hbm.1, f32[2,1024]{1,0:T(2,128)} %obs_hbm.1, ...), custom_call_target="tpu_custom_call" | custom-call | flops 1048576 | bytes 2097152 | tf_op jit(solution)/shard_map/send/pallas_call | solution.py:545
  3.3 22.7 %all_to_all.10 = bf16[640,2,128]{2,1,0:T(2,128)(2,1)S(1)} all-to-all(bf16[640,2,128]{2,1,0:T(2,128)(2,1)S(1)} %bitcast.10), channel_id=1, replica_groups=mesh['facet'=4,'sub'=32] {'facet','sub'}, dimensions={0} | all-to-all | bytes 655360 | tf_op jit(solution)/shard_map/all_to_all | solution.py:526
  26.0 0.6 %rows.1 = (bf16[128,128]{1,0:T(8,128)(2,1)S(1)}, bf16[512,256]{1,0:T(8,128)(2,1)S(1)}, f32[2,2,128,128]{3,2,1,0:T(8,128)S(1)}, f32[2,128,128]{2,1,0:T(8,128)S(1)}) custom-call(bf16[1280,128]{1,0:T(8,128)(2,1)S(1)} %bitcast.8, bf16[2,256,512]{2,1,0:T(8,128)(2,1)S(1)} %get-tuple-element.20.fwd_ref), custom_call_target="tpu_custom_call" | custom-call | flops 1048576 | bytes 2097152 | tf_op jit(solution)/shard_map/rows/pallas_call | solution.py:545
  26.5 1.2 %collective-permute-start = (bf16[128,128]{1,0:T(8,128)(2,1)S(1)}, bf16[128,128]{1,0:T(8,128)(2,1)S(1)}, u32[]{:S(2)}, u32[]{:S(2)}) collective-permute-start(bf16[128,128]{1,0:T(8,128)(2,1)S(1)} %get-tuple-element.24), channel_id=1, source_target_pairs={{0,1},{1,0},{2,3},{3,2},{4,5},{5,4},{6,7},{7,6},{8,9},{9,8},{10,11... | collective-permute-start | bytes 98312 | tf_op jit(solution)/shard_map/ppermute | solution.py:530
  27.7 0.9 %tables.1 = (bf16[128,128]{1,0:T(8,128)(2,1)S(1)}, f32[80,128]{1,0:T(8,128)S(1)}, f32[2,2,128,128]{3,2,1,0:T(8,128)S(1)}, f32[2,128,1024]{2,1,0:T(8,128)S(1)}, bf16[2,128,1024]{2,1,0:T(8,128)(2,1)S(1)}) custom-call(f32[2,128,128]{2,1,0:T(8,128)S(1)} %get-tuple-element.21.raw_ref, bf16[2,256,512]{2,1,0:T(8,128)(2,1)S(1)} %get-tuple-element.20.fwd_ref, ...), custom_call_target="tpu_custom_call" | custom-call | flops 1048576 | bytes 2097152 | tf_op jit(solution)/shard_map/tables/pallas_call | solution.py:545
  28.6 0.0 collective-permute-done.other_ref
  28.6 1.0 %visibilities.1 = (bf16[128,128]{1,0:T(8,128)(2,1)S(1)}, f32[32,128]{1,0:T(8,128)S(1)}) custom-call(bf16[128,128]{1,0:T(8,128)(2,1)S(1)} %get-tuple-element.23.keep_ref, bf16[128,128]{1,0:T(8,128)(2,1)S(1)} %collective-permute-done.other_ref, f32[80,128]{1,0:T(8,128)S(1)} %get-tuple-element.25.vis_ref, f32[2,128,1024]{2,1,0:T(8,128)S(1)} %get-tuple-element.26.left, ...), custom_call_target="tpu_custom_call" | custom-call | flops 1048576 | bytes 2097152 | tf_op jit(solution)/shard_map/visibilities/pallas_call | solution.py:545
  29.6 0.4 collective-permute-start.1
  30.0 0.4 mine.1
  30.4 0.5 %collective-permute-done.1.other_ref = bf16[128,128]{1,0:T(8,128)(2,1)S(1)} collective-permute-done((bf16[128,128]{1,0:T(8,128)(2,1)S(1)}, bf16[128,128]{1,0:T(8,128)(2,1)S(1)}, u32[]{:S(2)}, u32[]{:S(2)}) %collective-permute-start.1) | collective-permute-done | bytes 32800 | tf_op jit(solution)/shard_map/ppermute | solution.py:530
  30.9 0.5 %images.1 = bf16[1280,128]{1,0:T(8,128)(2,1)S(1)} custom-call(f32[512,256]{1,0:T(8,128)S(1)} %get-tuple-element.32.part_ref, bf16[128,128]{1,0:T(8,128)(2,1)S(1)} %collective-permute-done.1.other_ref, f32[128,128]{1,0:T(8,128)S(1)} %get-tuple-element.33.tail_ref, f32[2,2,128,128]{3,2,1,0:T(8,128)S(1)} %get-tuple-element.34.rho_ref, ...), custom_call_target="tpu_custom_call" | custom-call | flops 1048576 | bytes 2097152 | tf_op jit(solution)/shard_map/images/pallas_call | solution.py:545
  31.4 0.0 copy-start
  31.5 0.0 copy-start.1
  31.5 0.0 copy-start.2
  31.5 15.2 %all_to_all.11 = bf16[640,2,128]{2,1,0:T(2,128)(2,1)S(1)} all-to-all(bf16[640,2,128]{2,1,0:T(2,128)(2,1)S(1)} %bitcast.9), channel_id=1, replica_groups=mesh['facet'=4,'sub'=32] {'facet','sub'}, dimensions={0} | all-to-all | bytes 655360 | tf_op jit(solution)/shard_map/all_to_all | solution.py:526
  46.7 0.0 copy-done
  46.7 0.0 copy-done.1
  46.7 0.0 copy-done.2
  46.7 1.7 %facet.1 = (f32[1,2,16,8192]{3,2,1,0:T(8,128)}, f32[2,1024]{1,0:T(2,128)}) custom-call(bf16[1280,128]{1,0:T(8,128)(2,1)S(1)} %bitcast.7, s32[8,1024]{1,0:T(8,128)S(1)} %get-tuple-element.35.meta_ref, bf16[256,64]{1,0:T(8,128)(2,1)S(1)} %copy-done.1, f32[4,128,128]{2,1,0:T(8,128)S(1)} %copy-done, bf16[256,128]{1,0:T(8,128)(2,1)S(1)} %copy-done.2), custom_call_target="tpu_custom_call" | custom-call | flops 1048576 | bytes 2097152 | tf_op jit(solution)/shard_map/facet/pallas_call | solution.py:545
Async XLA Ops:
  26.5 2.1 %collective-permute-start = (bf16[128,128]{1,0:T(8,128)(2,1)S(1)}, bf16[128,128]{1,0:T(8,128)(2,1)S(1)}, u32[]{:S(2)}, u32[]{:S(2)}) collective-permute-start(bf16[128,128]{1,0:T(8,128)(2,1)S(1)} %get-tuple-element.24), channel_id=1, source_target_pairs={{0,1},{1,0},{2,3},{3,2},{4,5},{5,4},{6,7},{7,6},{8,9},{9,8},{10,11... | collective-permute-start | bytes 98312 | tf_op jit(solution)/shard_map/ppermute | solution.py:530
  29.6 1.3 %collective-permute-start.1 = (bf16[128,128]{1,0:T(8,128)(2,1)S(1)}, bf16[128,128]{1,0:T(8,128)(2,1)S(1)}, u32[]{:S(2)}, u32[]{:S(2)}) collective-permute-start(bf16[128,128]{1,0:T(8,128)(2,1)S(1)} %get-tuple-element.28.corrected_ref), channel_id=1, source_target_pairs={{0,1},{1,0},{2,3},{3,2},{4,5},{5,4},{6,7},{7,6},{8,9},{9,8},{10,11... | collective-permute-start | bytes 98312 | tf_op jit(solution)/shard_map/ppermute | solution.py:530
  31.4 15.2 %copy-start = (f32[4,128,128]{2,1,0:T(8,128)S(1)}, f32[4,128,128]{2,1,0:T(8,128)}, u32[]{:S(2)}) copy-start(f32[4,128,128]{2,1,0:T(8,128)} %constant.17.clone.tw_ref) | copy-start | bytes 786436
  31.5 15.2 %copy-start.1 = (bf16[256,64]{1,0:T(8,128)(2,1)S(1)}, bf16[256,64]{1,0:T(8,128)(2,1)}, u32[]{:S(2)}) copy-start(bf16[256,64]{1,0:T(8,128)(2,1)} %constant.18.clone.coarse_ref) | copy-start | bytes 98308
  31.5 15.2 %copy-start.2 = (bf16[256,128]{1,0:T(8,128)(2,1)S(1)}, bf16[256,128]{1,0:T(8,128)(2,1)}, u32[]{:S(2)}) copy-start(bf16[256,128]{1,0:T(8,128)(2,1)} %constant.15.clone.col_ref) | copy-start | bytes 196612

commit v8 on v7

--- a/solution.py
+++ b/solution.py
@@ -497,7 +497,10 @@
     n = 2 * SLOT
     back = flat[pl.ds(NR2, NDEV, stride=MSG), :].T[:3 * n]
     owner, place = meta_ref[0:1, :], meta_ref[1:2, :]
-    own = jnp.where(iota((NDEV, NV), 0) == owner, 1.0, 0.0).astype(BF)
+    one, zero = jnp.ones((), BF), jnp.zeros((), BF)
+    own = jnp.where(
+        iota((NDEV, NV), 0).astype(F32).astype(BF) == owner.astype(F32).astype(BF), one, zero
+    )
     found = jnp.dot(back.astype(BF), own, preferred_element_type=F32)
     found = found[:n] + found[n:2 * n] + found[2 * n:]
     here = iota((SLOT, NV), 0) == place
@@ -532,7 +535,7 @@
 
 def on_device(slab, offsets, position, observed, subgrid_of, clip):
     t = {name: jnp.asarray(value) for name, value in TABLES.items()}
-    limit = pltpu.CompilerParams(vmem_limit_bytes=32 << 20)
+    limit = pltpu.CompilerParams(vmem_limit_bytes=20 << 20)
     shape = jax.ShapeDtypeStruct
     message = shape((NDEV * MSG, LANES), BF)
     fwd_table = shape((2, 4 * SUBG, NQ * RD), BF)

time: 48.6 us -> 48.6 us (level)
  no operation moved by 1% of the time
where the time goes in v8:
time: 48.6 us; the launch traced here: 48.4 us
  blocking collectives  37.9 us (78%)
  Pallas kernels  7.68 us (16%)
  starting transfers between devices  1.57 us (3%)
  between operations  0.71 us (1%)
  waiting for transfers between devices  0.53 us (1%)
    all_to_all x2, blocking collectives, exchange(): lax.all_to_all(pairs, ALL, split_axis=0, concat_axis=0, tiled=True)  37.9 us
    pallas_call x7, Pallas kernels, call(): pl.pallas_call(kernel, out_shape=outs, in_specs=in_specs or [VMEM] * len(...  7.68 us
    ppermute x2, starting transfers between devices, other_core(): return lax.ppermute(x, 'sub', [(i, i ^ 1) for i in range(NQ)])  1.57 us
  transfers between devices with their start and end apart: 2, of which 1 were waited for; matrix products, arithmetic and copies ran while one was open for 0% of the time, Pallas kernels for 3%

profile of v8, /device:TPU:1, one launch (start us, length us, event | category | flops | bytes accessed | tf_op | source)
XLA Modules:
  0.0 48.4 jit_solution(15173828343172457414)
XLA Ops:
  0.6 2.7 %send.1 = (bf16[1280,128]{1,0:T(8,128)(2,1)S(1)}, s32[8,1024]{1,0:T(8,128)S(1)}, bf16[2,256,512]{2,1,0:T(8,128)(2,1)S(1)}, bf16[2,512,256]{2,1,0:T(8,128)(2,1)S(1)}) custom-call(s32[1,2]{1,0:T(1,128)} %off_hbm.1, bf16[1,2,16,8192]{3,2,1,0:T(8,128)(2,1)} %slab_hbm.1, f32[2,1024]{1,0:T(2,128)} %pos_hbm.1, f32[2,1024]{1,0:T(2,128)} %obs_hbm.1, ...), custom_call_target="tpu_custom_call" | custom-call | flops 1048576 | bytes 2097152 | tf_op jit(solution)/shard_map/send/pallas_call | solution.py:548
  3.3 22.7 %all_to_all.10 = bf16[640,2,128]{2,1,0:T(2,128)(2,1)S(1)} all-to-all(bf16[640,2,128]{2,1,0:T(2,128)(2,1)S(1)} %bitcast.10), channel_id=1, replica_groups=mesh['facet'=4,'sub'=32] {'facet','sub'}, dimensions={0} | all-to-all | bytes 655360 | tf_op jit(solution)/shard_map/all_to_all | solution.py:529
  26.0 0.6 %rows.1 = (bf16[128,128]{1,0:T(8,128)(2,1)S(1)}, bf16[512,256]{1,0:T(8,128)(2,1)S(1)}, f32[2,2,128,128]{3,2,1,0:T(8,128)S(1)}, f32[2,128,128]{2,1,0:T(8,128)S(1)}) custom-call(bf16[1280,128]{1,0:T(8,128)(2,1)S(1)} %bitcast.8, bf16[2,256,512]{2,1,0:T(8,128)(2,1)S(1)} %get-tuple-element.20.fwd_ref), custom_call_target="tpu_custom_call" | custom-call | flops 1048576 | bytes 2097152 | tf_op jit(solution)/shard_map/rows/pallas_call | solution.py:548
  26.5 1.2 %collective-permute-start = (bf16[128,128]{1,0:T(8,128)(2,1)S(1)}, bf16[128,128]{1,0:T(8,128)(2,1)S(1)}, u32[]{:S(2)}, u32[]{:S(2)}) collective-permute-start(bf16[128,128]{1,0:T(8,128)(2,1)S(1)} %get-tuple-element.24), channel_id=1, source_target_pairs={{0,1},{1,0},{2,3},{3,2},{4,5},{5,4},{6,7},{7,6},{8,9},{9,8},{10,11... | collective-permute-start | bytes 98312 | tf_op jit(solution)/shard_map/ppermute | solution.py:533
  27.7 0.9 %tables.1 = (bf16[128,128]{1,0:T(8,128)(2,1)S(1)}, f32[80,128]{1,0:T(8,128)S(1)}, f32[2,2,128,128]{3,2,1,0:T(8,128)S(1)}, f32[2,128,1024]{2,1,0:T(8,128)S(1)}, bf16[2,128,1024]{2,1,0:T(8,128)(2,1)S(1)}) custom-call(f32[2,128,128]{2,1,0:T(8,128)S(1)} %get-tuple-element.21.raw_ref, bf16[2,256,512]{2,1,0:T(8,128)(2,1)S(1)} %get-tuple-element.20.fwd_ref, ...), custom_call_target="tpu_custom_call" | custom-call | flops 1048576 | bytes 2097152 | tf_op jit(solution)/shard_map/tables/pallas_call | solution.py:548
  28.6 0.0 collective-permute-done.other_ref
  28.6 1.0 %visibilities.1 = (bf16[128,128]{1,0:T(8,128)(2,1)S(1)}, f32[32,128]{1,0:T(8,128)S(1)}) custom-call(bf16[128,128]{1,0:T(8,128)(2,1)S(1)} %get-tuple-element.23.keep_ref, bf16[128,128]{1,0:T(8,128)(2,1)S(1)} %collective-permute-done.other_ref, f32[80,128]{1,0:T(8,128)S(1)} %get-tuple-element.25.vis_ref, f32[2,128,1024]{2,1,0:T(8,128)S(1)} %get-tuple-element.26.left, ...), custom_call_target="tpu_custom_call" | custom-call | flops 1048576 | bytes 2097152 | tf_op jit(solution)/shard_map/visibilities/pallas_call | solution.py:548
  29.6 0.4 collective-permute-start.1
  30.0 0.4 mine.1
  30.4 0.5 %collective-permute-done.1.other_ref = bf16[128,128]{1,0:T(8,128)(2,1)S(1)} collective-permute-done((bf16[128,128]{1,0:T(8,128)(2,1)S(1)}, bf16[128,128]{1,0:T(8,128)(2,1)S(1)}, u32[]{:S(2)}, u32[]{:S(2)}) %collective-permute-start.1) | collective-permute-done | bytes 32800 | tf_op jit(solution)/shard_map/ppermute | solution.py:533
  30.9 0.5 %images.1 = bf16[1280,128]{1,0:T(8,128)(2,1)S(1)} custom-call(f32[512,256]{1,0:T(8,128)S(1)} %get-tuple-element.32.part_ref, bf16[128,128]{1,0:T(8,128)(2,1)S(1)} %collective-permute-done.1.other_ref, f32[128,128]{1,0:T(8,128)S(1)} %get-tuple-element.33.tail_ref, f32[2,2,128,128]{3,2,1,0:T(8,128)S(1)} %get-tuple-element.34.rho_ref, ...), custom_call_target="tpu_custom_call" | custom-call | flops 1048576 | bytes 2097152 | tf_op jit(solution)/shard_map/images/pallas_call | solution.py:548
  31.4 0.0 copy-start
  31.5 0.0 copy-start.1
  31.5 0.0 copy-start.2
  31.5 15.2 %all_to_all.11 = bf16[640,2,128]{2,1,0:T(2,128)(2,1)S(1)} all-to-all(bf16[640,2,128]{2,1,0:T(2,128)(2,1)S(1)} %bitcast.9), channel_id=1, replica_groups=mesh['facet'=4,'sub'=32] {'facet','sub'}, dimensions={0} | all-to-all | bytes 655360 | tf_op jit(solution)/shard_map/all_to_all | solution.py:529
  46.7 0.0 copy-done
  46.7 0.0 copy-done.1
  46.7 0.0 copy-done.2
  46.7 1.7 %facet.1 = (f32[1,2,16,8192]{3,2,1,0:T(8,128)}, f32[2,1024]{1,0:T(2,128)}) custom-call(bf16[1280,128]{1,0:T(8,128)(2,1)S(1)} %bitcast.7, s32[8,1024]{1,0:T(8,128)S(1)} %get-tuple-element.35.meta_ref, bf16[256,64]{1,0:T(8,128)(2,1)S(1)} %copy-done.1, f32[4,128,128]{2,1,0:T(8,128)S(1)} %copy-done, bf16[256,128]{1,0:T(8,128)(2,1)S(1)} %copy-done.2), custom_call_target="tpu_custom_call" | custom-call | flops 1048576 | bytes 2097152 | tf_op jit(solution)/shard_map/facet/pallas_call | solution.py:548
Async XLA Ops:
  26.5 2.1 %collective-permute-start = (bf16[128,128]{1,0:T(8,128)(2,1)S(1)}, bf16[128,128]{1,0:T(8,128)(2,1)S(1)}, u32[]{:S(2)}, u32[]{:S(2)}) collective-permute-start(bf16[128,128]{1,0:T(8,128)(2,1)S(1)} %get-tuple-element.24), channel_id=1, source_target_pairs={{0,1},{1,0},{2,3},{3,2},{4,5},{5,4},{6,7},{7,6},{8,9},{9,8},{10,11... | collective-permute-start | bytes 98312 | tf_op jit(solution)/shard_map/ppermute | solution.py:533
  29.6 1.3 %collective-permute-start.1 = (bf16[128,128]{1,0:T(8,128)(2,1)S(1)}, bf16[128,128]{1,0:T(8,128)(2,1)S(1)}, u32[]{:S(2)}, u32[]{:S(2)}) collective-permute-start(bf16[128,128]{1,0:T(8,128)(2,1)S(1)} %get-tuple-element.28.corrected_ref), channel_id=1, source_target_pairs={{0,1},{1,0},{2,3},{3,2},{4,5},{5,4},{6,7},{7,6},{8,9},{9,8},{10,11... | collective-permute-start | bytes 98312 | tf_op jit(solution)/shard_map/ppermute | solution.py:533
  31.4 15.2 %copy-start = (f32[4,128,128]{2,1,0:T(8,128)S(1)}, f32[4,128,128]{2,1,0:T(8,128)}, u32[]{:S(2)}) copy-start(f32[4,128,128]{2,1,0:T(8,128)} %constant.17.clone.tw_ref) | copy-start | bytes 786436
  31.5 15.2 %copy-start.1 = (bf16[256,64]{1,0:T(8,128)(2,1)S(1)}, bf16[256,64]{1,0:T(8,128)(2,1)}, u32[]{:S(2)}) copy-start(bf16[256,64]{1,0:T(8,128)(2,1)} %constant.18.clone.coarse_ref) | copy-start | bytes 98308
  31.5 15.2 %copy-start.2 = (bf16[256,128]{1,0:T(8,128)(2,1)S(1)}, bf16[256,128]{1,0:T(8,128)(2,1)}, u32[]{:S(2)}) copy-start(bf16[256,128]{1,0:T(8,128)(2,1)} %constant.15.clone.col_ref) | copy-start | bytes 196612

commit v9 on v7

--- a/solution.py
+++ b/solution.py
@@ -114,8 +114,8 @@
 
 
 def send_kernel(
-    off_hbm, slab_hbm, pos_hbm, obs_hbm, ids_hbm, ids8_hbm, clip_hbm, table_hbm, tw_hbm, fwd_hbm, adj_hbm,
-    msg_ref, meta_ref, fwd_ref, adj_ref, off_ref, slab_ref, pos_ref, obs_ref, ids_ref, ids8_ref, clip_ref, table_ref, tw_ref,
+    off_hbm, slab_hbm, pos_hbm, obs_hbm, ids_hbm, ids8_hbm, clip_hbm, table_hbm, tw_hbm, fwd_hbm,
+    msg_ref, meta_ref, fwd_ref, off_ref, slab_ref, pos_ref, obs_ref, ids_ref, ids8_ref, clip_ref, table_ref, tw_ref,
     wide, flat, y_ref, z_ref, sems,
 ):
     pairs = [
@@ -126,7 +126,6 @@
     four = lax.axis_index("facet") // 2
     later = [
         pltpu.make_async_copy(fwd_hbm.at[four], fwd_ref, sems.at[len(pairs)]),
-        pltpu.make_async_copy(adj_hbm.at[four], adj_ref, sems.at[len(pairs) + 1]),
     ]
     for copy in copies + later:
         copy.start()
@@ -410,10 +409,11 @@
             jnp.concatenate([(x * rc + turned * rs).astype(BF), (x * rs - turned * rc).astype(BF)], 0)
         )
     half = NQ * NR2
+    four = lax.axis_index("facet") // 2
     table = jnp.concatenate(
         [
-            adj_ref[pair, pl.ds(pl.multiple_of(core * half, half), half), :],
-            adj_ref[pair, pl.ds(pl.multiple_of((1 - core) * half, half), half), :],
+            adj_ref[four, pair, pl.ds(pl.multiple_of(core * half, half), half), :],
+            adj_ref[four, pair, pl.ds(pl.multiple_of((1 - core) * half, half), half), :],
         ], 0
     )
     return jnp.dot(table, jnp.concatenate(cols, 1), preferred_element_type=F32)
@@ -536,7 +536,6 @@
     shape = jax.ShapeDtypeStruct
     message = shape((NDEV * MSG, LANES), BF)
     fwd_table = shape((2, 4 * SUBG, NQ * RD), BF)
-    adj_table = shape((2, NQ * RD, 4 * SUBG), BF)
     square = shape((LANES, LANES), BF)
     phases = shape((2, 2, LANES, LANES), F32)
     flat = pltpu.VMEM((NDEV * MSG, LANES), F32)
@@ -557,9 +556,9 @@
         offsets, slab, position, observed, subgrid_of.reshape(1, NV), subgrid_of.reshape(8, LANES),
         clip.reshape(1, NV // VIS_BLOCK), t["column"], t["tw_fwd"],
     )
-    sent, meta, fwd, adj = call(
-        send_kernel, "send", in_place(inputs + (t["row_fwd"], t["row_adj"])),
-        (message, shape((8, NV), jnp.int32), fwd_table, adj_table),
+    sent, meta, fwd = call(
+        send_kernel, "send", in_place(inputs + (t["row_fwd"],)),
+        (message, shape((8, NV), jnp.int32), fwd_table),
         [pltpu.SMEM((1, 2), jnp.int32)]
         + [pltpu.VMEM(x.shape, x.dtype) for x in inputs[1:]]
         + [
@@ -567,9 +566,9 @@
             flat,
             pltpu.VMEM((LANES, RD * LANES), F32),
             pltpu.VMEM((NR2 * LANES, 2 * LANES), BF),
-            pltpu.SemaphoreType.DMA((len(inputs) + 2,)),
+            pltpu.SemaphoreType.DMA((len(inputs) + 5,)),
         ],
-        in_specs=[HBM] * (len(inputs) + 2),
+        in_specs=[HBM] * (len(inputs) + 1),
     )
     got = exchange(sent)
     give, rhs, other_rho, raw = call(
@@ -595,10 +594,10 @@
     )
     other = other_core(corrected)
     part, tail = call(
-        mine_kernel, "mine", (corrected, back, rho, adj),
+        mine_kernel, "mine", (corrected, back, rho, t["row_adj"]),
         (shape((NQ * RD, 2 * LANES), F32), shape((LANES, LANES), F32)), [],
     )
-    (answer,) = call(images_kernel, "images", (part, other, tail, other_rho, adj), (message,), [flat])
+    (answer,) = call(images_kernel, "images", (part, other, tail, other_rho, t["row_adj"]), (message,), [flat])
     facet_adjoint, residual = call(
         facet_kernel, "facet",
         (exchange(answer), meta, t["coarse_adj"], t["tw_adj"], t["col_adj"]),

time: 48.6 us -> 48.6 us (level)
  no operation moved by 1% of the time
where the time goes in v9:
time: 48.6 us; the launch traced here: 48.4 us
  blocking collectives  37.8 us (78%)
  Pallas kernels  7.73 us (16%)
  starting transfers between devices  1.54 us (3%)
  between operations  0.72 us (1%)
  waiting for transfers between devices  0.56 us (1%)
    all_to_all x2, blocking collectives, exchange(): lax.all_to_all(pairs, ALL, split_axis=0, concat_axis=0, tiled=True)  37.8 us
    pallas_call x7, Pallas kernels, call(): pl.pallas_call(kernel, out_shape=outs, in_specs=in_specs or [VMEM] * len(...  7.73 us
    ppermute x2, starting transfers between devices, other_core(): return lax.ppermute(x, 'sub', [(i, i ^ 1) for i in range(NQ)])  1.54 us
  transfers between devices with their start and end apart: 2, of which 1 were waited for; matrix products, arithmetic and copies ran while one was open for 0% of the time, Pallas kernels for 3%

profile of v9, /device:TPU:1, one launch (start us, length us, event | category | flops | bytes accessed | tf_op | source)
XLA Modules:
  0.0 48.4 jit_solution(11509374247602796289)
XLA Ops:
  0.6 2.7 %send.1 = (bf16[1280,128]{1,0:T(8,128)(2,1)S(1)}, s32[8,1024]{1,0:T(8,128)S(1)}, bf16[2,256,512]{2,1,0:T(8,128)(2,1)S(1)}) custom-call(s32[1,2]{1,0:T(1,128)} %off_hbm.1, bf16[1,2,16,8192]{3,2,1,0:T(8,128)(2,1)} %slab_hbm.1, f32[2,1024]{1,0:T(2,128)} %pos_hbm.1, f32[2,1024]{1,0:T(2,128)} %obs_hbm.1, s32[1,1024]{1,0:T(1,128)} %bitcast.11, s32[8,128]{1,0:T(8,128)} %bitcast.12, ...), custom_call_target="tpu_custom_call" | custom-call | flops 1048576 | bytes 2097152 | tf_op jit(solution)/shard_map/send/pallas_call | solution.py:544
  3.3 22.7 %all_to_all.10 = bf16[640,2,128]{2,1,0:T(2,128)(2,1)S(1)} all-to-all(bf16[640,2,128]{2,1,0:T(2,128)(2,1)S(1)} %bitcast.10), channel_id=1, replica_groups=mesh['facet'=4,'sub'=32] {'facet','sub'}, dimensions={0} | all-to-all | bytes 655360 | tf_op jit(solution)/shard_map/all_to_all | solution.py:526
  26.0 0.6 %rows.1 = (bf16[128,128]{1,0:T(8,128)(2,1)S(1)}, bf16[512,256]{1,0:T(8,128)(2,1)S(1)}, f32[2,2,128,128]{3,2,1,0:T(8,128)S(1)}, f32[2,128,128]{2,1,0:T(8,128)S(1)}) custom-call(bf16[1280,128]{1,0:T(8,128)(2,1)S(1)} %bitcast.9, bf16[2,256,512]{2,1,0:T(8,128)(2,1)S(1)} %get-tuple-element.19.fwd_ref), custom_call_target="tpu_custom_call" | custom-call | flops 1048576 | bytes 2097152 | tf_op jit(solution)/shard_map/rows/pallas_call | solution.py:544
  26.6 1.2 %collective-permute-start = (bf16[128,128]{1,0:T(8,128)(2,1)S(1)}, bf16[128,128]{1,0:T(8,128)(2,1)S(1)}, u32[]{:S(2)}, u32[]{:S(2)}) collective-permute-start(bf16[128,128]{1,0:T(8,128)(2,1)S(1)} %get-tuple-element.23), channel_id=1, source_target_pairs={{0,1},{1,0},{2,3},{3,2},{4,5},{5,4},{6,7},{7,6},{8,9},{9,8},{10,11... | collective-permute-start | bytes 98312 | tf_op jit(solution)/shard_map/ppermute | solution.py:530
  27.8 0.9 %tables.1 = (bf16[128,128]{1,0:T(8,128)(2,1)S(1)}, f32[80,128]{1,0:T(8,128)S(1)}, f32[2,2,128,128]{3,2,1,0:T(8,128)S(1)}, f32[2,128,1024]{2,1,0:T(8,128)S(1)}, bf16[2,128,1024]{2,1,0:T(8,128)(2,1)S(1)}) custom-call(f32[2,128,128]{2,1,0:T(8,128)S(1)} %get-tuple-element.20.raw_ref, bf16[2,256,512]{2,1,0:T(8,128)(2,1)S(1)} %get-tuple-element.19.fwd_ref, ...), custom_call_target="tpu_custom_call" | custom-call | flops 1048576 | bytes 2097152 | tf_op jit(solution)/shard_map/tables/pallas_call | solution.py:544
  28.7 0.0 copy-start
  28.7 0.0 collective-permute-done.other_ref
  28.7 1.0 %visibilities.1 = (bf16[128,128]{1,0:T(8,128)(2,1)S(1)}, f32[32,128]{1,0:T(8,128)S(1)}) custom-call(bf16[128,128]{1,0:T(8,128)(2,1)S(1)} %get-tuple-element.22.keep_ref, bf16[128,128]{1,0:T(8,128)(2,1)S(1)} %collective-permute-done.other_ref, f32[80,128]{1,0:T(8,128)S(1)} %get-tuple-element.24.vis_ref, f32[2,128,1024]{2,1,0:T(8,128)S(1)} %get-tuple-element.25.left, ...), custom_call_target="tpu_custom_call" | custom-call | flops 1048576 | bytes 2097152 | tf_op jit(solution)/shard_map/visibilities/pallas_call | solution.py:544
  29.7 0.3 collective-permute-start.1
  30.0 0.0 copy-done
  30.0 0.4 mine.1
  30.4 0.6 %collective-permute-done.1.other_ref = bf16[128,128]{1,0:T(8,128)(2,1)S(1)} collective-permute-done((bf16[128,128]{1,0:T(8,128)(2,1)S(1)}, bf16[128,128]{1,0:T(8,128)(2,1)S(1)}, u32[]{:S(2)}, u32[]{:S(2)}) %collective-permute-start.1) | collective-permute-done | bytes 32800 | tf_op jit(solution)/shard_map/ppermute | solution.py:530
  31.0 0.5 %images.1 = bf16[1280,128]{1,0:T(8,128)(2,1)S(1)} custom-call(f32[512,256]{1,0:T(8,128)S(1)} %get-tuple-element.30.part_ref, bf16[128,128]{1,0:T(8,128)(2,1)S(1)} %collective-permute-done.1.other_ref, f32[128,128]{1,0:T(8,128)S(1)} %get-tuple-element.31.tail_ref, f32[2,2,128,128]{3,2,1,0:T(8,128)S(1)} %get-tuple-element.32.rho_ref, ...), custom_call_target="tpu_custom_call" | custom-call | flops 1048576 | bytes 2097152 | tf_op jit(solution)/shard_map/images/pallas_call | solution.py:544
  31.5 0.0 copy-start.1
  31.5 0.0 copy-start.2
  31.5 0.0 copy-start.3
  31.5 15.2 %all_to_all.11 = bf16[640,2,128]{2,1,0:T(2,128)(2,1)S(1)} all-to-all(bf16[640,2,128]{2,1,0:T(2,128)(2,1)S(1)} %bitcast.7), channel_id=1, replica_groups=mesh['facet'=4,'sub'=32] {'facet','sub'}, dimensions={0} | all-to-all | bytes 655360 | tf_op jit(solution)/shard_map/all_to_all | solution.py:526
  46.7 0.0 copy-done.1
  46.7 0.0 copy-done.2
  46.7 0.0 copy-done.3
  46.7 1.7 %facet.1 = (f32[1,2,16,8192]{3,2,1,0:T(8,128)}, f32[2,1024]{1,0:T(2,128)}) custom-call(bf16[1280,128]{1,0:T(8,128)(2,1)S(1)} %bitcast.8, s32[8,1024]{1,0:T(8,128)S(1)} %get-tuple-element.33.meta_ref, bf16[256,64]{1,0:T(8,128)(2,1)S(1)} %copy-done.2, f32[4,128,128]{2,1,0:T(8,128)S(1)} %copy-done.1, bf16[256,128]{1,0:T(8,128)(2,1)S(1)} %copy-done.3), custom_call_target="tpu_custom_call" | custom-call | flops 1048576 | bytes 2097152 | tf_op jit(solution)/shard_map/facet/pallas_call | solution.py:544
Async XLA Ops:
  26.6 2.1 %collective-permute-start = (bf16[128,128]{1,0:T(8,128)(2,1)S(1)}, bf16[128,128]{1,0:T(8,128)(2,1)S(1)}, u32[]{:S(2)}, u32[]{:S(2)}) collective-permute-start(bf16[128,128]{1,0:T(8,128)(2,1)S(1)} %get-tuple-element.23), channel_id=1, source_target_pairs={{0,1},{1,0},{2,3},{3,2},{4,5},{5,4},{6,7},{7,6},{8,9},{9,8},{10,11... | collective-permute-start | bytes 98312 | tf_op jit(solution)/shard_map/ppermute | solution.py:530
  28.7 1.4 %copy-start = (bf16[2,2,512,256]{3,2,1,0:T(8,128)(2,1)S(1)}, bf16[2,2,512,256]{3,2,1,0:T(8,128)(2,1)}, u32[]{:S(2)}) copy-start(bf16[2,2,512,256]{3,2,1,0:T(8,128)(2,1)} %constant.20.clone.adj_ref) | copy-start | bytes 3145732
  29.7 1.3 %collective-permute-start.1 = (bf16[128,128]{1,0:T(8,128)(2,1)S(1)}, bf16[128,128]{1,0:T(8,128)(2,1)S(1)}, u32[]{:S(2)}, u32[]{:S(2)}) collective-permute-start(bf16[128,128]{1,0:T(8,128)(2,1)S(1)} %get-tuple-element.27.corrected_ref), channel_id=1, source_target_pairs={{0,1},{1,0},{2,3},{3,2},{4,5},{5,4},{6,7},{7,6},{8,9},{9,8},{10,11... | collective-permute-start | bytes 98312 | tf_op jit(solution)/shard_map/ppermute | solution.py:530
  31.5 15.2 %copy-start.1 = (f32[4,128,128]{2,1,0:T(8,128)S(1)}, f32[4,128,128]{2,1,0:T(8,128)}, u32[]{:S(2)}) copy-start(f32[4,128,128]{2,1,0:T(8,128)} %constant.17.clone.tw_ref) | copy-start | bytes 786436
  31.5 15.2 %copy-start.2 = (bf16[256,64]{1,0:T(8,128)(2,1)S(1)}, bf16[256,64]{1,0:T(8,128)(2,1)}, u32[]{:S(2)}) copy-start(bf16[256,64]{1,0:T(8,128)(2,1)} %constant.18.clone.coarse_ref) | copy-start | bytes 98308
  31.5 15.2 %copy-start.3 = (bf16[256,128]{1,0:T(8,128)(2,1)S(1)}, bf16[256,128]{1,0:T(8,128)(2,1)}, u32[]{:S(2)}) copy-start(bf16[256,128]{1,0:T(8,128)(2,1)} %constant.15.clone.col_ref) | copy-start | bytes 196612
